TPU v7x, 32 devices: a whole 2x2x4 slice. The times are simulated.
32 devices in a mesh: dp: 8 (over z, x), mp: 4 (over y, core).
Axes of the slice: x: 2, y: 2, z: 4, core: 2. Of those that a mesh axis runs over, the one named last changes fastest.
Arguments:
- source_ids: int32 [2, 8, 1024], P(None, 'dp'), may hold values from 0 to 383
- target_ids: int32 [2, 8, 256], P(None, 'dp'), may hold values from 0 to 383
- source_lengths: int32 [2, 8], P(None, 'dp'), may hold values from 512 to 1024
- target_lengths: int32 [2, 8], P(None, 'dp'), may hold values from 64 to 256
- embedding: float32 [384, 1536], P('mp', 'dp'), may hold values from -6 to 6
- unembedding: float32 [1536, 384], P('dp', 'mp'), may hold values from -0.3125 to 0.3125
- attention_in: float32 [3, 1536, 3, 768], P(None, 'dp', None, 'mp'), may hold values from -0.15625 to 0.15625
- attention_out: float32 [3, 768, 1536], P(None, 'mp', 'dp'), may hold values from -1.75 to 1.75
- feed_in: float32 [2, 1536, 2, 3968], P(None, 'dp', None, 'mp'), may hold values from -0.15625 to 0.15625
- feed_out: float32 [2, 3968, 1536], P(None, 'mp', 'dp'), may hold values from -0.09375 to 0.09375
- norm_gains: float32 [7, 1536], P(None, ('dp', 'mp')), may hold values from 0.5 to 1.5
- embedding_first: float32 [384, 1536], P('mp', 'dp'), may hold values from -1.4305115e-06 to 1.4305115e-06
- unembedding_first: float32 [1536, 384], P('dp', 'mp'), may hold values from -4.7683716e-06 to 4.7683716e-06
- attention_in_first: float32 [3, 1536, 3, 768], P(None, 'dp', None, 'mp'), may hold values from -4.7683716e-06 to 4.7683716e-06
- attention_out_first: float32 [3, 768, 1536], P(None, 'mp', 'dp'), may hold values from -4.7683716e-06 to 4.7683716e-06
- feed_in_first: float32 [2, 1536, 2, 3968], P(None, 'dp', None, 'mp'), may hold values from -4.7683716e-06 to 4.7683716e-06
- feed_out_first: float32 [2, 3968, 1536], P(None, 'mp', 'dp'), may hold values from -4.7683716e-06 to 4.7683716e-06
- norm_gains_first: float32 [7, 1536], P(None, ('dp', 'mp')), may hold values from -4.7683716e-06 to 4.7683716e-06
- embedding_second: float32 [384, 1536], P('mp', 'dp'), may hold values from 5.7786472e-15 to 2.3114589e-14
- unembedding_second: float32 [1536, 384], P('dp', 'mp'), may hold values from 4.8155395e-14 to 1.9262158e-13
- attention_in_second: float32 [3, 1536, 3, 768], P(None, 'dp', None, 'mp'), may hold values from 4.8155395e-14 to 1.9262158e-13
- attention_out_second: float32 [3, 768, 1536], P(None, 'mp', 'dp'), may hold values from 4.8155395e-14 to 1.9262158e-13
- feed_in_second: float32 [2, 1536, 2, 3968], P(None, 'dp', None, 'mp'), may hold values from 4.8155395e-14 to 1.9262158e-13
- feed_out_second: float32 [2, 3968, 1536], P(None, 'mp', 'dp'), may hold values from 4.8155395e-14 to 1.9262158e-13
- norm_gains_second: float32 [7, 1536], P(None, ('dp', 'mp')), may hold values from 4.8155395e-14 to 1.9262158e-13
Outputs:
- loss: float32 [], replicated
- grad_norm: float32 [], replicated
- new_embedding: float32 [384, 1536], P('mp', 'dp')
- new_unembedding: float32 [1536, 384], P('dp', 'mp')
- new_attention_in: float32 [3, 1536, 3, 768], P(None, 'dp', None, 'mp')
- new_attention_out: float32 [3, 768, 1536], P(None, 'mp', 'dp')
- new_feed_in: float32 [2, 1536, 2, 3968], P(None, 'dp', None, 'mp')
- new_feed_out: float32 [2, 3968, 1536], P(None, 'mp', 'dp')
- new_norm_gains: float32 [7, 1536], P(None, ('dp', 'mp'))
- new_embedding_first: float32 [384, 1536], P('mp', 'dp')
- new_unembedding_first: float32 [1536, 384], P('dp', 'mp')
- new_attention_in_first: float32 [3, 1536, 3, 768], P(None, 'dp', None, 'mp')
- new_attention_out_first: float32 [3, 768, 1536], P(None, 'mp', 'dp')
- new_feed_in_first: float32 [2, 1536, 2, 3968], P(None, 'dp', None, 'mp')
- new_feed_out_first: float32 [2, 3968, 1536], P(None, 'mp', 'dp')
- new_norm_gains_first: float32 [7, 1536], P(None, ('dp', 'mp'))
- new_embedding_second: float32 [384, 1536], P('mp', 'dp')
- new_unembedding_second: float32 [1536, 384], P('dp', 'mp')
- new_attention_in_second: float32 [3, 1536, 3, 768], P(None, 'dp', None, 'mp')
- new_attention_out_second: float32 [3, 768, 1536], P(None, 'mp', 'dp')
- new_feed_in_second: float32 [2, 1536, 2, 3968], P(None, 'dp', None, 'mp')
- new_feed_out_second: float32 [2, 3968, 1536], P(None, 'mp', 'dp')
- new_norm_gains_second: float32 [7, 1536], P(None, ('dp', 'mp'))
All inputs are finite; a program needn't handle non-finite values.
Results may differ from a plain program's by a relative error of at most 0.02.
Values may be sent and summed in bfloat16 or wider, within the bound.
No kernel may reach another device: no remote copies, remote signals or barrier semaphores. Data moves between devices by JAX's collectives and lax.ppermute only.
A program may use at most 384 MiB of HBM per device.

v0:
```python
import jax
import jax.numpy as jnp
from jax import lax
from jax.sharding import PartitionSpec as P

DK = 64
STEP = 10


norm_eps = 1e-06
clip_limit = 0.05
step_rates = (0.4, 0.02, 0.02, 0.1, 0.02, 0.02, 0.25)
beta_one = 0.9
beta_two = 0.999
adam_eps = 1e-08
decay = 0.01
masked = -1000000000.0


def joined(part, axis, combine):
    gathered = jax.tree.map(lambda a: lax.all_gather(a, axis), part)

    def take(source):
        return jax.tree.map(lambda a: lax.dynamic_index_in_dim(a, source, 0, False), gathered)

    return lax.fori_loop(
        1, lax.axis_size(axis), lambda source, state: combine(state, take(source)), take(0)
    )


def collect(part):
    return lax.all_gather(part, "mp", axis=0, tiled=True)


def spread(part):
    return lax.psum_scatter(part, "mp", scatter_dimension=0, tiled=True)


def pull_rows(grad):
    return lax.all_gather(grad.astype(jnp.bfloat16), "mp", axis=0, tiled=True)


def push_rows(part):
    return lax.psum_scatter(part, "mp", scatter_dimension=0, tiled=True)


def product(left, right):
    return jnp.dot(left, right, preferred_element_type=jnp.float32)


def product_left(left, right):
    return lax.dot_general(
        left, right, (((0,), (0,)), ((), ())), preferred_element_type=jnp.float32
    )


def product_right(left, right):
    return lax.dot_general(
        left, right, (((1,), (1,)), ((), ())), preferred_element_type=jnp.float32
    )


def rms_norm(stream, gain):
    return stream * lax.rsqrt(jnp.mean(stream * stream, axis=-1, keepdims=True) + norm_eps) * gain


def normalize(stream, gain):
    return collect(rms_norm(stream, gain).astype(jnp.bfloat16))


def norm_back(stream, gain, grad):
    _, pull = jax.vjp(rms_norm, stream, gain)
    return pull(grad)


def score_block(query, key, bias):
    q_heads = query.reshape(query.shape[0], -1, DK)
    k_heads = key.reshape(key.shape[0], -1, DK)
    return (
        jnp.einsum("rhd,shd->hrs", q_heads, k_heads, preferred_element_type=jnp.float32) * 0.125
        + bias
    )


def attend(x_query, x_keys, w_in, w_out, bias):
    query = product(x_query, w_in[:, 0]).astype(jnp.bfloat16)
    key = product(x_keys, w_in[:, 1]).astype(jnp.bfloat16)
    value = product(x_keys, w_in[:, 2]).astype(jnp.bfloat16)
    scores = score_block(query, key, bias)
    peak = jnp.max(scores, axis=-1, keepdims=True)
    raw = jnp.exp(scores - peak)
    total = jnp.sum(raw, axis=-1, keepdims=True)
    probs = (raw / total).astype(jnp.bfloat16)
    mixed = jnp.einsum(
        "hrs,shd->rhd",
        probs,
        value.reshape(value.shape[0], -1, DK),
        preferred_element_type=jnp.float32,
    )
    mixed = mixed.reshape(query.shape[0], -1).astype(jnp.bfloat16)
    return (product(mixed, w_out), (query, key, value, peak + jnp.log(total), mixed))


def attend_back(x_query, x_keys, w_in, w_out, bias, kept, d_full):
    query, key, value, lse, mixed = kept
    rows = query.shape[0]
    cols = key.shape[0]
    g_out = product_left(mixed, d_full)
    d_mixed = product_right(d_full, w_out).astype(jnp.bfloat16).reshape(rows, -1, DK)
    probs = jnp.exp(score_block(query, key, bias) - lse)
    d_value = jnp.einsum(
        "hrs,rhd->shd", probs.astype(jnp.bfloat16), d_mixed, preferred_element_type=jnp.float32
    )
    d_value = d_value.reshape(cols, -1).astype(jnp.bfloat16)
    d_probs = jnp.einsum(
        "rhd,shd->hrs", d_mixed, value.reshape(cols, -1, DK), preferred_element_type=jnp.float32
    )
    d_scores = (probs * (d_probs - jnp.sum(probs * d_probs, axis=-1, keepdims=True))).astype(
        jnp.bfloat16
    )
    d_query = (
        jnp.einsum(
            "hrs,shd->rhd", d_scores, key.reshape(cols, -1, DK), preferred_element_type=jnp.float32
        )
        * 0.125
    )
    d_query = d_query.reshape(rows, -1).astype(jnp.bfloat16)
    d_key = (
        jnp.einsum(
            "hrs,rhd->shd",
            d_scores,
            query.reshape(rows, -1, DK),
            preferred_element_type=jnp.float32,
        )
        * 0.125
    )
    d_key = d_key.reshape(cols, -1).astype(jnp.bfloat16)
    g_in = jnp.stack(
        [
            product_left(x_query, d_query),
            product_left(x_keys, d_key),
            product_left(x_keys, d_value),
        ],
        axis=1,
    )
    d_in_query = product_right(d_query, w_in[:, 0])
    d_in_keys = product_right(d_key, w_in[:, 1]) + product_right(d_value, w_in[:, 2])
    return (g_in, g_out, d_in_query, d_in_keys)


def gated(gate, upper):
    return jax.nn.gelu(gate, approximate=True) * upper


def expand(x_in, w_in, w_out):
    gate = product(x_in, w_in[:, 0])
    upper = product(x_in, w_in[:, 1])
    hidden = gated(gate, upper).astype(jnp.bfloat16)
    return (product(hidden, w_out), (gate, upper, hidden))


def expand_back(x_in, w_in, w_out, kept, d_full):
    gate, upper, hidden = kept
    g_out = product_left(hidden, d_full)
    _, pull = jax.vjp(gated, gate, upper)
    d_gate, d_upper = pull(product_right(d_full, w_out))
    d_gate = d_gate.astype(jnp.bfloat16)
    d_upper = d_upper.astype(jnp.bfloat16)
    g_in = jnp.stack([product_left(x_in, d_gate), product_left(x_in, d_upper)], axis=1)
    return (g_in, g_out, product_right(d_gate, w_in[:, 0]) + product_right(d_upper, w_in[:, 1]))


def vocab_table(ids, vocab_rows):
    start = lax.axis_index("mp") * vocab_rows
    return ids[:, None] == start + jnp.arange(vocab_rows, dtype=jnp.int32)[None, :]


def combine_stats(first, second):
    peak = jnp.maximum(first[0], second[0])
    total = first[1] * jnp.exp(first[0] - peak) + second[1] * jnp.exp(second[0] - peak)
    return (peak, total, first[2] + second[2])


def micro_grads(weights, gains, count, source, target, source_len, target_len):
    w_table, w_head, w_attn_in, w_attn_out, w_feed_in, w_feed_out = weights
    vocab_rows = w_table.shape[0]
    src_pos = jnp.arange(source.shape[0], dtype=jnp.int32)
    tgt_pos = jnp.arange(target.shape[0], dtype=jnp.int32)
    key_bias = jnp.where(src_pos < source_len, 0.0, masked)[None, None, :]
    causal = jnp.where(tgt_pos[:, None] >= tgt_pos[None, :], 0.0, masked)[None]
    source_hot = vocab_table(source, vocab_rows).astype(jnp.bfloat16)
    shifted = jnp.concatenate([jnp.zeros((1,), jnp.int32), target[:-1]])
    target_hot = vocab_table(shifted, vocab_rows).astype(jnp.bfloat16)
    src_embed = spread(product(source_hot, w_table))
    src_norm_a = normalize(src_embed, gains[0])
    part, keep_src_a = attend(src_norm_a, src_norm_a, w_attn_in[0], w_attn_out[0], key_bias)
    src_mid = src_embed + spread(part)
    src_norm_b = normalize(src_mid, gains[1])
    part, keep_src_b = expand(src_norm_b, w_feed_in[0], w_feed_out[0])
    src_top = src_mid + spread(part)
    encoded = normalize(src_top, gains[2])
    tgt_embed = spread(product(target_hot, w_table))
    tgt_norm_a = normalize(tgt_embed, gains[3])
    part, keep_tgt_a = attend(tgt_norm_a, tgt_norm_a, w_attn_in[1], w_attn_out[1], causal)
    tgt_self = tgt_embed + spread(part)
    tgt_norm_b = normalize(tgt_self, gains[4])
    part, keep_tgt_b = attend(tgt_norm_b, encoded, w_attn_in[2], w_attn_out[2], key_bias)
    tgt_cross = tgt_self + spread(part)
    tgt_norm_c = normalize(tgt_cross, gains[5])
    part, keep_tgt_c = expand(tgt_norm_c, w_feed_in[1], w_feed_out[1])
    tgt_top = tgt_cross + spread(part)
    tgt_norm_d = normalize(tgt_top, gains[6])
    logits = product(tgt_norm_d, w_head)
    hits = vocab_table(target, vocab_rows)
    peak = jnp.max(logits, axis=-1)
    total = jnp.sum(jnp.exp(logits - peak[:, None]), axis=-1)
    picked = jnp.sum(jnp.where(hits, logits, 0.0), axis=-1)
    peak, total, picked = joined((peak, total, picked), "mp", combine_stats)
    lse = peak + jnp.log(total)
    weight = (tgt_pos < target_len).astype(jnp.float32) / count
    own_rows = tgt_embed.shape[0]
    loss = jnp.sum(
        lax.dynamic_slice_in_dim((lse - picked) * weight, lax.axis_index("mp") * own_rows, own_rows)
    )
    d_logits = (
        (jnp.exp(logits - lse[:, None]) - hits.astype(jnp.float32)) * weight[:, None]
    ).astype(jnp.bfloat16)
    g_head = product_left(tgt_norm_d, d_logits)
    d_tgt, gain_six = norm_back(tgt_top, gains[6], push_rows(product_right(d_logits, w_head)))
    feed_in_one, feed_out_one, d_in = expand_back(
        tgt_norm_c, w_feed_in[1], w_feed_out[1], keep_tgt_c, pull_rows(d_tgt)
    )
    d_more, gain_five = norm_back(tgt_cross, gains[5], push_rows(d_in))
    d_tgt = d_tgt + d_more
    attn_in_two, attn_out_two, d_query, d_keys = attend_back(
        tgt_norm_b, encoded, w_attn_in[2], w_attn_out[2], key_bias, keep_tgt_b, pull_rows(d_tgt)
    )
    d_query, d_encoded = push_rows((d_query, d_keys))
    d_more, gain_four = norm_back(tgt_self, gains[4], d_query)
    d_tgt = d_tgt + d_more
    attn_in_one, attn_out_one, d_query, d_keys = attend_back(
        tgt_norm_a, tgt_norm_a, w_attn_in[1], w_attn_out[1], causal, keep_tgt_a, pull_rows(d_tgt)
    )
    d_more, gain_three = norm_back(tgt_embed, gains[3], push_rows(d_query + d_keys))
    d_tgt = d_tgt + d_more
    g_table = product_left(target_hot, pull_rows(d_tgt))
    d_src, gain_two = norm_back(src_top, gains[2], d_encoded)
    feed_in_zero, feed_out_zero, d_in = expand_back(
        src_norm_b, w_feed_in[0], w_feed_out[0], keep_src_b, pull_rows(d_src)
    )
    d_more, gain_one = norm_back(src_mid, gains[1], push_rows(d_in))
    d_src = d_src + d_more
    attn_in_zero, attn_out_zero, d_query, d_keys = attend_back(
        src_norm_a, src_norm_a, w_attn_in[0], w_attn_out[0], key_bias, keep_src_a, pull_rows(d_src)
    )
    d_more, gain_zero = norm_back(src_embed, gains[0], push_rows(d_query + d_keys))
    d_src = d_src + d_more
    g_table = g_table + product_left(source_hot, pull_rows(d_src))
    g_mats = (
        g_table,
        g_head,
        jnp.stack([attn_in_zero, attn_in_one, attn_in_two]),
        jnp.stack([attn_out_zero, attn_out_one, attn_out_two]),
        jnp.stack([feed_in_zero, feed_in_one]),
        jnp.stack([feed_out_zero, feed_out_one]),
    )
    g_gains = jnp.stack([gain_zero, gain_one, gain_two, gain_three, gain_four, gain_five, gain_six])
    return (g_mats, g_gains, loss)


def adam(weight, grad, first, second, step_rate):
    first = beta_one * first + (1 - beta_one) * grad
    second = beta_two * second + (1 - beta_two) * grad * grad
    step_size = first / (1 - beta_one**STEP) / (jnp.sqrt(second / (1 - beta_two**STEP)) + adam_eps)
    return (weight - step_rate * (step_size + decay * weight), first, second)


def on_device(
    source_ids,
    target_ids,
    source_lengths,
    target_lengths,
    embedding,
    unembedding,
    attention_in,
    attention_out,
    feed_in,
    feed_out,
    norm_gains,
    embedding_first,
    unembedding_first,
    attention_in_first,
    attention_out_first,
    feed_in_first,
    feed_out_first,
    norm_gains_first,
    embedding_second,
    unembedding_second,
    attention_in_second,
    attention_out_second,
    feed_in_second,
    feed_out_second,
    norm_gains_second,
):
    masters = (embedding, unembedding, attention_in, attention_out, feed_in, feed_out)
    weights = (
        lax.all_gather(embedding.astype(jnp.bfloat16), "dp", axis=1, tiled=True),
        lax.all_gather(unembedding.astype(jnp.bfloat16), "dp", axis=0, tiled=True),
        lax.all_gather(attention_in.astype(jnp.bfloat16), "dp", axis=1, tiled=True),
        lax.all_gather(attention_out.astype(jnp.bfloat16), "dp", axis=2, tiled=True),
        lax.all_gather(feed_in.astype(jnp.bfloat16), "dp", axis=1, tiled=True),
        lax.all_gather(feed_out.astype(jnp.bfloat16), "dp", axis=2, tiled=True),
    )
    full_gains = lax.all_gather(norm_gains, ("dp", "mp"), axis=1, tiled=True)
    count = lax.psum(jnp.sum(target_lengths).astype(jnp.float32), "dp")

    def one_batch(carry, batch):
        summed, gain_sum, loss_sum = carry
        source, target, source_len, target_len = batch
        g_mats, g_gains, loss = micro_grads(
            weights, full_gains, count, source, target, source_len, target_len
        )
        summed = tuple((a + g for a, g in zip(summed, g_mats)))
        return ((summed, gain_sum + g_gains, loss_sum + loss), None)

    start = tuple((jnp.zeros(w.shape, jnp.float32) for w in weights))
    batches = (source_ids[:, 0], target_ids[:, 0], source_lengths[:, 0], target_lengths[:, 0])
    init = (start, jnp.zeros(full_gains.shape, jnp.float32), jnp.zeros((), jnp.float32))
    (summed, gain_sum, loss_sum), _ = lax.scan(one_batch, init, batches)
    reduced = (
        lax.psum_scatter(
            summed[0].astype(jnp.bfloat16), "dp", scatter_dimension=1, tiled=True
        ).astype(jnp.float32),
        lax.psum_scatter(
            summed[1].astype(jnp.bfloat16), "dp", scatter_dimension=0, tiled=True
        ).astype(jnp.float32),
        lax.psum_scatter(
            summed[2].astype(jnp.bfloat16), "dp", scatter_dimension=1, tiled=True
        ).astype(jnp.float32),
        lax.psum_scatter(
            summed[3].astype(jnp.bfloat16), "dp", scatter_dimension=2, tiled=True
        ).astype(jnp.float32),
        lax.psum_scatter(
            summed[4].astype(jnp.bfloat16), "dp", scatter_dimension=1, tiled=True
        ).astype(jnp.float32),
        lax.psum_scatter(
            summed[5].astype(jnp.bfloat16), "dp", scatter_dimension=2, tiled=True
        ).astype(jnp.float32),
    )
    gain_grad = lax.psum_scatter(gain_sum, ("dp", "mp"), scatter_dimension=1, tiled=True)
    grads = tuple(reduced) + (gain_grad,)
    local_squares = sum((jnp.sum(g * g) for g in grads))
    squares, loss = lax.psum((local_squares, loss_sum), ("dp", "mp"))
    grad_norm = jnp.sqrt(squares)
    scale = jnp.minimum(1.0, clip_limit / grad_norm)
    states = tuple(masters) + (norm_gains,)
    firsts = (
        embedding_first,
        unembedding_first,
        attention_in_first,
        attention_out_first,
        feed_in_first,
        feed_out_first,
        norm_gains_first,
    )
    seconds = (
        embedding_second,
        unembedding_second,
        attention_in_second,
        attention_out_second,
        feed_in_second,
        feed_out_second,
        norm_gains_second,
    )
    results = [
        adam(w, g * scale, m, v, r)
        for w, g, m, v, r in zip(states, grads, firsts, seconds, step_rates)
    ]
    news = tuple((r[0] for r in results))
    moms = tuple((r[1] for r in results))
    secs = tuple((r[2] for r in results))
    return (
        loss,
        grad_norm,
        news[0],
        news[1],
        news[2],
        news[3],
        news[4],
        news[5],
        news[6],
        moms[0],
        moms[1],
        moms[2],
        moms[3],
        moms[4],
        moms[5],
        moms[6],
        secs[0],
        secs[1],
        secs[2],
        secs[3],
        secs[4],
        secs[5],
        secs[6],
    )


def solution(mesh):
    placed = (
        P(None, "dp", None),
        P(None, "dp", None),
        P(None, "dp"),
        P(None, "dp"),
        P("mp", "dp"),
        P("dp", "mp"),
        P(None, "dp", None, "mp"),
        P(None, "mp", "dp"),
        P(None, "dp", None, "mp"),
        P(None, "mp", "dp"),
        P(None, ("dp", "mp")),
        P("mp", "dp"),
        P("dp", "mp"),
        P(None, "dp", None, "mp"),
        P(None, "mp", "dp"),
        P(None, "dp", None, "mp"),
        P(None, "mp", "dp"),
        P(None, ("dp", "mp")),
        P("mp", "dp"),
        P("dp", "mp"),
        P(None, "dp", None, "mp"),
        P(None, "mp", "dp"),
        P(None, "dp", None, "mp"),
        P(None, "mp", "dp"),
        P(None, ("dp", "mp")),
    )
    return jax.shard_map(
        on_device,
        mesh=mesh,
        in_specs=placed,
        out_specs=(
            P(),
            P(),
            P("mp", "dp"),
            P("dp", "mp"),
            P(None, "dp", None, "mp"),
            P(None, "mp", "dp"),
            P(None, "dp", None, "mp"),
            P(None, "mp", "dp"),
            P(None, ("dp", "mp")),
            P("mp", "dp"),
            P("dp", "mp"),
            P(None, "dp", None, "mp"),
            P(None, "mp", "dp"),
            P(None, "dp", None, "mp"),
            P(None, "mp", "dp"),
            P(None, ("dp", "mp")),
            P("mp", "dp"),
            P("dp", "mp"),
            P(None, "dp", None, "mp"),
            P(None, "mp", "dp"),
            P(None, "dp", None, "mp"),
            P(None, "mp", "dp"),
            P(None, ("dp", "mp")),
        ),
        check_vma=False,
    )
```

profile of v0, /device:TPU:0, one launch (start us, length us, event | category | flops | bytes accessed | tf_op | source)
XLA Modules:
  0.0 3401.4 jit_solution(12093368368837299163)
XLA Ops:
  44.2 32.8 all_gather.201
  77.2 39.5 %all-gather.6 = f32[32,48,7]{1,2,0:T(8,128)S(1)} all-gather(f32[1,48,7]{1,2,0:T(8,128)S(1)} %bitcast.869), channel_id=1, replica_groups=mesh['dp'=8,'mp'=4] {'dp','mp'}, dimensions={0}, use_global_device_ids=true | all-gather | bytes 44352 | tf_op jit(solution)/shard_map/all_gather | solution.py:314
  118.7 34.9 %all_gather.207 = bf16[1536,96]{1,0:T(8,128)(2,1)} all-gather(bf16[192,96]{1,0:T(8,128)(2,1)S(1)} %convert_element_type.728), channel_id=1, replica_groups=mesh['dp'=8,'mp'=4] {'dp'}, dimensions={0}, use_global_device_ids=true | all-gather | bytes 331776 | tf_op jit(solution)/shard_map/all_gather | solution.py:308
  157.8 64.5 %all-gather.27.cloned.1.call-done = bf16[3,1536,3,192]{3,2,0,1:T(4,128)(2,1)} async-done(((bf16[3,192,3,192]{3,2,0,1:T(4,128)(2,1)}), bf16[3,1536,3,192]{3,2,0,1:T(4,128)(2,1)}) %all-gather.27.cloned.1.call-update) | async-done | bytes 5308432 | tf_op jit(solution)/shard_map/all_gather | solution.py:309
  236.6 85.8 %all-gather.33.cloned.1.call-done = bf16[2,992,1536]{1,0,2:T(2,128)(2,1)} async-done(((bf16[2,992,192]{1,0,2:T(2,128)(2,1)}), bf16[2,992,1536]{1,0,2:T(2,128)(2,1)}) %all-gather.33.cloned.1.call-update) | async-done | bytes 6094864 | tf_op jit(solution)/shard_map/all_gather | solution.py:312
  338.8 160.6 %all-gather.31.cloned.1.call-done = bf16[2,1536,2,992]{3,2,0,1:T(2,128)(2,1)} async-done(((bf16[2,192,2,992]{3,2,0,1:T(2,128)(2,1)}), bf16[2,1536,2,992]{3,2,0,1:T(2,128)(2,1)}) %all-gather.31.cloned.1.call-update) | async-done | bytes 12189712 | tf_op jit(solution)/shard_map/all_gather | solution.py:311
  499.4 31.1 copy.182
  530.5 2022.4 %while.75 = (s32[]{:T(128)}, f32[96,1536]{1,0:T(8,128)}, f32[1536,96]{0,1:T(8,128)}, f32[3,1536,3,192]{1,3,2,0:T(8,128)}, f32[3,192,1536]{2,1,0:T(8,128)}, /*ind...) while((s32[]{:T(128)}, f32[96,1536]{1,0:T(8,128)}, ...), condition=%wide.region_53.54_spmd.clone, body=%wide.region_2.53_spmd.clone.sunk | while | flops 53058658304 | bytes 1822317952 | solution.py:329
  537.4 55.2 %reduce-scatter.54.cloned.1.call-done = f32[256,1536]{1,0:T(8,128)} async-done(((f32[1024,1536]{1,0:T(8,128)}), f32[256,1536]{1,0:T(8,128)}) %reduce-scatter.54.cloned.1.call-update) | async-done | bytes 1572880 | tf_op jit(solution)/shard_map/while/body/eval_jaxpr/reduce_scatter | solution.py:36
  643.5 58.9 %reduce-scatter.56.cloned.1.call-done = f32[256,1536]{1,0:T(8,128)} async-done(((f32[1024,1536]{1,0:T(8,128)}), f32[256,1536]{1,0:T(8,128)}) %reduce-scatter.56.cloned.1.call-update) | async-done | bytes 1572880 | tf_op jit(solution)/shard_map/while/body/eval_jaxpr/reduce_scatter | solution.py:36
  781.3 45.2 %reduce-scatter.58.cloned.1.call-done = f32[256,1536]{1,0:T(8,128)} async-done(((f32[1024,1536]{1,0:T(8,128)}), f32[256,1536]{1,0:T(8,128)}) %reduce-scatter.58.cloned.1.call-update) | async-done | bytes 1572880 | tf_op jit(solution)/shard_map/while/body/eval_jaxpr/reduce_scatter | solution.py:36
  900.5 28.1 reduce-scatter.60.cloned.1.call-done
  1026.8 28.6 reduce-scatter.64.cloned.1.call-done
  1127.3 59.5 %reduce-scatter.72.cloned.1.call-done = f32[256,1536]{1,0:T(8,128)} async-done(((f32[1024,1536]{1,0:T(8,128)}), f32[256,1536]{1,0:T(8,128)}) %reduce-scatter.72.cloned.1.call-update) | async-done | bytes 1572880 | tf_op jit(solution)/shard_map/while/body/eval_jaxpr/reduce_scatter | solution.py:44
  1190.6 28.6 all-gather.41.cloned.1.call-done
  1249.5 53.4 %reduce-scatter.74.cloned.1.call-done = f32[256,1536]{1,0:T(8,128)} async-done(((f32[1024,1536]{1,0:T(8,128)}), f32[256,1536]{1,0:T(8,128)}) %reduce-scatter.74.cloned.1.call-update) | async-done | bytes 1572880 | tf_op jit(solution)/shard_map/while/body/eval_jaxpr/reduce_scatter | solution.py:44
  1536.2 57.2 %reduce-scatter.54.cloned.1.call-done = f32[256,1536]{1,0:T(8,128)} async-done(((f32[1024,1536]{1,0:T(8,128)}), f32[256,1536]{1,0:T(8,128)}) %reduce-scatter.54.cloned.1.call-update) | async-done | bytes 1572880 | tf_op jit(solution)/shard_map/while/body/eval_jaxpr/reduce_scatter | solution.py:36
  1644.2 58.9 %reduce-scatter.56.cloned.1.call-done = f32[256,1536]{1,0:T(8,128)} async-done(((f32[1024,1536]{1,0:T(8,128)}), f32[256,1536]{1,0:T(8,128)}) %reduce-scatter.56.cloned.1.call-update) | async-done | bytes 1572880 | tf_op jit(solution)/shard_map/while/body/eval_jaxpr/reduce_scatter | solution.py:36
  1782.0 45.2 %reduce-scatter.58.cloned.1.call-done = f32[256,1536]{1,0:T(8,128)} async-done(((f32[1024,1536]{1,0:T(8,128)}), f32[256,1536]{1,0:T(8,128)}) %reduce-scatter.58.cloned.1.call-update) | async-done | bytes 1572880 | tf_op jit(solution)/shard_map/while/body/eval_jaxpr/reduce_scatter | solution.py:36
  1901.3 28.1 reduce-scatter.60.cloned.1.call-done
  2027.6 28.7 reduce-scatter.64.cloned.1.call-done
  2128.5 59.5 %reduce-scatter.72.cloned.1.call-done = f32[256,1536]{1,0:T(8,128)} async-done(((f32[1024,1536]{1,0:T(8,128)}), f32[256,1536]{1,0:T(8,128)}) %reduce-scatter.72.cloned.1.call-update) | async-done | bytes 1572880 | tf_op jit(solution)/shard_map/while/body/eval_jaxpr/reduce_scatter | solution.py:44
  2191.8 28.6 all-gather.41.cloned.1.call-done
  2250.7 53.4 %reduce-scatter.74.cloned.1.call-done = f32[256,1536]{1,0:T(8,128)} async-done(((f32[1024,1536]{1,0:T(8,128)}), f32[256,1536]{1,0:T(8,128)}) %reduce-scatter.74.cloned.1.call-update) | async-done | bytes 1572880 | tf_op jit(solution)/shard_map/while/body/eval_jaxpr/reduce_scatter | solution.py:44
  2660.9 31.8 copy.222
  2692.7 28.4 reshape.643
  2739.1 46.9 %reduce-scatter.38.cloned.1.call-done = bf16[192,96]{1,0:T(8,128)(2,1)} async-done(((bf16[1536,96]{1,0:T(8,128)(2,1)}), bf16[192,96]{1,0:T(8,128)(2,1)}) %reduce-scatter.38.cloned.1.call-update) | async-done | bytes 36880
  2789.4 66.3 %reduce-scatter.42.cloned.1.call-done = bf16[192,576]{1,0:T(8,128)(2,1)} async-done(((bf16[1536,576]{1,0:T(8,128)(2,1)}), bf16[192,576]{1,0:T(8,128)(2,1)}) %reduce-scatter.42.cloned.1.call-update) | async-done | bytes 221200
  2857.9 107.3 %reduce-scatter.40.cloned.1.call-done = bf16[192,1728]{1,0:T(8,128)(2,1)} async-done(((bf16[1536,1728]{1,0:T(8,128)(2,1)}), bf16[192,1728]{1,0:T(8,128)(2,1)}) %reduce-scatter.40.cloned.1.call-update) | async-done | bytes 663568
  2971.2 114.9 %reduce-scatter.46.cloned.1.call-done = bf16[192,1984]{1,0:T(8,128)(2,1)} async-done(((bf16[1536,1984]{1,0:T(8,128)(2,1)}), bf16[192,1984]{1,0:T(8,128)(2,1)}) %reduce-scatter.46.cloned.1.call-update) | async-done | bytes 761872
  3091.6 199.3 %reduce-scatter.44.cloned.1.call-done = bf16[192,3968]{1,0:T(8,128)(2,1)} async-done(((bf16[1536,3968]{1,0:T(8,128)(2,1)}), bf16[192,3968]{1,0:T(8,128)(2,1)}) %reduce-scatter.44.cloned.1.call-update) | async-done | bytes 1523728
  3301.7 40.0 %all-reduce = (f32[]{:T(128)}, f32[]{:T(128)}) all-reduce(f32[]{:T(128)} %get-tuple-element.656, f32[]{:T(128)S(6)} %add.824), channel_id=1, replica_groups=mesh['dp'=8,'mp'=4] {'dp','mp'}, use_global_device_ids=true, to_apply=%region_54.55 | all-reduce | flops 2 | bytes 16 | tf_op jit(solution)/shard_map/psum | solution.py:353
  (1415 shorter events, 1590.8 us)
Async XLA Ops:
  7.2 146.4 %all-gather.29.cloned.1.call-start = ((), (), s32[]{:S(2)}) async-start(), calls=%async_computation.22 | async-start | bytes 3538944 | tf_op jit(solution)/shard_map/all_gather | solution.py:310
  9.5 212.9 %all-gather.27.cloned.1.call-start = ((), (), s32[]{:S(2)}) async-start(), calls=%async_computation.21 | async-start | bytes 10616832 | tf_op jit(solution)/shard_map/all_gather | solution.py:309
  11.5 311.0 %all-gather.33.cloned.1.call-start = ((), (), s32[]{:S(2)}) async-start(), calls=%async_computation.24 | async-start | bytes 7077888 | tf_op jit(solution)/shard_map/all_gather | solution.py:312
  15.1 484.3 %all-gather.31.cloned.1.call-start = ((), (), s32[]{:S(2)}) async-start(), calls=%async_computation.23 | async-start | bytes 14155776 | tf_op jit(solution)/shard_map/all_gather | solution.py:311
  596.8 105.6 %reduce-scatter.56.cloned.1.call-start = ((), (), s32[]{:S(2)}) async-start(), calls=%async_computation.36 | async-start | bytes 7864320 | tf_op jit(solution)/shard_map/while/body/eval_jaxpr/reduce_scatter | solution.py:36
  708.2 118.3 %reduce-scatter.58.cloned.1.call-start = ((), (), s32[]{:S(2)}) async-start(), calls=%async_computation.38 | async-start | bytes 7864320 | tf_op jit(solution)/shard_map/while/body/eval_jaxpr/reduce_scatter | solution.py:36
  781.3 106.9 %all-gather.39.cloned.1.call-start = ((), (), s32[]{:S(2)}) async-start(), calls=%async_computation.39 | async-start | bytes 3932160 | tf_op jit(solution)/shard_map/while/body/eval_jaxpr/all_gather | solution.py:32
  949.7 105.7 %reduce-scatter.64.cloned.1.call-start = ((), (), s32[]{:S(2)}) async-start(), calls=%async_computation.42 | async-start | bytes 1966080 | tf_op jit(solution)/shard_map/while/body/eval_jaxpr/reduce_scatter | solution.py:44
  1075.7 111.1 %reduce-scatter.72.cloned.1.call-start = ((), (), s32[]{:S(2)}) async-start(), calls=%async_computation.46 | async-start | bytes 7864320 | tf_op jit(solution)/shard_map/while/body/eval_jaxpr/reduce_scatter | solution.py:44
  1190.6 112.4 %reduce-scatter.74.cloned.1.call-start = ((), (), s32[]{:S(2)}) async-start(), calls=%async_computation.48 | async-start | bytes 7864320 | tf_op jit(solution)/shard_map/while/body/eval_jaxpr/reduce_scatter | solution.py:44
  1249.5 115.1 %all-gather.43.cloned.1.call-start = ((), (), s32[]{:S(2)}) async-start(), calls=%async_computation.49 | async-start | bytes 3932160 | tf_op jit(solution)/shard_map/while/body/eval_jaxpr/all_gather | solution.py:40
  1307.7 123.1 %reduce-scatter.70.cloned.1.call-start = ((), (), s32[]{:S(2)}) async-start(), calls=%async_computation.45 | async-start | bytes 1966080 | tf_op jit(solution)/shard_map/while/body/eval_jaxpr/reduce_scatter | solution.py:44
  1351.5 137.6 %reduce-scatter.76.cloned.1.call-start = ((), (), s32[]{:S(2)}) async-start(), calls=%async_computation.50 | async-start | bytes 7864320 | tf_op jit(solution)/shard_map/while/body/eval_jaxpr/reduce_scatter | solution.py:44
  1397.2 128.6 %all-gather.45.cloned.1.call-start = ((), (), s32[]{:S(2)}) async-start(), calls=%async_computation.51 | async-start | bytes 3932160 | tf_op jit(solution)/shard_map/while/body/eval_jaxpr/all_gather | solution.py:40
  1597.5 105.6 %reduce-scatter.56.cloned.1.call-start = ((), (), s32[]{:S(2)}) async-start(), calls=%async_computation.36 | async-start | bytes 7864320 | tf_op jit(solution)/shard_map/while/body/eval_jaxpr/reduce_scatter | solution.py:36
  1708.9 118.3 %reduce-scatter.58.cloned.1.call-start = ((), (), s32[]{:S(2)}) async-start(), calls=%async_computation.38 | async-start | bytes 7864320 | tf_op jit(solution)/shard_map/while/body/eval_jaxpr/reduce_scatter | solution.py:36
  1753.4 105.0 %reduce-scatter.52.cloned.1.call-start = ((), (), s32[]{:S(2)}) async-start(), calls=%async_computation.33 | async-start | bytes 1966080 | tf_op jit(solution)/shard_map/while/body/eval_jaxpr/reduce_scatter | solution.py:36
  1782.0 107.1 %all-gather.39.cloned.1.call-start = ((), (), s32[]{:S(2)}) async-start(), calls=%async_computation.39 | async-start | bytes 3932160 | tf_op jit(solution)/shard_map/while/body/eval_jaxpr/all_gather | solution.py:32
  1950.6 105.7 %reduce-scatter.64.cloned.1.call-start = ((), (), s32[]{:S(2)}) async-start(), calls=%async_computation.42 | async-start | bytes 1966080 | tf_op jit(solution)/shard_map/while/body/eval_jaxpr/reduce_scatter | solution.py:44
  2076.6 111.3 %reduce-scatter.72.cloned.1.call-start = ((), (), s32[]{:S(2)}) async-start(), calls=%async_computation.46 | async-start | bytes 7864320 | tf_op jit(solution)/shard_map/while/body/eval_jaxpr/reduce_scatter | solution.py:44
  2191.7 112.4 %reduce-scatter.74.cloned.1.call-start = ((), (), s32[]{:S(2)}) async-start(), calls=%async_computation.48 | async-start | bytes 7864320 | tf_op jit(solution)/shard_map/while/body/eval_jaxpr/reduce_scatter | solution.py:44
  2250.6 115.2 %all-gather.43.cloned.1.call-start = ((), (), s32[]{:S(2)}) async-start(), calls=%async_computation.49 | async-start | bytes 3932160 | tf_op jit(solution)/shard_map/while/body/eval_jaxpr/all_gather | solution.py:40
  2308.8 123.3 %reduce-scatter.70.cloned.1.call-start = ((), (), s32[]{:S(2)}) async-start(), calls=%async_computation.45 | async-start | bytes 1966080 | tf_op jit(solution)/shard_map/while/body/eval_jaxpr/reduce_scatter | solution.py:44
  2352.8 146.3 %reduce-scatter.76.cloned.1.call-start = ((), (), s32[]{:S(2)}) async-start(), calls=%async_computation.50 | async-start | bytes 7864320 | tf_op jit(solution)/shard_map/while/body/eval_jaxpr/reduce_scatter | solution.py:44
  2398.5 146.5 %all-gather.45.cloned.1.call-start = ((), (), s32[]{:S(2)}) async-start(), calls=%async_computation.51 | async-start | bytes 3932160 | tf_op jit(solution)/shard_map/while/body/eval_jaxpr/all_gather | solution.py:40
  2552.9 183.9 %reduce-scatter.48.cloned.1.call-start = ((), (), s32[]{:S(2)}) async-start(), calls=%async_computation.31 | async-start | bytes 811008
  2555.1 183.1 %reduce-scatter.36.cloned.1.call-start = ((), (), s32[]{:S(2)}) async-start(), calls=%async_computation.25 | async-start | bytes 442368
  2558.9 227.1 %reduce-scatter.38.cloned.1.call-start = ((), (), s32[]{:S(2)}) async-start(), calls=%async_computation.26 | async-start | bytes 442368
  2562.6 293.1 %reduce-scatter.42.cloned.1.call-start = ((), (), s32[]{:S(2)}) async-start(), calls=%async_computation.28 | async-start | bytes 2211840
  2572.1 393.1 %reduce-scatter.40.cloned.1.call-start = ((), (), s32[]{:S(2)}) async-start(), calls=%async_computation.27 | async-start | bytes 6193152
  2611.0 475.2 %reduce-scatter.46.cloned.1.call-start = ((), (), s32[]{:S(2)}) async-start(), calls=%async_computation.30 | async-start | bytes 7077888
  2647.4 643.4 %reduce-scatter.44.cloned.1.call-start = ((), (), s32[]{:S(2)}) async-start(), calls=%async_computation.29 | async-start | bytes 13713408
  (421 other events, 6348.9 us)
Sparse Core Ops, SparseCore 0:
  10.8 68.6 all-gather.28
  82.2 140.1 all-gather.26
  225.1 97.3 all-gather.32
  325.1 174.2 all-gather.30
  535.6 57.0 reduce-scatter.53
  596.9 28.5 all-gather.34
  643.5 58.8 reduce-scatter.55
  767.6 58.8 reduce-scatter.57
  949.9 28.5 reduce-scatter.61
  1026.8 28.5 reduce-scatter.63
  1075.8 28.5 reduce-scatter.65
  1127.4 59.3 reduce-scatter.71
  1244.0 58.8 reduce-scatter.73
  1398.3 63.0 reduce-scatter.75
  1494.8 28.7 all-gather.44
  1534.3 59.0 reduce-scatter.53
  1644.2 58.8 reduce-scatter.55
  1768.3 58.8 reduce-scatter.57
  1950.7 28.5 reduce-scatter.61
  2027.7 28.5 reduce-scatter.63
  2076.7 28.5 reduce-scatter.65
  2128.5 59.3 reduce-scatter.71
  2245.2 58.8 reduce-scatter.73
  2399.4 63.0 reduce-scatter.75
  2504.8 29.1 all-gather.44
  2559.1 96.9 reduce-scatter.47
  2659.7 61.2 reduce-scatter.35
  2724.7 61.1 reduce-scatter.37
  2789.3 66.3 reduce-scatter.41
  2859.2 105.9 reduce-scatter.39
  2968.7 117.3 reduce-scatter.45
  3089.7 201.1 reduce-scatter.43
  (19 shorter events, 535.5 us)
where the time goes:
time: 3420 us; the launch traced here: 3400 us
  waiting for transfers between devices  1930 us (56%)
  local copies, waits for them, and re-layouts  385 us (11%)
  matrix products  367 us (11%)
  blocking collectives  343 us (10%)
  other arithmetic  340 us (10%)
    unnamed x18, waiting for transfers between devices  535 us
    reduce_scatter x14, waiting for transfers between devices, spread(): return lax.psum_scatter(part, 'mp', scatter_dimension=0, tiled=True)  505 us
    reduce_scatter x14, waiting for transfers between devices, push_rows(): return lax.psum_scatter(part, 'mp', scatter_dimension=0, tiled=True)  387 us
    unnamed x110, local copies, waits for them, and re-layouts  260 us
    all_gather x1, waiting for transfers between devices, on_device(): lax.all_gather(feed_in.astype(jnp.bfloat16), 'dp', axis=1, tiled=True)  161 us
    dot_general x42, matrix products, product(): return jnp.dot(left, right, preferred_element_type=jnp.float32)  115 us
    dot_general x38, matrix products, product_right(): lax.dot_general(left, right, (((1,), (1,)), ((), ())), preferred_element_...  113 us
    all_gather x6, waiting for transfers between devices, collect(): return lax.all_gather(part, 'mp', axis=0, tiled=True)  108 us
  transfers between devices with their start and end apart: 51, of which 42 were waited for; matrix products, arithmetic and copies ran while one was open for 20% of the time, Pallas kernels for 0%

commit v1 on v0

v1 whole, which is shorter than its diff:
```python
import jax
import jax.numpy as jnp
import numpy as np
from jax import lax
from jax.sharding import Mesh
from jax.sharding import PartitionSpec as P

DK = 64
STEP = 10


norm_eps = 1e-06
clip_limit = 0.05
step_rates = (0.4, 0.02, 0.02, 0.1, 0.02, 0.02, 0.25)
beta_one = 0.9
beta_two = 0.999
adam_eps = 1e-08
decay = 0.01
masked = -1000000000.0

half = jnp.bfloat16


def spin(part, axis, shift):
    size = lax.axis_size(axis)
    return lax.ppermute(part, axis, [(i, (i + shift) % size) for i in range(size)])


def flip(part, axis, bit):
    size = lax.axis_size(axis)
    return lax.ppermute(part, axis, [(i, i ^ bit) for i in range(size)])


def gather_rows(part, axis):
    pieces = [part] + [spin(part, axis, k) for k in range(1, lax.axis_size(axis))]
    return jnp.concatenate(pieces, axis=0)


def scatter_rows(part, axis):
    size = lax.axis_size(axis)
    rows = part.shape[0] // size
    total = part[:rows].astype(jnp.float32)
    for k in range(1, size):
        total = total + spin(part[k * rows : (k + 1) * rows], axis, -k).astype(jnp.float32)
    return total


def gather_unit(part, axes, inner_first):
    for axis in axes[:-1]:
        part = gather_rows(part, axis)
    if inner_first:
        part = gather_rows(part, axes[-1])
        return [part, spin(part, "y", 1)]
    other = spin(part, "y", 1)
    return [gather_rows(part, axes[-1]), gather_rows(other, axes[-1])]


def meet(own, sent):
    return own.astype(jnp.float32) + spin(sent, "y", 1).astype(jnp.float32)


def scatter_unit(parts, axes, inner_first):
    if inner_first:
        part = scatter_rows(meet(parts[0], parts[1]).astype(half), axes[-1])
    else:
        own, sent = [scatter_rows(p, axes[-1]).astype(half) for p in parts]
        part = meet(own, sent)
    for axis in axes[:-1][::-1]:
        part = scatter_rows(part.astype(half), axis)
    return part


def total_over(value, axes):
    for axis in axes:
        bit = 1
        while bit < lax.axis_size(axis):
            value = value + flip(value, axis, bit)
            bit *= 2
    return value


def in_order(own, other, axis):
    first = lax.axis_index(axis) == 0
    return jnp.where(
        first, jnp.concatenate([own, other], axis=1), jnp.concatenate([other, own], axis=1)
    )


def collect(own):
    return jnp.concatenate([own, spin(own, "c", 1)], axis=0)


def fold(part):
    rows = part.shape[0] // 2
    return part[:rows] + spin(part[rows:].astype(half), "c", 1).astype(jnp.float32)


def product(left, right):
    return jnp.dot(left, right, preferred_element_type=jnp.float32)


def product_left(left, right):
    return lax.dot_general(
        left, right, (((0,), (0,)), ((), ())), preferred_element_type=jnp.float32
    )


def product_right(left, right):
    return lax.dot_general(
        left, right, (((1,), (1,)), ((), ())), preferred_element_type=jnp.float32
    )


def rms_norm(stream, gain):
    return stream * lax.rsqrt(jnp.mean(stream * stream, axis=-1, keepdims=True) + norm_eps) * gain


def normalize(stream, gain):
    return rms_norm(stream, gain).astype(half)


def norm_back(stream, gain, grad):
    _, pull = jax.vjp(rms_norm, stream, gain)
    return pull(grad)


def heads(flat):
    return flat.reshape(flat.shape[0], -1, DK)


def score_block(query, key, bias):
    return (
        jnp.einsum("rhd,shd->hrs", heads(query), heads(key), preferred_element_type=jnp.float32)
        * 0.125
        + bias
    )


def attend(query, key, value, bias):
    scores = score_block(query, key, bias)
    peak = jnp.max(scores, axis=-1, keepdims=True)
    raw = jnp.exp(scores - peak)
    total = jnp.sum(raw, axis=-1, keepdims=True)
    probs = (raw / total).astype(half)
    mixed = jnp.einsum("hrs,shd->rhd", probs, heads(value), preferred_element_type=jnp.float32)
    mixed = mixed.reshape(query.shape[0], -1).astype(half)
    return mixed, peak + jnp.log(total)


def attend_back(query, key, value, lse, bias, d_mixed):
    rows = query.shape[0]
    cols = key.shape[0]
    d_heads = heads(d_mixed)
    probs = jnp.exp(score_block(query, key, bias) - lse)
    d_value = jnp.einsum(
        "hrs,rhd->shd", probs.astype(half), d_heads, preferred_element_type=jnp.float32
    )
    d_probs = jnp.einsum("rhd,shd->hrs", d_heads, heads(value), preferred_element_type=jnp.float32)
    d_scores = (probs * (d_probs - jnp.sum(probs * d_probs, axis=-1, keepdims=True))).astype(half)
    d_query = (
        jnp.einsum("hrs,shd->rhd", d_scores, heads(key), preferred_element_type=jnp.float32) * 0.125
    )
    d_key = (
        jnp.einsum("hrs,rhd->shd", d_scores, heads(query), preferred_element_type=jnp.float32)
        * 0.125
    )
    return (
        d_query.reshape(rows, -1).astype(half),
        d_key.reshape(cols, -1).astype(half),
        d_value.reshape(cols, -1).astype(half),
    )


def self_attention(x_in, blocks, bias):
    part = 0.0
    kept = []
    for block in blocks:
        width = block.shape[1] // 4
        qkv = product(x_in, block[:, : 3 * width]).astype(half)
        query, key, value = qkv[:, :width], qkv[:, width : 2 * width], qkv[:, 2 * width :]
        mixed, lse = attend(query, key, value, bias)
        part = part + product_right(mixed, block[:, 3 * width :])
        kept.append((query, key, value, lse, mixed))
    return part, kept


def self_attention_back(x_in, blocks, bias, kept, d_full):
    d_in = 0.0
    grads = []
    for block, (query, key, value, lse, mixed) in zip(blocks, kept):
        width = block.shape[1] // 4
        g_out = product_left(d_full, mixed).astype(half)
        d_mixed = product(d_full, block[:, 3 * width :]).astype(half)
        d_qkv = jnp.concatenate(attend_back(query, key, value, lse, bias, d_mixed), axis=1)
        g_in = product_left(x_in, d_qkv).astype(half)
        grads.append(jnp.concatenate([g_in, g_out], axis=1))
        d_in = d_in + product_right(d_qkv, block[:, : 3 * width])
    return grads, d_in


def cross_attention(x_in, x_keys, blocks, bias):
    part = 0.0
    kept = []
    for block in blocks:
        width = block.shape[1] // 4
        query = product(x_in, block[:, :width]).astype(half)
        pair = product(x_keys, block[:, width : 3 * width]).astype(half)
        key, value = pair[:, :width], pair[:, width:]
        mixed, lse = attend(query, key, value, bias)
        part = part + product_right(mixed, block[:, 3 * width :])
        kept.append((query, key, value, lse, mixed))
    return part, kept


def cross_attention_back(x_in, x_keys, blocks, bias, kept, d_full):
    d_in = 0.0
    d_keys = 0.0
    grads = []
    for block, (query, key, value, lse, mixed) in zip(blocks, kept):
        width = block.shape[1] // 4
        g_out = product_left(d_full, mixed).astype(half)
        d_mixed = product(d_full, block[:, 3 * width :]).astype(half)
        d_query, d_key, d_value = attend_back(query, key, value, lse, bias, d_mixed)
        d_pair = jnp.concatenate([d_key, d_value], axis=1)
        g_query = product_left(x_in, d_query).astype(half)
        g_pair = product_left(x_keys, d_pair).astype(half)
        grads.append(jnp.concatenate([g_query, g_pair, g_out], axis=1))
        d_in = d_in + product_right(d_query, block[:, :width])
        d_keys = d_keys + product_right(d_pair, block[:, width : 3 * width])
    return grads, d_in, d_keys


def gated(gate, upper):
    return jax.nn.gelu(gate, approximate=True) * upper


def expand(x_in, gates, uppers, downs):
    part = 0.0
    kept = []
    for w_gate, w_upper, w_down in zip(gates, uppers, downs):
        gate = product(x_in, w_gate)
        upper = product(x_in, w_upper)
        hidden = gated(gate, upper).astype(half)
        part = part + product_right(hidden, w_down)
        kept.append((gate, upper, hidden))
    return part, kept


def expand_back(x_in, gates, uppers, downs, kept, d_full):
    d_in = 0.0
    g_gates, g_uppers, g_downs = [], [], []
    for w_gate, w_upper, w_down, (gate, upper, hidden) in zip(gates, uppers, downs, kept):
        g_downs.append(product_left(d_full, hidden).astype(half))
        _, pull = jax.vjp(gated, gate, upper)
        d_gate, d_upper = pull(product(d_full, w_down))
        d_gate = d_gate.astype(half)
        d_upper = d_upper.astype(half)
        g_gates.append(product_left(x_in, d_gate).astype(half))
        g_uppers.append(product_left(x_in, d_upper).astype(half))
        d_in = d_in + product_right(d_gate, w_gate) + product_right(d_upper, w_upper)
    return g_gates, g_uppers, g_downs, d_in


def adam(weight, grad, first, second, step_rate):
    first = beta_one * first + (1 - beta_one) * grad
    second = beta_two * second + (1 - beta_two) * grad * grad
    step_size = first / (1 - beta_one**STEP) / (jnp.sqrt(second / (1 - beta_two**STEP)) + adam_eps)
    return (weight - step_rate * (step_size + decay * weight), first, second)


def own_part(whole, rows):
    return lax.dynamic_slice_in_dim(whole, lax.axis_index("c") * rows, rows)


def positions(rows):
    core = lax.axis_index("c")
    near = jnp.arange(rows, dtype=jnp.int32)
    return jnp.concatenate([core * rows + near, (1 - core) * rows + near])


def on_device(axes, *args):
    source_ids, target_ids, source_lengths, target_lengths = args[:4]
    masters, firsts, seconds = args[4:11], args[11:18], args[18:25]
    embedding, unembedding, attention_in, attention_out, feed_in, feed_out, norm_gains = masters
    row = lax.axis_index("y")
    core = lax.axis_index("c")
    everywhere = axes + ("y", "c")

    vocab_rows = embedding.shape[0]
    table_pair = jnp.concatenate([embedding.T.astype(half), unembedding.astype(half)], axis=1)
    table_pairs = gather_unit(table_pair, axes, True)
    table_pairs = table_pairs + [spin(p, "c", 1) for p in table_pairs]
    table_t = jnp.concatenate([p[:, :vocab_rows] for p in table_pairs], axis=1)
    w_head = jnp.concatenate([p[:, vocab_rows:] for p in table_pairs], axis=1)
    near = jnp.arange(vocab_rows, dtype=jnp.int32)
    vocab_ids = jnp.concatenate(
        [
            ((row ^ y_step) * 2 + (core ^ c_step)) * vocab_rows + near
            for c_step in (0, 1)
            for y_step in (0, 1)
        ]
    )

    own_count = jnp.sum(target_lengths).astype(jnp.float32)
    gain_part = jnp.concatenate(
        [norm_gains, jnp.full((1, norm_gains.shape[1]), own_count, jnp.float32)]
    )
    gain_part = in_order(gain_part, spin(gain_part, "c", 1), "c")
    gain_part = in_order(gain_part, spin(gain_part, "y", 1), "y")
    feature_rows = gain_part.shape[1]
    gain_part = gain_part.T
    for axis in axes:
        gain_part = gather_rows(gain_part, axis)
    gains = gain_part.T
    count = jnp.sum(gain_part[::feature_rows, -1])
    gains = gains[:-1]

    def attention_unit(layer):
        w_in = attention_in[layer].astype(half)
        w_in = w_in.reshape(w_in.shape[0], -1)
        return jnp.concatenate([w_in, attention_out[layer].T.astype(half)], axis=1)

    def feed_units(layer):
        return (
            feed_in[layer, :, 0].astype(half),
            feed_in[layer, :, 1].astype(half),
            feed_out[layer].T.astype(half),
        )

    attn_order = (True, False, False)
    feed_order = ((True, False, True), (False, True, False))
    attn = [None] * 3
    feed = [None] * 2
    attn[0] = gather_unit(attention_unit(0), axes, attn_order[0])
    feed[0] = [gather_unit(u, axes, o) for u, o in zip(feed_units(0), feed_order[0])]
    attn[1] = gather_unit(attention_unit(1), axes, attn_order[1])
    attn[2] = gather_unit(attention_unit(2), axes, attn_order[2])
    feed[1] = [gather_unit(u, axes, o) for u, o in zip(feed_units(1), feed_order[1])]

    source = lax.dynamic_index_in_dim(source_ids, row, 0, False)[0]
    target = lax.dynamic_index_in_dim(target_ids, row, 0, False)[0]
    source_len = lax.dynamic_index_in_dim(source_lengths, row, 0, False)[0]
    target_len = lax.dynamic_index_in_dim(target_lengths, row, 0, False)[0]
    src_rows = source.shape[0] // 2
    tgt_rows = target.shape[0] // 2
    src_pos = positions(src_rows)
    tgt_pos = positions(tgt_rows)
    key_bias = jnp.where(src_pos < source_len, 0.0, masked)[None, None, :]
    causal = jnp.where(tgt_pos[:, None] >= tgt_pos[None, :], 0.0, masked)[None]
    shifted = jnp.concatenate([jnp.zeros((1,), jnp.int32), target[:-1]])
    source_hot = (own_part(source, src_rows)[:, None] == vocab_ids[None, :]).astype(half)
    target_hot = (own_part(shifted, tgt_rows)[:, None] == vocab_ids[None, :]).astype(half)
    hits = own_part(target, tgt_rows)[:, None] == vocab_ids[None, :]

    src_embed = product_right(source_hot, table_t)
    src_norm_a = collect(normalize(src_embed, gains[0]))
    part, keep_src_a = self_attention(src_norm_a, attn[0], key_bias)
    src_mid = src_embed + fold(part)
    src_norm_b = collect(normalize(src_mid, gains[1]))
    part, keep_src_b = expand(src_norm_b, *feed[0])
    src_top = src_mid + fold(part)
    encoded = collect(normalize(src_top, gains[2]))

    tgt_embed = product_right(target_hot, table_t)
    tgt_norm_a = collect(normalize(tgt_embed, gains[3]))
    part, keep_tgt_a = self_attention(tgt_norm_a, attn[1], causal)
    tgt_self = tgt_embed + fold(part)
    tgt_norm_b = collect(normalize(tgt_self, gains[4]))
    part, keep_tgt_b = cross_attention(tgt_norm_b, encoded, attn[2], key_bias)
    tgt_cross = tgt_self + fold(part)
    tgt_norm_c = collect(normalize(tgt_cross, gains[5]))
    part, keep_tgt_c = expand(tgt_norm_c, *feed[1])
    tgt_top = tgt_cross + fold(part)
    tgt_norm_d = normalize(tgt_top, gains[6])

    logits = product(tgt_norm_d, w_head)
    peak = jnp.max(logits, axis=-1, keepdims=True)
    lse = peak + jnp.log(jnp.sum(jnp.exp(logits - peak), axis=-1, keepdims=True))
    picked = jnp.sum(jnp.where(hits, logits, 0.0), axis=-1, keepdims=True)
    weight = (tgt_pos[:tgt_rows] < target_len).astype(jnp.float32)[:, None] / count
    own_loss = jnp.sum((lse - picked) * weight)
    d_logits = ((jnp.exp(logits - lse) - hits.astype(jnp.float32)) * weight).astype(half)
    g_head = product_left(tgt_norm_d, d_logits).astype(half)

    attn_grads = [None] * 3
    feed_grads = [None] * 2
    d_tgt, gain_six = norm_back(tgt_top, gains[6], product_right(d_logits, w_head))
    *grads, d_in = expand_back(tgt_norm_c, *feed[1], keep_tgt_c, collect(d_tgt.astype(half)))
    feed_grads[1] = [scatter_unit(g, axes, o) for g, o in zip(grads, feed_order[1])]
    d_more, gain_five = norm_back(tgt_cross, gains[5], fold(d_in))
    d_tgt = d_tgt + d_more
    grads, d_query, d_keys = cross_attention_back(
        tgt_norm_b, encoded, attn[2], key_bias, keep_tgt_b, collect(d_tgt.astype(half))
    )
    attn_grads[2] = scatter_unit(grads, axes, attn_order[2])
    d_encoded = fold(d_keys)
    d_more, gain_four = norm_back(tgt_self, gains[4], fold(d_query))
    d_tgt = d_tgt + d_more
    grads, d_in = self_attention_back(
        tgt_norm_a, attn[1], causal, keep_tgt_a, collect(d_tgt.astype(half))
    )
    attn_grads[1] = scatter_unit(grads, axes, attn_order[1])
    d_more, gain_three = norm_back(tgt_embed, gains[3], fold(d_in))
    d_tgt = d_tgt + d_more

    d_src, gain_two = norm_back(src_top, gains[2], d_encoded)
    *grads, d_in = expand_back(src_norm_b, *feed[0], keep_src_b, collect(d_src.astype(half)))
    feed_grads[0] = [scatter_unit(g, axes, o) for g, o in zip(grads, feed_order[0])]
    d_more, gain_one = norm_back(src_mid, gains[1], fold(d_in))
    d_src = d_src + d_more
    grads, d_in = self_attention_back(
        src_norm_a, attn[0], key_bias, keep_src_a, collect(d_src.astype(half))
    )
    attn_grads[0] = scatter_unit(grads, axes, attn_order[0])
    d_more, gain_zero = norm_back(src_embed, gains[0], fold(d_in))
    d_src = d_src + d_more

    g_table = product_left(d_src.astype(half), source_hot)
    g_table = (g_table + product_left(d_tgt.astype(half), target_hot)).astype(half)
    pairs = [
        jnp.concatenate(
            [
                g_table[:, k * vocab_rows : (k + 1) * vocab_rows],
                g_head[:, k * vocab_rows : (k + 1) * vocab_rows],
            ],
            axis=1,
        )
        for k in range(4)
    ]
    pairs = [
        (a.astype(jnp.float32) + spin(b, "c", 1).astype(jnp.float32)).astype(half)
        for a, b in zip(pairs[:2], pairs[2:])
    ]
    pair_grad = scatter_unit(pairs, axes, True)

    g_gains = jnp.stack([gain_zero, gain_one, gain_two, gain_three, gain_four, gain_five, gain_six])
    g_gains = g_gains.T
    for axis in axes[::-1]:
        g_gains = scatter_rows(g_gains, axis)
    g_gains = total_over(g_gains, ("y", "c"))
    own_gains = norm_gains.shape[1]
    g_gains = lax.dynamic_slice_in_dim(g_gains, (row * 2 + core) * own_gains, own_gains).T

    width = attention_out.shape[1]
    units = [pair_grad] + attn_grads + feed_grads[0] + feed_grads[1]
    squares = sum(jnp.sum(g * g) for g in units) + jnp.sum(g_gains * g_gains)
    squares, loss = total_over(jnp.stack([squares, own_loss]), everywhere)
    grads = (
        pair_grad[:, :vocab_rows].T,
        pair_grad[:, vocab_rows:],
        jnp.stack([g[:, : 3 * width].reshape(-1, 3, width) for g in attn_grads]),
        jnp.stack([g[:, 3 * width :].T for g in attn_grads]),
        jnp.stack([jnp.stack([g[0], g[1]], axis=1) for g in feed_grads]),
        jnp.stack([g[2].T for g in feed_grads]),
        g_gains,
    )
    grad_norm = jnp.sqrt(squares)
    scale = jnp.minimum(1.0, clip_limit / grad_norm)
    results = [
        adam(w, g * scale, m, v, r)
        for w, g, m, v, r in zip(masters, grads, firsts, seconds, step_rates)
    ]
    return (loss, grad_norm) + tuple(r[i] for i in range(3) for r in results)


def solution(mesh):
    data = mesh.shape["dp"]
    sizes = [2]
    data //= 2
    while data > 1:
        size = 4 if data % 4 == 0 else data
        sizes.insert(0, size)
        data //= size
    axes = tuple(f"d{i}" for i in range(len(sizes)))
    devices = np.asarray(mesh.devices).reshape(tuple(sizes) + (mesh.shape["mp"] // 2, 2))
    inner = Mesh(devices, axes + ("y", "c"))
    dp = axes
    mp = ("y", "c")
    params = (
        P(mp, dp),
        P(dp, mp),
        P(None, dp, None, mp),
        P(None, mp, dp),
        P(None, dp, None, mp),
        P(None, mp, dp),
        P(None, dp + mp),
    )
    ids = (P(None, dp, None), P(None, dp, None), P(None, dp), P(None, dp))
    return jax.shard_map(
        lambda *args: on_device(axes, *args),
        mesh=inner,
        in_specs=ids + params * 3,
        out_specs=(P(), P()) + params * 3,
        check_vma=False,
    )
```

time: 3420 us -> 1890 us (0.55)
  waiting for transfers between devices: 1930 us -> 866 us
  blocking collectives: 343 us -> 0 us
  starting transfers between devices: 3.85 us -> 235 us
  other arithmetic: 340 us -> 183 us
  local copies, waits for them, and re-layouts: 385 us -> 272 us
  matrix products: 367 us -> 303 us
    reduce_scatter x28 -> x0, waiting for transfers between devices: 892 us -> none  [the longest x14 505 us: spread(): return lax.psum_scatter(part, 'mp', scatter_dimension=0, tiled=True)]
    ppermute x0 -> x153, waiting for transfers between devices: none -> 866 us  [the longest x146 835 us: spin(): lax.ppermute(part, axis, [(i, (i + shift) % size) for i in range(size)])]
    unnamed x18 -> x0, waiting for transfers between devices: 535 us -> none
    all_gather x16 -> x0, waiting for transfers between devices: 502 us -> none  [the longest x1 161 us: on_device(): lax.all_gather(feed_in.astype(jnp.bfloat16), 'dp', axis=1, tiled=True)]
    all_gather x25 -> x0, blocking collectives: 279 us -> none  [the longest x8 76.4 us: pull_rows(): return lax.all_gather(grad.astype(jnp.bfloat16), 'mp', axis=0, tiled=True)]
    ppermute x0 -> x153, starting transfers between devices: none -> 235 us  [the longest x146 233 us: spin(): lax.ppermute(part, axis, [(i, (i + shift) % size) for i in range(size)])]
    unnamed x110 -> x738, local copies, waits for them, and re-layouts: 260 us -> 82.2 us
    add x30 -> x20, other arithmetic: 97.1 us -> 5.12 us  [the longest x6 3.63 us: attend(): return (mixed, peak + jnp.log(total))]
  transfers between devices with their start and end apart: 51 -> 153, of which waited for: 42 -> 59; matrix products, arithmetic and copies ran while one was open for 20% -> 34% of each run, Pallas kernels for 0% -> 0%
where the time goes in v1:
time: 1890 us; the launch traced here: 1880 us
  waiting for transfers between devices  866 us (46%)
  matrix products  303 us (16%)
  local copies, waits for them, and re-layouts  272 us (14%)
  starting transfers between devices  235 us (12%)
  other arithmetic  183 us (10%)
    ppermute x146, waiting for transfers between devices, spin(): lax.ppermute(part, axis, [(i, (i + shift) % size) for i in range(size)])  835 us
    ppermute x146, starting transfers between devices, spin(): lax.ppermute(part, axis, [(i, (i + shift) % size) for i in range(size)])  233 us
    dot_general x27, matrix products, product(): return jnp.dot(left, right, preferred_element_type=jnp.float32)  91.5 us
    dot_general x29, matrix products, product_left(): lax.dot_general(left, right, (((0,), (0,)), ((), ())), preferred_element_...  86 us
    unnamed x738, local copies, waits for them, and re-layouts  82.2 us
    dot_general x29, matrix products, product_right(): lax.dot_general(left, right, (((1,), (1,)), ((), ())), preferred_element_...  72.1 us
    concatenate x20, local copies, waits for them, and re-layouts, gather_rows(): return jnp.concatenate(pieces, axis=0)  63.2 us
    ppermute x24, local copies, waits for them, and re-layouts, spin(): lax.ppermute(part, axis, [(i, (i + shift) % size) for i in range(size)])  51.7 us
  transfers between devices with their start and end apart: 153, of which 59 were waited for; matrix products, arithmetic and copies ran while one was open for 34% of the time, Pallas kernels for 0%

profile of v1, /device:TPU:0, one launch (start us, length us, event | category | flops | bytes accessed | tf_op | source)
XLA Modules:
  0.0 1876.6 jit_solution(14565463711172333388)
XLA Ops:
  77.1 23.7 %collective-permute-done.23 = bf16[192,768]{0,1:T(8,128)(2,1)S(1)} collective-permute-done((bf16[192,768]{0,1:T(8,128)(2,1)}, bf16[192,768]{0,1:T(8,128)(2,1)S(1)}, u32[]{:S(2)}, u32[]{:S(2)}) %collective-permute-start.23) | collective-permute-done | bytes 294944 | tf_op jit(solution)/shard_map/ppermute | solution.py:26
  102.0 19.4 %collective-permute-start.61 = (bf16[192,992]{1,0:T(8,128)(2,1)S(1)}, bf16[192,992]{1,0:T(8,128)(2,1)S(1)}, u32[]{:S(2)}, u32[]{:S(2)}) collective-permute-start(bf16[192,992]{1,0:T(8,128)(2,1)S(1)} %get-tuple-element.250), channel_id=1, source_target_pairs={{0,16},{8,24},{16,0},{24,8},{1,17},{9,25},{17,1},{25,9},{2,18},{10... | collective-permute-start | bytes 1142792 | tf_op jit(solution)/shard_map/ppermute | solution.py:26
  126.6 24.7 %collective-permute-done.15 = bf16[192,768]{0,1:T(8,128)(2,1)S(1)} collective-permute-done((bf16[192,768]{0,1:T(8,128)(2,1)}, bf16[192,768]{0,1:T(8,128)(2,1)S(1)}, u32[]{:S(2)}, u32[]{:S(2)}) %collective-permute-start.15) | collective-permute-done | bytes 294944 | tf_op jit(solution)/shard_map/ppermute | solution.py:26
  151.4 11.8 collective-permute-start.39
  165.4 19.7 %collective-permute-done.61 = bf16[192,992]{1,0:T(8,128)(2,1)S(1)} collective-permute-done((bf16[192,992]{1,0:T(8,128)(2,1)S(1)}, bf16[192,992]{1,0:T(8,128)(2,1)S(1)}, u32[]{:S(2)}, u32[]{:S(2)}) %collective-permute-start.61) | collective-permute-done | bytes 380960 | tf_op jit(solution)/shard_map/ppermute | solution.py:26
  189.6 12.3 collective-permute-done.39
  202.0 18.3 collective-permute-start.34
  235.8 23.3 %collective-permute-start.42 = (bf16[192,992]{0,1:T(8,128)(2,1)S(1)}, bf16[192,992]{0,1:T(8,128)(2,1)}, u32[]{:S(2)}, u32[]{:S(2)}) collective-permute-start(bf16[192,992]{0,1:T(8,128)(2,1)S(1)} %copy-done.83), channel_id=1, source_target_pairs={{0,8},{8,16},{16,24},{24,0},{1,9},{9,17},{17,25},{25,1},{2,10},{10... | collective-permute-start | bytes 1142792 | tf_op jit(solution)/shard_map/ppermute | solution.py:26
  268.3 11.1 collective-permute-done.43
  279.4 18.2 collective-permute-start.56
  323.0 56.1 %collective-permute-done.31 = bf16[1536,768]{0,1:T(8,128)(2,1)} collective-permute-done((bf16[1536,768]{0,1:T(8,128)(2,1)S(1)}, bf16[1536,768]{0,1:T(8,128)(2,1)}, u32[]{:S(2)}, u32[]{:S(2)}) %collective-permute-start.31) | collective-permute-done | bytes 2359328 | tf_op jit(solution)/shard_map/ppermute | solution.py:26
  409.2 31.6 %collective-permute-done.45 = bf16[768,992]{0,1:T(8,128)(2,1)S(1)} collective-permute-done((bf16[768,992]{0,1:T(8,128)(2,1)S(1)}, bf16[768,992]{0,1:T(8,128)(2,1)S(1)}, u32[]{:S(2)}, u32[]{:S(2)}) %collective-permute-start.45) | collective-permute-done | bytes 1523744 | tf_op jit(solution)/shard_map/ppermute | solution.py:26
  483.3 20.7 %collective-permute-done.37 = bf16[768,992]{0,1:T(8,128)(2,1)} collective-permute-done((bf16[768,992]{0,1:T(8,128)(2,1)}, bf16[768,992]{0,1:T(8,128)(2,1)}, u32[]{:S(2)}, u32[]{:S(2)}) %collective-permute-start.37) | collective-permute-done | bytes 1523744 | tf_op jit(solution)/shard_map/ppermute | solution.py:26
  539.7 22.9 %collective-permute-done.48 = bf16[768,992]{0,1:T(8,128)(2,1)S(1)} collective-permute-done((bf16[768,992]{0,1:T(8,128)(2,1)}, bf16[768,992]{0,1:T(8,128)(2,1)S(1)}, u32[]{:S(2)}, u32[]{:S(2)}) %collective-permute-start.48) | collective-permute-done | bytes 1523744 | tf_op jit(solution)/shard_map/ppermute | solution.py:26
  603.8 64.7 %collective-permute-done.49 = bf16[1536,992]{0,1:T(8,128)(2,1)S(1)} collective-permute-done((bf16[1536,992]{0,1:T(8,128)(2,1)S(1)}, bf16[1536,992]{0,1:T(8,128)(2,1)S(1)}, u32[]{:S(2)}, u32[]{:S(2)}) %collective-permute-start.49) | collective-permute-done | bytes 3047456 | tf_op jit(solution)/shard_map/ppermute | solution.py:26
  725.3 14.3 collective-permute-done.71
  740.5 70.8 %collective-permute-done.63 = bf16[768,992]{0,1:T(8,128)(2,1)S(1)} collective-permute-done((bf16[768,992]{0,1:T(8,128)(2,1)S(1)}, bf16[768,992]{0,1:T(8,128)(2,1)S(1)}, u32[]{:S(2)}, u32[]{:S(2)}) %collective-permute-start.63) | collective-permute-done | bytes 1523744 | tf_op jit(solution)/shard_map/ppermute | solution.py:26
  861.5 39.4 %collective-permute-done.69 = bf16[768,992]{0,1:T(8,128)(2,1)S(1)} collective-permute-done((bf16[768,992]{0,1:T(8,128)(2,1)}, bf16[768,992]{0,1:T(8,128)(2,1)S(1)}, u32[]{:S(2)}, u32[]{:S(2)}) %collective-permute-start.69) | collective-permute-done | bytes 1523744 | tf_op jit(solution)/shard_map/ppermute | solution.py:26
  1008.7 31.7 %collective-permute-done.136 = bf16[768,992]{0,1:T(8,128)(2,1)} collective-permute-done((bf16[768,992]{0,1:T(8,128)(2,1)}, bf16[768,992]{0,1:T(8,128)(2,1)}, u32[]{:S(2)}, u32[]{:S(2)}) %collective-permute-start.136) | collective-permute-done | bytes 1523744 | tf_op jit(solution)/shard_map/ppermute | solution.py:26
  1043.6 29.5 %collective-permute-done.125 = bf16[768,992]{0,1:T(8,128)(2,1)} collective-permute-done((bf16[768,992]{0,1:T(8,128)(2,1)}, bf16[768,992]{0,1:T(8,128)(2,1)}, u32[]{:S(2)}, u32[]{:S(2)}) %collective-permute-start.125) | collective-permute-done | bytes 1523744 | tf_op jit(solution)/shard_map/ppermute | solution.py:26
  1108.8 39.4 %collective-permute-done.98 = bf16[768,768]{0,1:T(8,128)(2,1)S(1)} collective-permute-done((bf16[768,768]{0,1:T(8,128)(2,1)S(1)}, bf16[768,768]{0,1:T(8,128)(2,1)S(1)}, u32[]{:S(2)}, u32[]{:S(2)}) %collective-permute-start.98) | collective-permute-done | bytes 1179680 | tf_op jit(solution)/shard_map/ppermute | solution.py:26
  1150.1 13.9 collective-permute-done.138
  1199.8 12.8 collective-permute-done.140
  1231.2 13.5 collective-permute-done.129
  1266.8 14.6 collective-permute-done.107
  1414.6 11.9 collective-permute-done.134
  1447.8 17.9 collective-permute-done.120
  1476.2 54.7 %collective-permute-done.109 = bf16[1536,992]{0,1:T(8,128)(2,1)} collective-permute-done((bf16[1536,992]{0,1:T(8,128)(2,1)}, bf16[1536,992]{0,1:T(8,128)(2,1)}, u32[]{:S(2)}, u32[]{:S(2)}) %collective-permute-start.109) | collective-permute-done | bytes 3047456 | tf_op jit(solution)/shard_map/ppermute | solution.py:26
  1541.5 21.1 %collective-permute-done.116 = bf16[768,992]{0,1:T(8,128)(2,1)} collective-permute-done((bf16[768,992]{0,1:T(8,128)(2,1)}, bf16[768,992]{0,1:T(8,128)(2,1)}, u32[]{:S(2)}, u32[]{:S(2)}) %collective-permute-start.116) | collective-permute-done | bytes 1523744 | tf_op jit(solution)/shard_map/ppermute | solution.py:26
  1688.6 15.3 collective-permute-done.146
  1738.0 21.4 %collective-permute-done.112 = bf16[192,992]{1,0:T(8,128)(2,1)S(1)} collective-permute-done((bf16[192,992]{1,0:T(8,128)(2,1)S(1)}, bf16[192,992]{1,0:T(8,128)(2,1)S(1)}, u32[]{:S(2)}, u32[]{:S(2)}) %collective-permute-start.112) | collective-permute-done | bytes 380960 | tf_op jit(solution)/shard_map/ppermute | solution.py:26
  1790.2 16.8 collective-permute-done.95
  (1419 shorter events, 1043.0 us)
Async XLA Ops:
  185.1 123.7 %collective-permute-start.26 = (bf16[512,1536]{1,0:T(8,128)(2,1)}, bf16[512,1536]{1,0:T(8,128)(2,1)}, u32[]{:S(2)}, u32[]{:S(2)}) collective-permute-start(bf16[512,1536]{1,0:T(8,128)(2,1)} %multiply_convert_fusion.10), channel_id=1, source_target_pairs={{0,1},{1,0},{2,3},{3,2},{4,5},{5,4},{6,7},{7,6},{8,9},{9,8},{10,11... | collective-permute-start | bytes 4718600 | tf_op jit(solution)/shard_map/ppermute | solution.py:26
  188.0 112.8 %collective-permute-start.30 = (bf16[768,768]{0,1:T(8,128)(2,1)}, bf16[768,768]{0,1:T(8,128)(2,1)}, u32[]{:S(2)}, u32[]{:S(2)}) collective-permute-start(bf16[768,768]{0,1:T(8,128)(2,1)} %pad_maximum_fusion.19), channel_id=1, source_target_pairs={{0,4},{4,0},{1,5},{5,1},{2,6},{6,2},{3,7},{7,3},{8,12},{12,8},{9,1... | collective-permute-start | bytes 3538952 | tf_op jit(solution)/shard_map/ppermute | solution.py:26
  268.3 126.1 %collective-permute-start.58 = (bf16[192,992]{1,0:T(8,128)(2,1)S(1)}, bf16[192,992]{1,0:T(8,128)(2,1)}, u32[]{:S(2)}, u32[]{:S(2)}) collective-permute-start(bf16[192,992]{1,0:T(8,128)(2,1)S(1)} %get-tuple-element.249), channel_id=1, source_target_pairs={{0,24},{8,0},{16,8},{24,16},{1,25},{9,1},{17,9},{25,17},{2,26},{10... | collective-permute-start | bytes 1142792 | tf_op jit(solution)/shard_map/ppermute | solution.py:26
  279.4 117.7 %collective-permute-start.57 = (bf16[192,992]{1,0:T(8,128)(2,1)S(1)}, bf16[192,992]{1,0:T(8,128)(2,1)}, u32[]{:S(2)}, u32[]{:S(2)}) collective-permute-start(bf16[192,992]{1,0:T(8,128)(2,1)S(1)} %get-tuple-element.249), channel_id=1, source_target_pairs={{0,16},{8,24},{16,0},{24,8},{1,17},{9,25},{17,1},{25,9},{2,18},{10... | collective-permute-start | bytes 1142792 | tf_op jit(solution)/shard_map/ppermute | solution.py:26
  279.4 119.3 %collective-permute-start.56 = (bf16[192,992]{1,0:T(8,128)(2,1)S(1)}, bf16[192,992]{1,0:T(8,128)(2,1)}, u32[]{:S(2)}, u32[]{:S(2)}) collective-permute-start(bf16[192,992]{1,0:T(8,128)(2,1)S(1)} %get-tuple-element.249), channel_id=1, source_target_pairs={{0,8},{8,16},{16,24},{24,0},{1,9},{9,17},{17,25},{25,1},{2,10},{10... | collective-permute-start | bytes 1142792 | tf_op jit(solution)/shard_map/ppermute | solution.py:26
  300.8 99.4 %collective-permute-start.18 = (bf16[768,768]{0,1:T(8,128)(2,1)}, bf16[768,768]{0,1:T(8,128)(2,1)}, u32[]{:S(2)}, u32[]{:S(2)}) collective-permute-start(bf16[768,768]{0,1:T(8,128)(2,1)} %pad_maximum_fusion.17), channel_id=1, source_target_pairs={{0,2},{2,0},{1,3},{3,1},{4,6},{6,4},{5,7},{7,5},{8,10},{10,8},{9,1... | collective-permute-start | bytes 3538952 | tf_op jit(solution)/shard_map/ppermute | solution.py:26
  397.1 114.6 %collective-permute-start.47 = (bf16[768,992]{0,1:T(8,128)(2,1)}, bf16[768,992]{0,1:T(8,128)(2,1)}, u32[]{:S(2)}, u32[]{:S(2)}) collective-permute-start(bf16[768,992]{0,1:T(8,128)(2,1)} %copy.292), channel_id=1, source_target_pairs={{0,2},{2,0},{1,3},{3,1},{4,6},{6,4},{5,7},{7,5},{8,10},{10,8},{9,1... | collective-permute-start | bytes 4571144 | tf_op jit(solution)/shard_map/ppermute | solution.py:26
  400.2 103.8 %collective-permute-start.37 = (bf16[768,992]{0,1:T(8,128)(2,1)}, bf16[768,992]{0,1:T(8,128)(2,1)}, u32[]{:S(2)}, u32[]{:S(2)}) collective-permute-start(bf16[768,992]{0,1:T(8,128)(2,1)} %copy.287), channel_id=1, source_target_pairs={{0,4},{4,0},{1,5},{5,1},{2,6},{6,2},{3,7},{7,3},{8,12},{12,8},{9,1... | collective-permute-start | bytes 4571144 | tf_op jit(solution)/shard_map/ppermute | solution.py:26
  408.3 109.3 %collective-permute-start.32 = (bf16[512,1536]{1,0:T(8,128)(2,1)}, bf16[512,1536]{1,0:T(8,128)(2,1)}, u32[]{:S(2)}, u32[]{:S(2)}) collective-permute-start(bf16[512,1536]{1,0:T(8,128)(2,1)} %slice.1161), channel_id=1, source_target_pairs={{0,1},{1,0},{2,3},{3,2},{4,5},{5,4},{6,7},{7,6},{8,9},{9,8},{10,11... | collective-permute-start | bytes 4718600 | tf_op jit(solution)/shard_map/ppermute | solution.py:26
  476.5 206.3 %collective-permute-start.66 = (bf16[192,992]{0,1:T(8,128)(2,1)}, bf16[192,992]{0,1:T(8,128)(2,1)}, u32[]{:S(2)}, u32[]{:S(2)}) collective-permute-start(bf16[192,992]{0,1:T(8,128)(2,1)} %get-tuple-element.276), channel_id=1, source_target_pairs={{0,24},{8,0},{16,8},{24,16},{1,25},{9,1},{17,9},{25,17},{2,26},{10... | collective-permute-start | bytes 1142792 | tf_op jit(solution)/shard_map/ppermute | solution.py:26
  533.2 150.2 %collective-permute-start.65 = (bf16[192,992]{0,1:T(8,128)(2,1)}, bf16[192,992]{0,1:T(8,128)(2,1)S(1)}, u32[]{:S(2)}, u32[]{:S(2)}) collective-permute-start(bf16[192,992]{0,1:T(8,128)(2,1)} %get-tuple-element.276), channel_id=1, source_target_pairs={{0,16},{8,24},{16,0},{24,8},{1,17},{9,25},{17,1},{25,9},{2,18},{10... | collective-permute-start | bytes 1142792 | tf_op jit(solution)/shard_map/ppermute | solution.py:26
  562.6 146.9 %collective-permute-start.52 = (bf16[768,768]{0,1:T(8,128)(2,1)}, bf16[768,768]{0,1:T(8,128)(2,1)}, u32[]{:S(2)}, u32[]{:S(2)}) collective-permute-start(bf16[768,768]{0,1:T(8,128)(2,1)} %pad_maximum_fusion.18), channel_id=1, source_target_pairs={{0,2},{2,0},{1,3},{3,1},{4,6},{6,4},{5,7},{7,5},{8,10},{10,8},{9,1... | collective-permute-start | bytes 3538952 | tf_op jit(solution)/shard_map/ppermute | solution.py:26
  564.3 104.2 %collective-permute-start.49 = (bf16[1536,992]{0,1:T(8,128)(2,1)S(1)}, bf16[1536,992]{0,1:T(8,128)(2,1)S(1)}, u32[]{:S(2)}, u32[]{:S(2)}) collective-permute-start(bf16[1536,992]{0,1:T(8,128)(2,1)S(1)} %copy-done.110), channel_id=1, source_target_pairs={{0,2},{2,0},{1,3},{3,1},{4,6},{6,4},{5,7},{7,5},{8,10},{10,8},{9,1... | collective-permute-start | bytes 9142280 | tf_op jit(solution)/shard_map/ppermute | solution.py:26
  580.8 121.8 %collective-permute-start.25 = (bf16[768,768]{0,1:T(8,128)(2,1)}, bf16[768,768]{0,1:T(8,128)(2,1)S(1)}, u32[]{:S(2)}, u32[]{:S(2)}) collective-permute-start(bf16[768,768]{0,1:T(8,128)(2,1)} %pad_maximum_fusion.18), channel_id=1, source_target_pairs={{0,4},{4,0},{1,5},{5,1},{2,6},{6,2},{3,7},{7,3},{8,12},{12,8},{9,1... | collective-permute-start | bytes 3538952 | tf_op jit(solution)/shard_map/ppermute | solution.py:26
  709.5 111.7 %collective-permute-start.67 = (bf16[768,992]{0,1:T(8,128)(2,1)}, bf16[768,992]{0,1:T(8,128)(2,1)}, u32[]{:S(2)}, u32[]{:S(2)}) collective-permute-start(bf16[768,992]{0,1:T(8,128)(2,1)} %pad_maximum_fusion.13), channel_id=1, source_target_pairs={{0,4},{4,0},{1,5},{5,1},{2,6},{6,2},{3,7},{7,3},{8,12},{12,8},{9,1... | collective-permute-start | bytes 4571144 | tf_op jit(solution)/shard_map/ppermute | solution.py:26
  712.8 116.3 %collective-permute-start.59 = (bf16[768,992]{0,1:T(8,128)(2,1)}, bf16[768,992]{0,1:T(8,128)(2,1)}, u32[]{:S(2)}, u32[]{:S(2)}) collective-permute-start(bf16[768,992]{0,1:T(8,128)(2,1)} %copy.299), channel_id=1, source_target_pairs={{0,4},{4,0},{1,5},{5,1},{2,6},{6,2},{3,7},{7,3},{8,12},{12,8},{9,1... | collective-permute-start | bytes 4571144 | tf_op jit(solution)/shard_map/ppermute | solution.py:26
  716.7 94.6 %collective-permute-start.63 = (bf16[768,992]{0,1:T(8,128)(2,1)S(1)}, bf16[768,992]{0,1:T(8,128)(2,1)S(1)}, u32[]{:S(2)}, u32[]{:S(2)}) collective-permute-start(bf16[768,992]{0,1:T(8,128)(2,1)S(1)} %copy-done.178), channel_id=1, source_target_pairs={{0,4},{4,0},{1,5},{5,1},{2,6},{6,2},{3,7},{7,3},{8,12},{12,8},{9,1... | collective-permute-start | bytes 4571144 | tf_op jit(solution)/shard_map/ppermute | solution.py:26
  718.8 118.0 %collective-permute-start.53 = (bf16[768,768]{0,1:T(8,128)(2,1)}, bf16[768,768]{0,1:T(8,128)(2,1)}, u32[]{:S(2)}, u32[]{:S(2)}) collective-permute-start(bf16[768,768]{0,1:T(8,128)(2,1)} %collective-permute-done.52), channel_id=1, source_target_pairs={{0,4},{4,0},{1,5},{5,1},{2,6},{6,2},{3,7},{7,3},{8,12},{12,8},{9,1... | collective-permute-start | bytes 3538952 | tf_op jit(solution)/shard_map/ppermute | solution.py:26
  739.5 103.7 %collective-permute-start.51 = (bf16[512,1536]{1,0:T(8,128)(2,1)}, bf16[512,1536]{1,0:T(8,128)(2,1)}, u32[]{:S(2)}, u32[]{:S(2)}) collective-permute-start(bf16[512,1536]{1,0:T(8,128)(2,1)} %multiply_convert_fusion.8), channel_id=1, source_target_pairs={{0,1},{1,0},{2,3},{3,2},{4,5},{5,4},{6,7},{7,6},{8,9},{9,8},{10,11... | collective-permute-start | bytes 4718600 | tf_op jit(solution)/shard_map/ppermute | solution.py:26
  942.9 133.3 %collective-permute-start.137 = (bf16[768,992]{0,1:T(8,128)(2,1)}, bf16[768,992]{0,1:T(8,128)(2,1)}, u32[]{:S(2)}, u32[]{:S(2)}) collective-permute-start(bf16[768,992]{0,1:T(8,128)(2,1)} %slice.900), channel_id=1, source_target_pairs={{0,4},{4,0},{1,5},{5,1},{2,6},{6,2},{3,7},{7,3},{8,12},{12,8},{9,1... | collective-permute-start | bytes 4571144 | tf_op jit(solution)/shard_map/ppermute | solution.py:26
  959.6 113.5 %collective-permute-start.125 = (bf16[768,992]{0,1:T(8,128)(2,1)}, bf16[768,992]{0,1:T(8,128)(2,1)}, u32[]{:S(2)}, u32[]{:S(2)}) collective-permute-start(bf16[768,992]{0,1:T(8,128)(2,1)} %copy.335), channel_id=1, source_target_pairs={{0,4},{4,0},{1,5},{5,1},{2,6},{6,2},{3,7},{7,3},{8,12},{12,8},{9,1... | collective-permute-start | bytes 4571144 | tf_op jit(solution)/shard_map/ppermute | solution.py:26
  1002.1 175.7 %collective-permute-start.131 = (bf16[1536,992]{0,1:T(8,128)(2,1)}, bf16[1536,992]{0,1:T(8,128)(2,1)}, u32[]{:S(2)}, u32[]{:S(2)}) collective-permute-start(bf16[1536,992]{0,1:T(8,128)(2,1)} %convolution_convert_fusion.7), channel_id=1, source_target_pairs={{0,2},{2,0},{1,3},{3,1},{4,6},{6,4},{5,7},{7,5},{8,10},{10,8},{9,1... | collective-permute-start | bytes 9142280 | tf_op jit(solution)/shard_map/ppermute | solution.py:26
  1073.1 115.7 %collective-permute-start.103 = (bf16[768,768]{0,1:T(8,128)(2,1)}, bf16[768,768]{0,1:T(8,128)(2,1)}, u32[]{:S(2)}, u32[]{:S(2)}) collective-permute-start(bf16[768,768]{0,1:T(8,128)(2,1)} %slice.856), channel_id=1, source_target_pairs={{0,4},{4,0},{1,5},{5,1},{2,6},{6,2},{3,7},{7,3},{8,12},{12,8},{9,1... | collective-permute-start | bytes 3538952 | tf_op jit(solution)/shard_map/ppermute | solution.py:26
  1148.2 140.6 %collective-permute-start.97 = (bf16[768,768]{0,1:T(8,128)(2,1)}, bf16[768,768]{0,1:T(8,128)(2,1)}, u32[]{:S(2)}, u32[]{:S(2)}) collective-permute-start(bf16[768,768]{0,1:T(8,128)(2,1)} %pad_maximum_fusion.15), channel_id=1, source_target_pairs={{0,4},{4,0},{1,5},{5,1},{2,6},{6,2},{3,7},{7,3},{8,12},{12,8},{9,1... | collective-permute-start | bytes 3538952 | tf_op jit(solution)/shard_map/ppermute | solution.py:26
  1196.8 92.1 %collective-permute-start.99 = (bf16[768,768]{0,1:T(8,128)(2,1)}, bf16[768,768]{0,1:T(8,128)(2,1)}, u32[]{:S(2)}, u32[]{:S(2)}) collective-permute-start(bf16[768,768]{0,1:T(8,128)(2,1)} %add_convert_fusion.20), channel_id=1, source_target_pairs={{0,2},{2,0},{1,3},{3,1},{4,6},{6,4},{5,7},{7,5},{8,10},{10,8},{9,1... | collective-permute-start | bytes 3538952 | tf_op jit(solution)/shard_map/ppermute | solution.py:26
  1265.3 110.3 %collective-permute-start.132 = (bf16[768,992]{0,1:T(8,128)(2,1)}, bf16[768,992]{0,1:T(8,128)(2,1)}, u32[]{:S(2)}, u32[]{:S(2)}) collective-permute-start(bf16[768,992]{0,1:T(8,128)(2,1)} %copy.340), channel_id=1, source_target_pairs={{0,4},{4,0},{1,5},{5,1},{2,6},{6,2},{3,7},{7,3},{8,12},{12,8},{9,1... | collective-permute-start | bytes 4571144 | tf_op jit(solution)/shard_map/ppermute | solution.py:26
  1310.0 120.4 %collective-permute-start.115 = (bf16[768,992]{0,1:T(8,128)(2,1)}, bf16[768,992]{0,1:T(8,128)(2,1)}, u32[]{:S(2)}, u32[]{:S(2)}) collective-permute-start(bf16[768,992]{0,1:T(8,128)(2,1)} %slice.872), channel_id=1, source_target_pairs={{0,4},{4,0},{1,5},{5,1},{2,6},{6,2},{3,7},{7,3},{8,12},{12,8},{9,1... | collective-permute-start | bytes 4571144 | tf_op jit(solution)/shard_map/ppermute | solution.py:26
  1426.5 104.5 %collective-permute-start.109 = (bf16[1536,992]{0,1:T(8,128)(2,1)}, bf16[1536,992]{0,1:T(8,128)(2,1)}, u32[]{:S(2)}, u32[]{:S(2)}) collective-permute-start(bf16[1536,992]{0,1:T(8,128)(2,1)} %convolution_convert_fusion.11), channel_id=1, source_target_pairs={{0,2},{2,0},{1,3},{3,1},{4,6},{6,4},{5,7},{7,5},{8,10},{10,8},{9,1... | collective-permute-start | bytes 9142280 | tf_op jit(solution)/shard_map/ppermute | solution.py:26
  1433.4 129.3 %collective-permute-start.116 = (bf16[768,992]{0,1:T(8,128)(2,1)}, bf16[768,992]{0,1:T(8,128)(2,1)}, u32[]{:S(2)}, u32[]{:S(2)}) collective-permute-start(bf16[768,992]{0,1:T(8,128)(2,1)} %add_convert_fusion.15), channel_id=1, source_target_pairs={{0,2},{2,0},{1,3},{3,1},{4,6},{6,4},{5,7},{7,5},{8,10},{10,8},{9,1... | collective-permute-start | bytes 4571144 | tf_op jit(solution)/shard_map/ppermute | solution.py:26
  1447.8 123.7 %collective-permute-start.80 = (bf16[512,1536]{1,0:T(8,128)(2,1)}, bf16[512,1536]{1,0:T(8,128)(2,1)}, u32[]{:S(2)}, u32[]{:S(2)}) collective-permute-start(bf16[512,1536]{1,0:T(8,128)(2,1)} %get-tuple-element.192), channel_id=1, source_target_pairs={{0,1},{1,0},{2,3},{3,2},{4,5},{5,4},{6,7},{7,6},{8,9},{9,8},{10,11... | collective-permute-start | bytes 4718600 | tf_op jit(solution)/shard_map/ppermute | solution.py:26
  1475.7 178.0 %collective-permute-start.121 = (bf16[768,992]{0,1:T(8,128)(2,1)}, bf16[768,992]{0,1:T(8,128)(2,1)}, u32[]{:S(2)}, u32[]{:S(2)}) collective-permute-start(bf16[768,992]{0,1:T(8,128)(2,1)} %copy.332), channel_id=1, source_target_pairs={{0,4},{4,0},{1,5},{5,1},{2,6},{6,2},{3,7},{7,3},{8,12},{12,8},{9,1... | collective-permute-start | bytes 4571144 | tf_op jit(solution)/shard_map/ppermute | solution.py:26
  1541.0 123.0 %collective-permute-start.110 = (bf16[768,992]{0,1:T(8,128)(2,1)}, bf16[768,992]{0,1:T(8,128)(2,1)}, u32[]{:S(2)}, u32[]{:S(2)}) collective-permute-start(bf16[768,992]{0,1:T(8,128)(2,1)} %copy.324), channel_id=1, source_target_pairs={{0,4},{4,0},{1,5},{5,1},{2,6},{6,2},{3,7},{7,3},{8,12},{12,8},{9,1... | collective-permute-start | bytes 4571144 | tf_op jit(solution)/shard_map/ppermute | solution.py:26
  (482 other events, 10100.0 us)

commit v2 on v1

--- a/solution.py
+++ b/solution.py
@@ -2,6 +2,7 @@
 import jax.numpy as jnp
 import numpy as np
 from jax import lax
+from jax.experimental.layout import Layout, with_layout_constraint
 from jax.sharding import Mesh
 from jax.sharding import PartitionSpec as P
 
@@ -31,43 +32,64 @@
     return lax.ppermute(part, axis, [(i, i ^ bit) for i in range(size)])
 
 
-def gather_rows(part, axis):
-    pieces = [part] + [spin(part, axis, k) for k in range(1, lax.axis_size(axis))]
-    return jnp.concatenate(pieces, axis=0)
-
-
-def scatter_rows(part, axis):
-    size = lax.axis_size(axis)
-    rows = part.shape[0] // size
-    total = part[:rows].astype(jnp.float32)
-    for k in range(1, size):
-        total = total + spin(part[k * rows : (k + 1) * rows], axis, -k).astype(jnp.float32)
-    return total
-
-
-def gather_unit(part, axes, inner_first):
-    for axis in axes[:-1]:
-        part = gather_rows(part, axis)
-    if inner_first:
-        part = gather_rows(part, axes[-1])
-        return [part, spin(part, "y", 1)]
-    other = spin(part, "y", 1)
-    return [gather_rows(part, axes[-1]), gather_rows(other, axes[-1])]
-
-
-def meet(own, sent):
-    return own.astype(jnp.float32) + spin(sent, "y", 1).astype(jnp.float32)
-
-
-def scatter_unit(parts, axes, inner_first):
-    if inner_first:
-        part = scatter_rows(meet(parts[0], parts[1]).astype(half), axes[-1])
+def plain(part):
+    return with_layout_constraint(part, Layout(major_to_minor=tuple(range(part.ndim))))
+
+
+def gather_unit(part):
+    whole = lax.all_gather(plain(part), ("y", "dp"), axis=0, tiled=True)
+    rows = whole.shape[0] // 2
+    return [whole[:rows], whole[rows:]]
+
+
+def scatter_unit(parts):
+    whole = plain(jnp.concatenate(parts, axis=0))
+    part = lax.psum_scatter(whole, ("y", "dp"), scatter_dimension=0, tiled=True)
+    return part.astype(jnp.float32)
+
+
+def join_step(part, place, axis, bit):
+    other = flip(part, axis, bit)
+    mine = (lax.axis_index(axis) // bit) % 2 == 0
+    return jnp.stack([jnp.where(mine, part, other), jnp.where(mine, other, part)], axis=place)
+
+
+def gather_pairs(part, row_first):
+    bits = (lax.axis_size("dp") - 1).bit_length()
+    part = plain(part)
+    for bit in range(bits - 1, 0, -1):
+        part = join_step(part, bits - 1 - bit, "dp", 1 << bit)
+    if row_first:
+        part = join_step(part, 0, "y", 1)
+        part = join_step(part, bits, "dp", 1)
     else:
-        own, sent = [scatter_rows(p, axes[-1]).astype(half) for p in parts]
-        part = meet(own, sent)
-    for axis in axes[:-1][::-1]:
-        part = scatter_rows(part.astype(half), axis)
-    return part
+        part = join_step(part, bits - 1, "dp", 1)
+        part = join_step(part, 0, "y", 1)
+    part = part.reshape(2, -1, part.shape[-1])
+    return [part[0], part[1]]
+
+
+def split_step(whole, place, axis, bit):
+    mine = (lax.axis_index(axis) // bit) % 2
+    own = lax.dynamic_index_in_dim(whole, mine, place, False)
+    sent = lax.dynamic_index_in_dim(whole, 1 - mine, place, False)
+    return own.astype(jnp.float32) + flip(sent, axis, bit).astype(jnp.float32)
+
+
+def scatter_pairs(parts, row_first):
+    bits = (lax.axis_size("dp") - 1).bit_length()
+    whole = jnp.stack([plain(p) for p in parts])
+    columns = whole.shape[2]
+    whole = whole.reshape((2,) + (2,) * bits + (-1, columns))
+    if row_first:
+        whole = split_step(whole, 0, "y", 1).astype(half)
+        whole = split_step(whole, bits - 1, "dp", 1)
+    else:
+        whole = split_step(whole, bits, "dp", 1).astype(half)
+        whole = split_step(whole, 0, "y", 1)
+    for bit in range(1, bits):
+        whole = split_step(whole.astype(half), bits - 1 - bit, "dp", 1 << bit)
+    return whole
 
 
 def total_over(value, axes):
@@ -77,13 +99,6 @@
             value = value + flip(value, axis, bit)
             bit *= 2
     return value
-
-
-def in_order(own, other, axis):
-    first = lax.axis_index(axis) == 0
-    return jnp.where(
-        first, jnp.concatenate([own, other], axis=1), jnp.concatenate([other, own], axis=1)
-    )
 
 
 def collect(own):
@@ -278,64 +293,61 @@
     return jnp.concatenate([core * rows + near, (1 - core) * rows + near])
 
 
-def on_device(axes, *args):
+def on_device(*args):
     source_ids, target_ids, source_lengths, target_lengths = args[:4]
     masters, firsts, seconds = args[4:11], args[11:18], args[18:25]
     embedding, unembedding, attention_in, attention_out, feed_in, feed_out, norm_gains = masters
     row = lax.axis_index("y")
     core = lax.axis_index("c")
-    everywhere = axes + ("y", "c")
+    everywhere = ("dp", "y", "c")
+    size = lax.axis_size("dp")
 
     vocab_rows = embedding.shape[0]
     table_pair = jnp.concatenate([embedding.T.astype(half), unembedding.astype(half)], axis=1)
-    table_pairs = gather_unit(table_pair, axes, True)
-    table_pairs = table_pairs + [spin(p, "c", 1) for p in table_pairs]
-    table_t = jnp.concatenate([p[:, :vocab_rows] for p in table_pairs], axis=1)
-    w_head = jnp.concatenate([p[:, vocab_rows:] for p in table_pairs], axis=1)
-    near = jnp.arange(vocab_rows, dtype=jnp.int32)
-    vocab_ids = jnp.concatenate(
-        [
-            ((row ^ y_step) * 2 + (core ^ c_step)) * vocab_rows + near
-            for c_step in (0, 1)
-            for y_step in (0, 1)
-        ]
-    )
+    vocab_ids = jnp.arange(4 * vocab_rows, dtype=jnp.int32)
 
     own_count = jnp.sum(target_lengths).astype(jnp.float32)
     gain_part = jnp.concatenate(
         [norm_gains, jnp.full((1, norm_gains.shape[1]), own_count, jnp.float32)]
     )
-    gain_part = in_order(gain_part, spin(gain_part, "c", 1), "c")
-    gain_part = in_order(gain_part, spin(gain_part, "y", 1), "y")
-    feature_rows = gain_part.shape[1]
-    gain_part = gain_part.T
-    for axis in axes:
-        gain_part = gather_rows(gain_part, axis)
-    gains = gain_part.T
-    count = jnp.sum(gain_part[::feature_rows, -1])
-    gains = gains[:-1]
+    gain_part = lax.all_gather(gain_part, everywhere)
+    count = jnp.sum(gain_part[::4, -1, 0])
+    gains = gain_part[:, :-1].swapaxes(0, 1).reshape(norm_gains.shape[0], -1)
+
+    hidden_rows = feed_out.shape[1]
+    spare = ((0, 0), (0, -hidden_rows % 128))
 
     def attention_unit(layer):
         w_in = attention_in[layer].astype(half)
         w_in = w_in.reshape(w_in.shape[0], -1)
-        return jnp.concatenate([w_in, attention_out[layer].T.astype(half)], axis=1)
+        return [w_in, attention_out[layer].T.astype(half)]
 
     def feed_units(layer):
-        return (
-            feed_in[layer, :, 0].astype(half),
-            feed_in[layer, :, 1].astype(half),
-            feed_out[layer].T.astype(half),
-        )
-
-    attn_order = (True, False, False)
-    feed_order = ((True, False, True), (False, True, False))
-    attn = [None] * 3
-    feed = [None] * 2
-    attn[0] = gather_unit(attention_unit(0), axes, attn_order[0])
-    feed[0] = [gather_unit(u, axes, o) for u, o in zip(feed_units(0), feed_order[0])]
-    attn[1] = gather_unit(attention_unit(1), axes, attn_order[1])
-    attn[2] = gather_unit(attention_unit(2), axes, attn_order[2])
-    feed[1] = [gather_unit(u, axes, o) for u, o in zip(feed_units(1), feed_order[1])]
+        return [
+            jnp.pad(feed_in[layer, :, 0].astype(half), spare),
+            jnp.pad(feed_in[layer, :, 1].astype(half), spare),
+            jnp.pad(feed_out[layer].T.astype(half), spare),
+        ]
+
+    def thirds(blocks, start):
+        third = hidden_rows + spare[1][1]
+        return [
+            [b[:, start + k * third : start + (k + 1) * third] for b in blocks] for k in range(3)
+        ]
+
+    first = gather_unit(jnp.concatenate(attention_unit(0) + feed_units(0) + [table_pair], axis=1))
+    second = gather_unit(jnp.concatenate(feed_units(1), axis=1))
+    span = 4 * attention_out.shape[1]
+    edge = first[0].shape[1] - 2 * vocab_rows
+    attn = (
+        [b[:, :span] for b in first],
+        gather_pairs(jnp.concatenate(attention_unit(1), axis=1), False),
+        gather_pairs(jnp.concatenate(attention_unit(2), axis=1), True),
+    )
+    feed = (thirds(first, span), thirds(second, 0))
+    table_pairs = join_step(jnp.stack([plain(b[:, edge:]) for b in first]), 1, "c", 1)
+    table_pairs = table_pairs.reshape(4, -1, 2, vocab_rows).transpose(2, 1, 0, 3)
+    table_t, w_head = table_pairs.reshape(2, -1, 4 * vocab_rows)
 
     source = lax.dynamic_index_in_dim(source_ids, row, 0, False)[0]
     target = lax.dynamic_index_in_dim(target_ids, row, 0, False)[0]
@@ -382,78 +394,74 @@
     d_logits = ((jnp.exp(logits - lse) - hits.astype(jnp.float32)) * weight).astype(half)
     g_head = product_left(tgt_norm_d, d_logits).astype(half)
 
-    attn_grads = [None] * 3
-    feed_grads = [None] * 2
     d_tgt, gain_six = norm_back(tgt_top, gains[6], product_right(d_logits, w_head))
-    *grads, d_in = expand_back(tgt_norm_c, *feed[1], keep_tgt_c, collect(d_tgt.astype(half)))
-    feed_grads[1] = [scatter_unit(g, axes, o) for g, o in zip(grads, feed_order[1])]
+    *feed_one, d_in = expand_back(tgt_norm_c, *feed[1], keep_tgt_c, collect(d_tgt.astype(half)))
+    *feed_one, down_one = feed_one
+    down_one = scatter_pairs(down_one, False)
+    feed_one = scatter_unit([jnp.concatenate([plain(p) for p in g], axis=1) for g in zip(*feed_one)])
     d_more, gain_five = norm_back(tgt_cross, gains[5], fold(d_in))
     d_tgt = d_tgt + d_more
-    grads, d_query, d_keys = cross_attention_back(
+    attn_two, d_query, d_keys = cross_attention_back(
         tgt_norm_b, encoded, attn[2], key_bias, keep_tgt_b, collect(d_tgt.astype(half))
     )
-    attn_grads[2] = scatter_unit(grads, axes, attn_order[2])
+    attn_two = scatter_pairs(attn_two, True)
     d_encoded = fold(d_keys)
     d_more, gain_four = norm_back(tgt_self, gains[4], fold(d_query))
     d_tgt = d_tgt + d_more
-    grads, d_in = self_attention_back(
+    attn_one, d_in = self_attention_back(
         tgt_norm_a, attn[1], causal, keep_tgt_a, collect(d_tgt.astype(half))
     )
-    attn_grads[1] = scatter_unit(grads, axes, attn_order[1])
+    attn_one = scatter_pairs(attn_one, False)
     d_more, gain_three = norm_back(tgt_embed, gains[3], fold(d_in))
     d_tgt = d_tgt + d_more
 
     d_src, gain_two = norm_back(src_top, gains[2], d_encoded)
-    *grads, d_in = expand_back(src_norm_b, *feed[0], keep_src_b, collect(d_src.astype(half)))
-    feed_grads[0] = [scatter_unit(g, axes, o) for g, o in zip(grads, feed_order[0])]
+    *feed_zero, d_in = expand_back(src_norm_b, *feed[0], keep_src_b, collect(d_src.astype(half)))
+    *feed_zero, down_zero = feed_zero
+    down_zero = scatter_pairs(down_zero, False)
+    feed_zero = scatter_unit(
+        [jnp.concatenate([plain(p) for p in g], axis=1) for g in zip(*feed_zero)]
+    )
     d_more, gain_one = norm_back(src_mid, gains[1], fold(d_in))
     d_src = d_src + d_more
-    grads, d_in = self_attention_back(
+    attn_zero, d_in = self_attention_back(
         src_norm_a, attn[0], key_bias, keep_src_a, collect(d_src.astype(half))
     )
-    attn_grads[0] = scatter_unit(grads, axes, attn_order[0])
+    attn_zero = scatter_pairs(attn_zero, True)
     d_more, gain_zero = norm_back(src_embed, gains[0], fold(d_in))
     d_src = d_src + d_more
 
     g_table = product_left(d_src.astype(half), source_hot)
     g_table = (g_table + product_left(d_tgt.astype(half), target_hot)).astype(half)
-    pairs = [
-        jnp.concatenate(
-            [
-                g_table[:, k * vocab_rows : (k + 1) * vocab_rows],
-                g_head[:, k * vocab_rows : (k + 1) * vocab_rows],
-            ],
-            axis=1,
-        )
-        for k in range(4)
-    ]
-    pairs = [
-        (a.astype(jnp.float32) + spin(b, "c", 1).astype(jnp.float32)).astype(half)
-        for a, b in zip(pairs[:2], pairs[2:])
-    ]
-    pair_grad = scatter_unit(pairs, axes, True)
+    pairs = jnp.stack([g_table, g_head], axis=1).reshape(-1, 2, 2, 2, vocab_rows)
+    pairs = pairs.transpose(2, 3, 0, 1, 4).reshape(2, 2, -1, 2 * vocab_rows)
+    pairs = split_step(pairs, 1, "c", 1).astype(half)
+    pair_grad = scatter_pairs([pairs[0], pairs[1]], False)
 
     g_gains = jnp.stack([gain_zero, gain_one, gain_two, gain_three, gain_four, gain_five, gain_six])
+    g_gains = g_gains.T.reshape((2,) * (size - 1).bit_length() + (2, 2, -1, g_gains.shape[0]))
+    for axis in ("c", "y"):
+        g_gains = split_step(g_gains, g_gains.ndim - 3, axis, 1)
+    for bit in range((size - 1).bit_length()):
+        g_gains = split_step(g_gains, g_gains.ndim - 3, "dp", 1 << bit)
     g_gains = g_gains.T
-    for axis in axes[::-1]:
-        g_gains = scatter_rows(g_gains, axis)
-    g_gains = total_over(g_gains, ("y", "c"))
-    own_gains = norm_gains.shape[1]
-    g_gains = lax.dynamic_slice_in_dim(g_gains, (row * 2 + core) * own_gains, own_gains).T
 
     width = attention_out.shape[1]
-    units = [pair_grad] + attn_grads + feed_grads[0] + feed_grads[1]
+    attn_grads = [attn_zero, attn_one, attn_two]
+    units = [pair_grad, *attn_grads, feed_zero, feed_one, down_zero, down_one]
     squares = sum(jnp.sum(g * g) for g in units) + jnp.sum(g_gains * g_gains)
+    feed_grads = [g.reshape(-1, 2, hidden_rows + spare[1][1]) for g in (feed_zero, feed_one)]
     squares, loss = total_over(jnp.stack([squares, own_loss]), everywhere)
     grads = (
         pair_grad[:, :vocab_rows].T,
         pair_grad[:, vocab_rows:],
         jnp.stack([g[:, : 3 * width].reshape(-1, 3, width) for g in attn_grads]),
         jnp.stack([g[:, 3 * width :].T for g in attn_grads]),
-        jnp.stack([jnp.stack([g[0], g[1]], axis=1) for g in feed_grads]),
-        jnp.stack([g[2].T for g in feed_grads]),
+        jnp.stack(feed_grads)[..., :hidden_rows],
+        jnp.stack([g.T[:hidden_rows] for g in (down_zero, down_one)]),
         g_gains,
     )
+    grads = tuple(plain(g) for g in grads)
     grad_norm = jnp.sqrt(squares)
     scale = jnp.minimum(1.0, clip_limit / grad_norm)
     results = [
@@ -464,17 +472,9 @@
 
 
 def solution(mesh):
-    data = mesh.shape["dp"]
-    sizes = [2]
-    data //= 2
-    while data > 1:
-        size = 4 if data % 4 == 0 else data
-        sizes.insert(0, size)
-        data //= size
-    axes = tuple(f"d{i}" for i in range(len(sizes)))
-    devices = np.asarray(mesh.devices).reshape(tuple(sizes) + (mesh.shape["mp"] // 2, 2))
-    inner = Mesh(devices, axes + ("y", "c"))
-    dp = axes
+    shape = (mesh.shape["dp"], mesh.shape["mp"] // 2, 2)
+    inner = Mesh(np.asarray(mesh.devices).reshape(shape), ("dp", "y", "c"))
+    dp = "dp"
     mp = ("y", "c")
     params = (
         P(mp, dp),
@@ -483,11 +483,11 @@
         P(None, mp, dp),
         P(None, dp, None, mp),
         P(None, mp, dp),
-        P(None, dp + mp),
+        P(None, (dp,) + mp),
     )
     ids = (P(None, dp, None), P(None, dp, None), P(None, dp), P(None, dp))
     return jax.shard_map(
-        lambda *args: on_device(axes, *args),
+        on_device,
         mesh=inner,
         in_specs=ids + params * 3,
         out_specs=(P(), P()) + params * 3,

time: 1890 us -> 1670 us (0.88)
  waiting for transfers between devices: 866 us -> 578 us
  starting transfers between devices: 235 us -> 51.3 us
  other arithmetic: 183 us -> 299 us
  blocking collectives: 0 us -> 50.8 us
  matrix products: 303 us -> 349 us
  local copies, waits for them, and re-layouts: 272 us -> 299 us
    ppermute x146 -> x22, waiting for transfers between devices: 835 us -> 0.69 us  [spin(): lax.ppermute(part, axis, [(i, (i + shift) % size) for i in range(size)])]
    ppermute x7 -> x44, waiting for transfers between devices: 31.5 us -> 350 us  [flip(): return lax.ppermute(part, axis, [(i, i ^ bit) for i in range(size)])]
    ppermute x146 -> x22, starting transfers between devices: 233 us -> 5 us  [spin(): lax.ppermute(part, axis, [(i, (i + shift) % size) for i in range(size)])]
    all_gather x0 -> x2, waiting for transfers between devices: none -> 228 us  [gather_unit(): whole = lax.all_gather(plain(part), ('y', 'dp'), axis=0, tiled=True)]
    another operation x0 -> x18, local copies, waits for them, and re-layouts: none -> 61.8 us  [the longest x10 43.6 us: scatter_pairs(): whole = jnp.stack([plain(p) for p in parts])]
    concatenate x20 -> x1, local copies, waits for them, and re-layouts: 63.2 us -> 3.39 us  [on_device(): jnp.concatenate(attention_unit(0) + feed_units(0) + [table_pair], axis=1)]
    all_gather x0 -> x1, blocking collectives: none -> 50.8 us  [on_device(): gain_part = lax.all_gather(gain_part, everywhere)]
    concatenate x19 -> x5, other arithmetic: 25 us -> 72 us  [the longest x2 70.6 us: scatter_unit(): whole = plain(jnp.concatenate(parts, axis=0))]
  transfers between devices with their start and end apart: 153 -> 70, of which waited for: 59 -> 26; matrix products, arithmetic and copies ran while one was open for 34% -> 49% of each run, Pallas kernels for 0% -> 0%
where the time goes in v2:
time: 1670 us; the launch traced here: 1660 us
  waiting for transfers between devices  578 us (35%)
  matrix products  349 us (21%)
  local copies, waits for them, and re-layouts  299 us (18%)
  other arithmetic  299 us (18%)
  starting transfers between devices  51.3 us (3%)
  blocking collectives  50.8 us (3%)
  between operations  27.9 us (2%)
    ppermute x44, waiting for transfers between devices, flip(): return lax.ppermute(part, axis, [(i, i ^ bit) for i in range(size)])  350 us
    all_gather x2, waiting for transfers between devices, gather_unit(): whole = lax.all_gather(plain(part), ('y', 'dp'), axis=0, tiled=True)  228 us
    dot_general x29, matrix products, product_left(): lax.dot_general(left, right, (((0,), (0,)), ((), ())), preferred_element_...  104 us
    dot_general x27, matrix products, product(): return jnp.dot(left, right, preferred_element_type=jnp.float32)  97.8 us
    dot_general x29, matrix products, product_right(): lax.dot_general(left, right, (((1,), (1,)), ((), ())), preferred_element_...  76.5 us
    unnamed x657, local copies, waits for them, and re-layouts  71.2 us
    concatenate x2, other arithmetic, scatter_unit(): whole = plain(jnp.concatenate(parts, axis=0))  70.6 us
    all_gather x1, blocking collectives, on_device(): gain_part = lax.all_gather(gain_part, everywhere)  50.8 us
  transfers between devices with their start and end apart: 70, of which 26 were waited for; matrix products, arithmetic and copies ran while one was open for 49% of the time, Pallas kernels for 0%

profile of v2, /device:TPU:0, one launch (start us, length us, event | category | flops | bytes accessed | tf_op | source)
XLA Modules:
  0.0 1655.3 jit_solution(818634918342122933)
XLA Ops:
  30.9 50.8 %all-gather = f32[256,48]{1,0:T(8,128)S(1)} all-gather(f32[8,48]{1,0:T(8,128)S(1)} %concatenate.124), channel_id=2, replica_groups=mesh['dp'=8,'y'=2,'c'=2] {'dp','y','c'}, dimensions={0}, use_global_device_ids=true | all-gather | bytes 50688 | tf_op jit(solution)/shard_map/all_gather | solution.py:313
  85.6 227.6 %all-gather.4.cloned.1.call-done = bf16[3072,4032]{1,0:T(8,128)(2,1)} async-done(((bf16[192,4032]{1,0:T(8,128)(2,1)}), bf16[3072,4032]{1,0:T(8,128)(2,1)}) %all-gather.4.cloned.1.call-update) | async-done | bytes 24772624 | tf_op jit(solution)/shard_map/all_gather | solution.py:40
  323.2 26.3 %collective-permute-done.3 = bf16[2,192,768]{2,1,0:T(8,128)(2,1)S(1)} collective-permute-done((bf16[2,192,768]{2,1,0:T(8,128)(2,1)S(1)}, bf16[2,192,768]{2,1,0:T(8,128)(2,1)S(1)}, u32[]{:S(2)}, u32[]{:S(2)}) %collective-permute-start.3) | collective-permute-done | bytes 589856 | tf_op jit(solution)/shard_map/ppermute | solution.py:32
  364.4 7.0 collective-permute-done.9
  399.4 16.0 fusion.175
  435.6 61.7 %collective-permute-done.5 = bf16[2,2,2,192,768]{4,3,0,1,2:T(8,128)(2,1)} collective-permute-done((bf16[2,2,2,192,768]{4,3,0,1,2:T(8,128)(2,1)}, bf16[2,2,2,192,768]{4,3,0,1,2:T(8,128)(2,1)}, u32[]{:S(2)}, u32[]{:S(2)}) %collective-permute-start.5) | collective-permute-done | bytes 2359328 | tf_op jit(solution)/shard_map/ppermute | solution.py:32
  511.6 6.8 fusion.102
  518.4 9.9 multiply_convert_fusion.5
  535.0 8.0 multiply_convert_fusion.4
  568.5 43.6 %collective-permute-done.11 = bf16[2,2,2,192,768]{4,3,1,2,0:T(8,128)(2,1)} collective-permute-done((bf16[2,2,2,192,768]{4,3,1,2,0:T(8,128)(2,1)}, bf16[2,2,2,192,768]{4,3,1,2,0:T(8,128)(2,1)}, u32[]{:S(2)}, u32[]{:S(2)}) %collective-permute-start.11) | collective-permute-done | bytes 2359328 | tf_op jit(solution)/shard_map/ppermute | solution.py:32
  727.5 54.3 %maximum_maximum_fusion.1 = bf16[3072,2048]{1,0:T(8,128)(2,1)} fusion(bf16[1536,1024]{1,0:T(8,128)(2,1)S(1)} %convolution_convert_fusion.2, bf16[1536,1024]{1,0:T(8,128)(2,1)S(1)} %convolution_convert_fusion.3, bf16[1536,1024]{1,0:T(8,128)(2,1)S(1)} %convolution_convert_fusion.4, bf16[1536,1024]{1,0:T(8,128)(2,1)S(1)} %convolution_convert_fusion.5), kind=kLoop, calls=%fused_computation.1 | loop fusion | flops 50331648 | bytes 25165824 | tf_op jit(solution)/shard_map/concatenate | solution.py:46
  955.6 10.1 multiply_convert_fusion.3
  965.8 6.9 fusion.96
  978.3 9.9 multiply_convert_fusion.2
  988.2 8.1 fusion.88
  996.3 7.9 add_add_fusion
  1005.7 7.2 convolution_convert_fusion.6
  1051.8 7.4 convolution_convert_fusion.11
  1079.8 16.3 maximum_maximum_fusion
  1121.0 34.8 %collective-permute-done.47 = bf16[192,768]{0,1:T(8,128)(2,1)S(1)} collective-permute-done((bf16[192,768]{0,1:T(8,128)(2,1)}, bf16[192,768]{0,1:T(8,128)(2,1)S(1)}, u32[]{:S(2)}, u32[]{:S(2)}) %collective-permute-start.47) | collective-permute-done | bytes 294944 | tf_op jit(solution)/shard_map/ppermute | solution.py:32
  1177.4 10.0 collective-permute-done.42
  1189.5 45.4 %collective-permute-done.55 = bf16[192,1024]{0,1:T(8,128)(2,1)} collective-permute-done((bf16[192,1024]{0,1:T(8,128)(2,1)}, bf16[192,1024]{0,1:T(8,128)(2,1)}, u32[]{:S(2)}, u32[]{:S(2)}) %collective-permute-start.55) | collective-permute-done | bytes 393248 | tf_op jit(solution)/shard_map/ppermute | solution.py:32
  1237.9 10.5 collective-permute-done.43
  1257.6 10.4 multiply_reduce_fusion
  1270.3 10.9 multiply_convert_fusion
  1294.4 9.5 multiply_convert_fusion.1
  1408.5 37.0 %collective-permute-done.57 = f32[2,2,2,48,7]{3,2,4,1,0:T(2,128)S(1)} collective-permute-done((f32[2,2,2,48,7]{3,2,4,1,0:T(2,128)S(1)}, f32[2,2,2,48,7]{3,2,4,1,0:T(2,128)S(1)}, u32[]{:S(2)}, u32[]{:S(2)}) %collective-permute-start.57) | collective-permute-done | bytes 10784 | tf_op jit(solution)/shard_map/ppermute | solution.py:32
  1482.1 28.9 %collective-permute-done.32 = bf16[2,2,2,192,192]{4,3,1,2,0:T(8,128)(2,1)} collective-permute-done((bf16[2,2,2,192,192]{4,3,1,2,0:T(8,128)(2,1)}, bf16[2,2,2,192,192]{4,3,1,2,0:T(8,128)(2,1)}, u32[]{:S(2)}, u32[]{:S(2)}) %collective-permute-start.32) | collective-permute-done | bytes 589856 | tf_op jit(solution)/shard_map/ppermute | solution.py:32
  1528.0 11.2 collective-permute-done.34
  1546.3 9.0 collective-permute-done.35
  1612.3 10.0 copy_subtract_fusion
  1630.6 14.7 multiply_subtract_fusion
  (1202 shorter events, 799.1 us)
Async XLA Ops:
  7.2 306.0 %all-gather.4.cloned.1.call-start = ((), (), s32[]{:S(2)}) async-start(), calls=%async_computation.2 | async-start | bytes 26738688 | tf_op jit(solution)/shard_map/all_gather | solution.py:40
  23.0 626.4 %all-gather.6.cloned.1.call-start = ((), (), s32[]{:S(2)}) async-start(), calls=%async_computation.3 | async-start | bytes 20054016 | tf_op jit(solution)/shard_map/all_gather | solution.py:40
  23.6 59.1 %collective-permute-start.2 = (bf16[192,768]{1,0:T(8,128)(2,1)S(1)}, bf16[192,768]{1,0:T(8,128)(2,1)S(1)}, u32[]{:S(2)}, u32[]{:S(2)}) collective-permute-start(bf16[192,768]{1,0:T(8,128)(2,1)S(1)} %pad_maximum_fusion.40), channel_id=1, source_target_pairs={{0,16},{4,20},{8,24},{12,28},{16,0},{20,4},{24,8},{28,12},{1,17},{... | collective-permute-start | bytes 884744 | tf_op jit(solution)/shard_map/ppermute | solution.py:32
  28.2 55.2 %collective-permute-start.8 = (bf16[192,768]{1,0:T(8,128)(2,1)S(1)}, bf16[192,768]{1,0:T(8,128)(2,1)S(1)}, u32[]{:S(2)}, u32[]{:S(2)}) collective-permute-start(bf16[192,768]{1,0:T(8,128)(2,1)S(1)} %pad_maximum_fusion.41), channel_id=1, source_target_pairs={{0,16},{4,20},{8,24},{12,28},{16,0},{20,4},{24,8},{28,12},{1,17},{... | collective-permute-start | bytes 884744 | tf_op jit(solution)/shard_map/ppermute | solution.py:32
  29.5 1537.7 %reduce-scatter.5.cloned.1.call-start = ((), (), s32[]{:S(2)}) async-start(), calls=%async_computation.5 | async-start | bytes 13369344 | tf_op jit(solution)/shard_map/reduce_scatter | solution.py:47
  321.3 50.1 %collective-permute-start.9 = (bf16[2,192,768]{2,1,0:T(8,128)(2,1)}, bf16[2,192,768]{2,1,0:T(8,128)(2,1)}, u32[]{:S(2)}, u32[]{:S(2)}) collective-permute-start(bf16[2,192,768]{2,1,0:T(8,128)(2,1)} %pad_maximum_fusion.31), channel_id=1, source_target_pairs={{0,8},{4,12},{8,0},{12,4},{16,24},{20,28},{24,16},{28,20},{1,9},{5... | collective-permute-start | bytes 1769480 | tf_op jit(solution)/shard_map/ppermute | solution.py:32
  373.9 180.1 %collective-permute-start.10 = (bf16[2,2,192,768]{3,2,0,1:T(8,128)(2,1)}, bf16[2,2,192,768]{3,2,0,1:T(8,128)(2,1)}, u32[]{:S(2)}, u32[]{:S(2)}) collective-permute-start(bf16[2,2,192,768]{3,2,0,1:T(8,128)(2,1)} %pad_maximum_fusion.19), channel_id=1, source_target_pairs={{0,2},{2,0},{1,3},{3,1},{4,6},{6,4},{5,7},{7,5},{8,10},{10,8},{9,1... | collective-permute-start | bytes 3538952 | tf_op jit(solution)/shard_map/ppermute | solution.py:32
  381.5 115.8 %collective-permute-start.5 = (bf16[2,2,2,192,768]{4,3,0,1,2:T(8,128)(2,1)}, bf16[2,2,2,192,768]{4,3,0,1,2:T(8,128)(2,1)}, u32[]{:S(2)}, u32[]{:S(2)}) collective-permute-start(bf16[2,2,2,192,768]{4,3,0,1,2:T(8,128)(2,1)} %pad_maximum_fusion.8), channel_id=1, source_target_pairs={{0,2},{2,0},{1,3},{3,1},{4,6},{6,4},{5,7},{7,5},{8,10},{10,8},{9,1... | collective-permute-start | bytes 7077896 | tf_op jit(solution)/shard_map/ppermute | solution.py:32
  434.8 66.3 %collective-permute-start.13 = (bf16[512,1536]{1,0:T(8,128)(2,1)S(1)}, bf16[512,1536]{1,0:T(8,128)(2,1)S(1)}, u32[]{:S(2)}, u32[]{:S(2)}) collective-permute-start(bf16[512,1536]{1,0:T(8,128)(2,1)S(1)} %slice.828), channel_id=1, source_target_pairs={{0,1},{1,0},{2,3},{3,2},{4,5},{5,4},{6,7},{7,6},{8,9},{9,8},{10,11... | collective-permute-start | bytes 4718600 | tf_op jit(solution)/shard_map/ppermute | solution.py:27
  435.1 64.6 %collective-permute-start.1 = (bf16[128,1536]{1,0:T(8,128)(2,1)S(1)}, bf16[128,1536]{1,0:T(8,128)(2,1)S(1)}, u32[]{:S(2)}, u32[]{:S(2)}) collective-permute-start(bf16[128,1536]{1,0:T(8,128)(2,1)S(1)} %multiply_convert_fusion.20), channel_id=1, source_target_pairs={{0,1},{1,0},{2,3},{3,2},{4,5},{5,4},{6,7},{7,6},{8,9},{9,8},{10,11... | collective-permute-start | bytes 1179656 | tf_op jit(solution)/shard_map/ppermute | solution.py:27
  558.1 54.1 %collective-permute-start.11 = (bf16[2,2,2,192,768]{4,3,1,2,0:T(8,128)(2,1)}, bf16[2,2,2,192,768]{4,3,1,2,0:T(8,128)(2,1)}, u32[]{:S(2)}, u32[]{:S(2)}) collective-permute-start(bf16[2,2,2,192,768]{4,3,1,2,0:T(8,128)(2,1)} %pad_maximum_fusion.9), channel_id=1, source_target_pairs={{0,4},{4,0},{8,12},{12,8},{16,20},{20,16},{24,28},{28,24},{1,5},{5... | collective-permute-start | bytes 7077896 | tf_op jit(solution)/shard_map/ppermute | solution.py:32
  567.7 48.3 %collective-permute-start.16 = (bf16[512,1536]{1,0:T(8,128)(2,1)S(1)}, bf16[512,1536]{1,0:T(8,128)(2,1)S(1)}, u32[]{:S(2)}, u32[]{:S(2)}) collective-permute-start(bf16[512,1536]{1,0:T(8,128)(2,1)S(1)} %multiply_convert_fusion.8), channel_id=1, source_target_pairs={{0,1},{1,0},{2,3},{3,2},{4,5},{5,4},{6,7},{7,6},{8,9},{9,8},{10,11... | collective-permute-start | bytes 4718600 | tf_op jit(solution)/shard_map/ppermute | solution.py:27
  712.5 214.3 %collective-permute-start.52 = (bf16[2,2,2,192,1024]{4,3,2,1,0:T(8,128)(2,1)}, bf16[2,2,2,192,1024]{4,3,2,1,0:T(8,128)(2,1)}, u32[]{:S(2)}, u32[]{:S(2)}) collective-permute-start(bf16[2,2,2,192,1024]{4,3,2,1,0:T(8,128)(2,1)} %bitcast.569), channel_id=1, source_target_pairs={{0,4},{4,0},{8,12},{12,8},{16,20},{20,16},{24,28},{28,24},{1,5},{5... | collective-permute-start | bytes 9437192 | tf_op jit(solution)/shard_map/ppermute | solution.py:32
  727.4 55.7 %collective-permute-start.22 = (bf16[128,1536]{1,0:T(8,128)(2,1)}, bf16[128,1536]{1,0:T(8,128)(2,1)}, u32[]{:S(2)}, u32[]{:S(2)}) collective-permute-start(bf16[128,1536]{1,0:T(8,128)(2,1)} %get-tuple-element.263), channel_id=1, source_target_pairs={{0,1},{1,0},{2,3},{3,2},{4,5},{5,4},{6,7},{7,6},{8,9},{9,8},{10,11... | collective-permute-start | bytes 1179656 | tf_op jit(solution)/shard_map/ppermute | solution.py:27
  781.8 791.6 %reduce-scatter.3.cloned.1.call-start = ((), (), s32[]{:S(2)}) async-start(), calls=%async_computation.4 | async-start | bytes 13369344 | tf_op jit(solution)/shard_map/reduce_scatter | solution.py:47
  803.9 111.9 %collective-permute-start.23 = (bf16[512,1536]{1,0:T(8,128)(2,1)}, bf16[512,1536]{1,0:T(8,128)(2,1)}, u32[]{:S(2)}, u32[]{:S(2)}) collective-permute-start(bf16[512,1536]{1,0:T(8,128)(2,1)} %slice.826), channel_id=1, source_target_pairs={{0,1},{1,0},{2,3},{3,2},{4,5},{5,4},{6,7},{7,6},{8,9},{9,8},{10,11... | collective-permute-start | bytes 4718600 | tf_op jit(solution)/shard_map/ppermute | solution.py:27
  854.6 87.8 %collective-permute-start.44 = (bf16[2,2,2,192,768]{4,3,2,1,0:T(8,128)(2,1)}, bf16[2,2,2,192,768]{4,3,2,1,0:T(8,128)(2,1)}, u32[]{:S(2)}, u32[]{:S(2)}) collective-permute-start(bf16[2,2,2,192,768]{4,3,2,1,0:T(8,128)(2,1)} %bitcast.580), channel_id=1, source_target_pairs={{0,2},{2,0},{1,3},{3,1},{4,6},{6,4},{5,7},{7,5},{8,10},{10,8},{9,1... | collective-permute-start | bytes 7077896 | tf_op jit(solution)/shard_map/ppermute | solution.py:32
  911.4 129.3 %collective-permute-start.40 = (bf16[2,2,2,192,768]{4,3,2,1,0:T(8,128)(2,1)}, bf16[2,2,2,192,768]{4,3,2,1,0:T(8,128)(2,1)}, u32[]{:S(2)}, u32[]{:S(2)}) collective-permute-start(bf16[2,2,2,192,768]{4,3,2,1,0:T(8,128)(2,1)} %bitcast.582), channel_id=1, source_target_pairs={{0,4},{4,0},{8,12},{12,8},{16,20},{20,16},{24,28},{28,24},{1,5},{5... | collective-permute-start | bytes 7077896 | tf_op jit(solution)/shard_map/ppermute | solution.py:32
  941.2 155.0 %collective-permute-start.53 = (bf16[2,2,192,1024]{3,2,1,0:T(8,128)(2,1)}, bf16[2,2,192,1024]{3,2,1,0:T(8,128)(2,1)}, u32[]{:S(2)}, u32[]{:S(2)}) collective-permute-start(bf16[2,2,192,1024]{3,2,1,0:T(8,128)(2,1)} %bitcast.595), channel_id=1, source_target_pairs={{0,2},{2,0},{1,3},{3,1},{4,6},{6,4},{5,7},{7,5},{8,10},{10,8},{9,1... | collective-permute-start | bytes 4718600 | tf_op jit(solution)/shard_map/ppermute | solution.py:32
  954.9 119.0 %collective-permute-start.45 = (bf16[2,2,192,768]{3,2,1,0:T(8,128)(2,1)}, bf16[2,2,192,768]{3,2,1,0:T(8,128)(2,1)}, u32[]{:S(2)}, u32[]{:S(2)}) collective-permute-start(bf16[2,2,192,768]{3,2,1,0:T(8,128)(2,1)} %bitcast.180), channel_id=1, source_target_pairs={{0,4},{4,0},{8,12},{12,8},{16,20},{20,16},{24,28},{28,24},{1,5},{5... | collective-permute-start | bytes 3538952 | tf_op jit(solution)/shard_map/ppermute | solution.py:32
  1005.7 157.1 %collective-permute-start.25 = (bf16[512,1536]{1,0:T(8,128)(2,1)}, bf16[512,1536]{1,0:T(8,128)(2,1)}, u32[]{:S(2)}, u32[]{:S(2)}) collective-permute-start(bf16[512,1536]{1,0:T(8,128)(2,1)} %slice.825), channel_id=1, source_target_pairs={{0,1},{1,0},{2,3},{3,2},{4,5},{5,4},{6,7},{7,6},{8,9},{9,8},{10,11... | collective-permute-start | bytes 4718600 | tf_op jit(solution)/shard_map/ppermute | solution.py:27
  1039.0 288.4 %collective-permute-start.48 = (bf16[2,2,2,192,1024]{4,3,2,1,0:T(8,128)(2,1)}, bf16[2,2,2,192,1024]{4,3,2,1,0:T(8,128)(2,1)}, u32[]{:S(2)}, u32[]{:S(2)}) collective-permute-start(bf16[2,2,2,192,1024]{4,3,2,1,0:T(8,128)(2,1)} %bitcast.570), channel_id=1, source_target_pairs={{0,4},{4,0},{8,12},{12,8},{16,20},{20,16},{24,28},{28,24},{1,5},{5... | collective-permute-start | bytes 9437192 | tf_op jit(solution)/shard_map/ppermute | solution.py:32
  1051.8 58.7 %collective-permute-start.41 = (bf16[2,2,192,768]{3,2,1,0:T(8,128)(2,1)}, bf16[2,2,192,768]{3,2,1,0:T(8,128)(2,1)}, u32[]{:S(2)}, u32[]{:S(2)}) collective-permute-start(bf16[2,2,192,768]{3,2,1,0:T(8,128)(2,1)} %bitcast.610), channel_id=1, source_target_pairs={{0,2},{2,0},{1,3},{3,1},{4,6},{6,4},{5,7},{7,5},{8,10},{10,8},{9,1... | collective-permute-start | bytes 3538952 | tf_op jit(solution)/shard_map/ppermute | solution.py:32
  1103.9 56.6 %collective-permute-start.54 = (bf16[2,192,1024]{2,1,0:T(8,128)(2,1)}, bf16[2,192,1024]{2,1,0:T(8,128)(2,1)}, u32[]{:S(2)}, u32[]{:S(2)}) collective-permute-start(bf16[2,192,1024]{2,1,0:T(8,128)(2,1)} %bitcast.202), channel_id=1, source_target_pairs={{0,8},{4,12},{8,0},{12,4},{16,24},{20,28},{24,16},{28,20},{1,9},{5... | collective-permute-start | bytes 2359304 | tf_op jit(solution)/shard_map/ppermute | solution.py:32
  1119.5 67.8 %collective-permute-start.42 = (bf16[2,192,768]{2,1,0:T(8,128)(2,1)}, bf16[2,192,768]{2,1,0:T(8,128)(2,1)}, u32[]{:S(2)}, u32[]{:S(2)}) collective-permute-start(bf16[2,192,768]{2,1,0:T(8,128)(2,1)} %bitcast.620), channel_id=1, source_target_pairs={{0,8},{4,12},{8,0},{12,4},{16,24},{20,28},{24,16},{28,20},{1,9},{5... | collective-permute-start | bytes 1769480 | tf_op jit(solution)/shard_map/ppermute | solution.py:32
  1173.2 76.8 %collective-permute-start.26 = (bf16[512,1536]{1,0:T(8,128)(2,1)}, bf16[512,1536]{1,0:T(8,128)(2,1)}, u32[]{:S(2)}, u32[]{:S(2)}) collective-permute-start(bf16[512,1536]{1,0:T(8,128)(2,1)} %get-tuple-element.259), channel_id=1, source_target_pairs={{0,1},{1,0},{2,3},{3,2},{4,5},{5,4},{6,7},{7,6},{8,9},{9,8},{10,11... | collective-permute-start | bytes 4718600 | tf_op jit(solution)/shard_map/ppermute | solution.py:27
  1174.4 60.5 %collective-permute-start.55 = (bf16[192,1024]{0,1:T(8,128)(2,1)}, bf16[192,1024]{0,1:T(8,128)(2,1)}, u32[]{:S(2)}, u32[]{:S(2)}) collective-permute-start(bf16[192,1024]{0,1:T(8,128)(2,1)} %dynamic-slice_bitcast_fusion.1), channel_id=1, source_target_pairs={{0,16},{4,20},{8,24},{12,28},{16,0},{20,4},{24,8},{28,12},{1,17},{... | collective-permute-start | bytes 1179656 | tf_op jit(solution)/shard_map/ppermute | solution.py:32
  1189.0 59.4 %collective-permute-start.43 = (bf16[192,768]{0,1:T(8,128)(2,1)S(1)}, bf16[192,768]{0,1:T(8,128)(2,1)S(1)}, u32[]{:S(2)}, u32[]{:S(2)}) collective-permute-start(bf16[192,768]{0,1:T(8,128)(2,1)S(1)} %dynamic-slice_bitcast_fusion.4), channel_id=1, source_target_pairs={{0,16},{4,20},{8,24},{12,28},{16,0},{20,4},{24,8},{28,12},{1,17},{... | collective-permute-start | bytes 884744 | tf_op jit(solution)/shard_map/ppermute | solution.py:32
  1327.3 65.7 %collective-permute-start.27 = (bf16[512,1536]{1,0:T(8,128)(2,1)}, bf16[512,1536]{1,0:T(8,128)(2,1)}, u32[]{:S(2)}, u32[]{:S(2)}) collective-permute-start(bf16[512,1536]{1,0:T(8,128)(2,1)} %slice.824), channel_id=1, source_target_pairs={{0,1},{1,0},{2,3},{3,2},{4,5},{5,4},{6,7},{7,6},{8,9},{9,8},{10,11... | collective-permute-start | bytes 4718600 | tf_op jit(solution)/shard_map/ppermute | solution.py:27
  1342.0 55.1 %collective-permute-start.49 = (bf16[2,2,192,1024]{3,2,1,0:T(8,128)(2,1)}, bf16[2,2,192,1024]{3,2,1,0:T(8,128)(2,1)}, u32[]{:S(2)}, u32[]{:S(2)}) collective-permute-start(bf16[2,2,192,1024]{3,2,1,0:T(8,128)(2,1)} %bitcast.596), channel_id=1, source_target_pairs={{0,2},{2,0},{1,3},{3,1},{4,6},{6,4},{5,7},{7,5},{8,10},{10,8},{9,1... | collective-permute-start | bytes 4718600 | tf_op jit(solution)/shard_map/ppermute | solution.py:32
  1390.7 64.0 %collective-permute-start.36 = (bf16[2,2,2,192,768]{4,3,2,1,0:T(8,128)(2,1)}, bf16[2,2,2,192,768]{4,3,2,1,0:T(8,128)(2,1)}, u32[]{:S(2)}, u32[]{:S(2)}) collective-permute-start(bf16[2,2,2,192,768]{4,3,2,1,0:T(8,128)(2,1)} %bitcast.581), channel_id=1, source_target_pairs={{0,2},{2,0},{1,3},{3,1},{4,6},{6,4},{5,7},{7,5},{8,10},{10,8},{9,1... | collective-permute-start | bytes 7077896 | tf_op jit(solution)/shard_map/ppermute | solution.py:32
  1467.2 48.0 %collective-permute-start.37 = (bf16[2,2,192,768]{3,2,1,0:T(8,128)(2,1)}, bf16[2,2,192,768]{3,2,1,0:T(8,128)(2,1)}, u32[]{:S(2)}, u32[]{:S(2)}) collective-permute-start(bf16[2,2,192,768]{3,2,1,0:T(8,128)(2,1)} %bitcast.611), channel_id=1, source_target_pairs={{0,4},{4,0},{8,12},{12,8},{16,20},{20,16},{24,28},{28,24},{1,5},{5... | collective-permute-start | bytes 3538952 | tf_op jit(solution)/shard_map/ppermute | solution.py:32
  (359 other events, 4392.3 us)
Sparse Core Ops, SparseCore 0:
  23.1 289.9 all-gather.3
  315.9 255.7 all-gather.5
  781.9 240.7 reduce-scatter.4
  1096.3 276.3 reduce-scatter.2

commit v3 on v2

--- a/solution.py
+++ b/solution.py
@@ -36,60 +36,54 @@
     return with_layout_constraint(part, Layout(major_to_minor=tuple(range(part.ndim))))
 
 
+def ordered(part, order):
+    return with_layout_constraint(part, Layout(major_to_minor=order))
+
+
 def gather_unit(part):
-    whole = lax.all_gather(plain(part), ("y", "dp"), axis=0, tiled=True)
+    whole = lax.all_gather(plain(part), ("y", "near", "far"), axis=0, tiled=True)
     rows = whole.shape[0] // 2
     return [whole[:rows], whole[rows:]]
 
 
-def scatter_unit(parts):
-    whole = plain(jnp.concatenate(parts, axis=0))
-    part = lax.psum_scatter(whole, ("y", "dp"), scatter_dimension=0, tiled=True)
+def scatter_unit(blocks):
+    rows, columns = blocks[0][0].shape
+    whole = jnp.zeros((2 * rows, len(blocks) * columns), half)
+    for k, pair in enumerate(blocks):
+        for y, part in enumerate(pair):
+            whole = lax.dynamic_update_slice(whole, plain(part), (y * rows, k * columns))
+    part = lax.psum_scatter(
+        plain(whole), ("y", "near", "far"), scatter_dimension=0, tiled=True
+    )
     return part.astype(jnp.float32)
 
 
-def join_step(part, place, axis, bit):
-    other = flip(part, axis, bit)
-    mine = (lax.axis_index(axis) // bit) % 2 == 0
-    return jnp.stack([jnp.where(mine, part, other), jnp.where(mine, other, part)], axis=place)
-
-
-def gather_pairs(part, row_first):
-    bits = (lax.axis_size("dp") - 1).bit_length()
-    part = plain(part)
-    for bit in range(bits - 1, 0, -1):
-        part = join_step(part, bits - 1 - bit, "dp", 1 << bit)
-    if row_first:
-        part = join_step(part, 0, "y", 1)
-        part = join_step(part, bits, "dp", 1)
-    else:
-        part = join_step(part, bits - 1, "dp", 1)
-        part = join_step(part, 0, "y", 1)
-    part = part.reshape(2, -1, part.shape[-1])
-    return [part[0], part[1]]
-
-
-def split_step(whole, place, axis, bit):
+def choose(parts, axis):
+    first = lax.axis_index(axis) == 0
+    own = jnp.where(first, parts[0], parts[1]).astype(jnp.float32)
+    sent = plain(jnp.where(first, parts[1], parts[0]))
+    return own + flip(sent, axis, 1).astype(jnp.float32)
+
+
+def split_rows(whole, axis, bit):
+    rows = whole.shape[0] // 2
     mine = (lax.axis_index(axis) // bit) % 2
-    own = lax.dynamic_index_in_dim(whole, mine, place, False)
-    sent = lax.dynamic_index_in_dim(whole, 1 - mine, place, False)
+    own = lax.dynamic_slice_in_dim(whole, mine * rows, rows)
+    sent = plain(lax.dynamic_slice_in_dim(whole, (1 - mine) * rows, rows))
     return own.astype(jnp.float32) + flip(sent, axis, bit).astype(jnp.float32)
 
 
-def scatter_pairs(parts, row_first):
-    bits = (lax.axis_size("dp") - 1).bit_length()
-    whole = jnp.stack([plain(p) for p in parts])
-    columns = whole.shape[2]
-    whole = whole.reshape((2,) + (2,) * bits + (-1, columns))
-    if row_first:
-        whole = split_step(whole, 0, "y", 1).astype(half)
-        whole = split_step(whole, bits - 1, "dp", 1)
-    else:
-        whole = split_step(whole, bits, "dp", 1).astype(half)
-        whole = split_step(whole, 0, "y", 1)
-    for bit in range(1, bits):
-        whole = split_step(whole.astype(half), bits - 1 - bit, "dp", 1 << bit)
-    return whole
+def scatter_rows(part, kind):
+    part = split_rows(part.astype(kind), "near", 1)
+    bit = lax.axis_size("far") // 2
+    while bit:
+        part = split_rows(part.astype(kind), "far", bit)
+        bit //= 2
+    return part
+
+
+def scatter_pairs(parts):
+    return scatter_rows(choose([plain(p) for p in parts], "y"), half)
 
 
 def total_over(value, axes):
@@ -299,12 +293,14 @@
     embedding, unembedding, attention_in, attention_out, feed_in, feed_out, norm_gains = masters
     row = lax.axis_index("y")
     core = lax.axis_index("c")
-    everywhere = ("dp", "y", "c")
-    size = lax.axis_size("dp")
+    everywhere = ("near", "far", "y", "c")
 
     vocab_rows = embedding.shape[0]
     table_pair = jnp.concatenate([embedding.T.astype(half), unembedding.astype(half)], axis=1)
-    vocab_ids = jnp.arange(4 * vocab_rows, dtype=jnp.int32)
+    near = jnp.arange(vocab_rows, dtype=jnp.int32)
+    vocab_ids = jnp.concatenate(
+        [(y * 2 + (core ^ step)) * vocab_rows + near for step in (0, 1) for y in (0, 1)]
+    )
 
     own_count = jnp.sum(target_lengths).astype(jnp.float32)
     gain_part = jnp.concatenate(
@@ -335,19 +331,18 @@
             [b[:, start + k * third : start + (k + 1) * third] for b in blocks] for k in range(3)
         ]
 
-    first = gather_unit(jnp.concatenate(attention_unit(0) + feed_units(0) + [table_pair], axis=1))
+    first = [u for layer in range(3) for u in attention_unit(layer)]
+    first = gather_unit(jnp.concatenate(first + feed_units(0) + [table_pair], axis=1))
     second = gather_unit(jnp.concatenate(feed_units(1), axis=1))
     span = 4 * attention_out.shape[1]
     edge = first[0].shape[1] - 2 * vocab_rows
-    attn = (
-        [b[:, :span] for b in first],
-        gather_pairs(jnp.concatenate(attention_unit(1), axis=1), False),
-        gather_pairs(jnp.concatenate(attention_unit(2), axis=1), True),
-    )
-    feed = (thirds(first, span), thirds(second, 0))
-    table_pairs = join_step(jnp.stack([plain(b[:, edge:]) for b in first]), 1, "c", 1)
-    table_pairs = table_pairs.reshape(4, -1, 2, vocab_rows).transpose(2, 1, 0, 3)
-    table_t, w_head = table_pairs.reshape(2, -1, 4 * vocab_rows)
+    attn = [[b[:, k * span : (k + 1) * span] for b in first] for k in range(3)]
+    feed = (thirds(first, 3 * span), thirds(second, 0))
+    near_pair = jnp.concatenate([b[:, edge:] for b in first], axis=1)
+    table_pairs = [near_pair, flip(plain(near_pair), "c", 1)]
+    table_pairs = [p[:, k * vocab_rows :][:, :vocab_rows] for p in table_pairs for k in range(4)]
+    table_t = jnp.concatenate(table_pairs[::2], axis=1)
+    w_head = jnp.concatenate(table_pairs[1::2], axis=1)
 
     source = lax.dynamic_index_in_dim(source_ids, row, 0, False)[0]
     target = lax.dynamic_index_in_dim(target_ids, row, 0, False)[0]
@@ -396,72 +391,70 @@
 
     d_tgt, gain_six = norm_back(tgt_top, gains[6], product_right(d_logits, w_head))
     *feed_one, d_in = expand_back(tgt_norm_c, *feed[1], keep_tgt_c, collect(d_tgt.astype(half)))
-    *feed_one, down_one = feed_one
-    down_one = scatter_pairs(down_one, False)
-    feed_one = scatter_unit([jnp.concatenate([plain(p) for p in g], axis=1) for g in zip(*feed_one)])
+    feed_one = scatter_unit(feed_one)
     d_more, gain_five = norm_back(tgt_cross, gains[5], fold(d_in))
     d_tgt = d_tgt + d_more
     attn_two, d_query, d_keys = cross_attention_back(
         tgt_norm_b, encoded, attn[2], key_bias, keep_tgt_b, collect(d_tgt.astype(half))
     )
-    attn_two = scatter_pairs(attn_two, True)
+    attn_two = scatter_pairs(attn_two)
     d_encoded = fold(d_keys)
     d_more, gain_four = norm_back(tgt_self, gains[4], fold(d_query))
     d_tgt = d_tgt + d_more
     attn_one, d_in = self_attention_back(
         tgt_norm_a, attn[1], causal, keep_tgt_a, collect(d_tgt.astype(half))
     )
-    attn_one = scatter_pairs(attn_one, False)
+    attn_one = scatter_pairs(attn_one)
     d_more, gain_three = norm_back(tgt_embed, gains[3], fold(d_in))
     d_tgt = d_tgt + d_more
 
     d_src, gain_two = norm_back(src_top, gains[2], d_encoded)
     *feed_zero, d_in = expand_back(src_norm_b, *feed[0], keep_src_b, collect(d_src.astype(half)))
-    *feed_zero, down_zero = feed_zero
-    down_zero = scatter_pairs(down_zero, False)
-    feed_zero = scatter_unit(
-        [jnp.concatenate([plain(p) for p in g], axis=1) for g in zip(*feed_zero)]
-    )
+    feed_zero = scatter_unit(feed_zero)
     d_more, gain_one = norm_back(src_mid, gains[1], fold(d_in))
     d_src = d_src + d_more
     attn_zero, d_in = self_attention_back(
         src_norm_a, attn[0], key_bias, keep_src_a, collect(d_src.astype(half))
     )
-    attn_zero = scatter_pairs(attn_zero, True)
+    attn_zero = scatter_pairs(attn_zero)
     d_more, gain_zero = norm_back(src_embed, gains[0], fold(d_in))
     d_src = d_src + d_more
 
     g_table = product_left(d_src.astype(half), source_hot)
     g_table = (g_table + product_left(d_tgt.astype(half), target_hot)).astype(half)
-    pairs = jnp.stack([g_table, g_head], axis=1).reshape(-1, 2, 2, 2, vocab_rows)
-    pairs = pairs.transpose(2, 3, 0, 1, 4).reshape(2, 2, -1, 2 * vocab_rows)
-    pairs = split_step(pairs, 1, "c", 1).astype(half)
-    pair_grad = scatter_pairs([pairs[0], pairs[1]], False)
+    pairs = [g[:, k * vocab_rows :][:, :vocab_rows] for k in range(4) for g in (g_table, g_head)]
+    pairs = [jnp.concatenate(pairs[k : k + 2], axis=1) for k in range(0, 8, 2)]
+    pairs = jnp.concatenate([plain(p) for p in pairs], axis=0)
+    rows = pairs.shape[0] // 2
+    pairs = pairs[:rows].astype(jnp.float32) + flip(pairs[rows:], "c", 1).astype(jnp.float32)
+    pairs = pairs.astype(half)
+    pair_grad = scatter_pairs([pairs[: rows // 2], pairs[rows // 2 :]])
 
     g_gains = jnp.stack([gain_zero, gain_one, gain_two, gain_three, gain_four, gain_five, gain_six])
-    g_gains = g_gains.T.reshape((2,) * (size - 1).bit_length() + (2, 2, -1, g_gains.shape[0]))
-    for axis in ("c", "y"):
-        g_gains = split_step(g_gains, g_gains.ndim - 3, axis, 1)
-    for bit in range((size - 1).bit_length()):
-        g_gains = split_step(g_gains, g_gains.ndim - 3, "dp", 1 << bit)
-    g_gains = g_gains.T
+    g_gains = scatter_rows(g_gains.T, jnp.float32)
+    g_gains = split_rows(split_rows(g_gains, "y", 1), "c", 1).T
 
     width = attention_out.shape[1]
     attn_grads = [attn_zero, attn_one, attn_two]
-    units = [pair_grad, *attn_grads, feed_zero, feed_one, down_zero, down_one]
+    units = [pair_grad, *attn_grads, feed_zero, feed_one]
     squares = sum(jnp.sum(g * g) for g in units) + jnp.sum(g_gains * g_gains)
-    feed_grads = [g.reshape(-1, 2, hidden_rows + spare[1][1]) for g in (feed_zero, feed_one)]
+    feed_grads = [thirds([g], 0) for g in (feed_zero, feed_one)]
     squares, loss = total_over(jnp.stack([squares, own_loss]), everywhere)
+    attn_in = [g[:, : 3 * width].reshape(-1, 3, width) for g in attn_grads]
+    gates_uppers = [
+        jnp.stack([gate[0][:, :hidden_rows], upper[0][:, :hidden_rows]], axis=1)
+        for gate, upper, _ in feed_grads
+    ]
+    downs = [down[0][:, :hidden_rows].T for _, _, down in feed_grads]
     grads = (
-        pair_grad[:, :vocab_rows].T,
-        pair_grad[:, vocab_rows:],
-        jnp.stack([g[:, : 3 * width].reshape(-1, 3, width) for g in attn_grads]),
-        jnp.stack([g[:, 3 * width :].T for g in attn_grads]),
-        jnp.stack(feed_grads)[..., :hidden_rows],
-        jnp.stack([g.T[:hidden_rows] for g in (down_zero, down_one)]),
+        plain(pair_grad[:, :vocab_rows].T),
+        plain(pair_grad[:, vocab_rows:]),
+        ordered(jnp.stack(attn_in), (0, 2, 1, 3)),
+        plain(jnp.stack([g[:, 3 * width :].T for g in attn_grads])),
+        plain(jnp.stack(gates_uppers)),
+        ordered(jnp.stack(downs), (0, 2, 1)),
         g_gains,
     )
-    grads = tuple(plain(g) for g in grads)
     grad_norm = jnp.sqrt(squares)
     scale = jnp.minimum(1.0, clip_limit / grad_norm)
     results = [
@@ -472,9 +465,9 @@
 
 
 def solution(mesh):
-    shape = (mesh.shape["dp"], mesh.shape["mp"] // 2, 2)
-    inner = Mesh(np.asarray(mesh.devices).reshape(shape), ("dp", "y", "c"))
-    dp = "dp"
+    shape = (mesh.shape["dp"] // 2, 2, mesh.shape["mp"] // 2, 2)
+    inner = Mesh(np.asarray(mesh.devices).reshape(shape), ("far", "near", "y", "c"))
+    dp = ("far", "near")
     mp = ("y", "c")
     params = (
         P(mp, dp),
@@ -483,7 +476,7 @@
         P(None, mp, dp),
         P(None, dp, None, mp),
         P(None, mp, dp),
-        P(None, (dp,) + mp),
+        P(None, dp + mp),
     )
     ids = (P(None, dp, None), P(None, dp, None), P(None, dp), P(None, dp))
     return jax.shard_map(

time: 1670 us -> 1460 us (0.87)
  other arithmetic: 299 us -> 165 us
  local copies, waits for them, and re-layouts: 299 us -> 203 us
  waiting for transfers between devices: 578 us -> 612 us
  starting transfers between devices: 51.3 us -> 33.5 us
    all_gather x2, waiting for transfers between devices: 228 us -> 367 us  [gather_unit(): lax.all_gather(plain(part), ('y', 'near', 'far'), axis=0, tiled=True)]
    ppermute x44 -> x28, waiting for transfers between devices: 350 us -> 218 us  [flip(): return lax.ppermute(part, axis, [(i, i ^ bit) for i in range(size)])]
    concatenate x4, other arithmetic: 70.8 us -> 2.37 us  [the longest x1 1.81 us: on_device(): pairs = jnp.concatenate([plain(p) for p in pairs], axis=0)]
    ppermute x17 -> x2, local copies, waits for them, and re-layouts: 50.8 us -> 3.23 us  [flip(): return lax.ppermute(part, axis, [(i, i ^ bit) for i in range(size)])]
    dynamic_slice x35 -> x16, local copies, waits for them, and re-layouts: 45.1 us -> 5.85 us  [split_rows(): sent = plain(lax.dynamic_slice_in_dim(whole, (1 - mine) * rows, rows))]
    another operation x21 -> x13, local copies, waits for them, and re-layouts: 65.4 us -> 27.4 us  [the longest x7 21.9 us: plain(): with_layout_constraint(part, Layout(major_to_minor=tuple(range(part.ndim))))]
    another operation x25 -> x5, other arithmetic: 41.4 us -> 6.76 us  [the longest x3 5.15 us: on_device(): jnp.stack(gates_uppers)]
    dynamic_update_slice x0 -> x2, local copies, waits for them, and re-layouts: none -> 30.4 us  [scatter_unit(): lax.dynamic_update_slice(whole, plain(part), (y * rows, k * columns))]
  transfers between devices with their start and end apart: 70 -> 54, of which waited for: 26 -> 25; matrix products, arithmetic and copies ran while one was open for 49% -> 38% of each run, Pallas kernels for 0% -> 0%
where the time goes in v3:
time: 1460 us; the launch traced here: 1450 us
  waiting for transfers between devices  612 us (42%)
  matrix products  365 us (25%)
  local copies, waits for them, and re-layouts  203 us (14%)
  other arithmetic  165 us (11%)
  blocking collectives  45.6 us (3%)
  starting transfers between devices  33.5 us (2%)
  between operations  26.4 us (2%)
    all_gather x2, waiting for transfers between devices, gather_unit(): lax.all_gather(plain(part), ('y', 'near', 'far'), axis=0, tiled=True)  367 us
    ppermute x28, waiting for transfers between devices, flip(): return lax.ppermute(part, axis, [(i, i ^ bit) for i in range(size)])  218 us
    dot_general x27, matrix products, product(): return jnp.dot(left, right, preferred_element_type=jnp.float32)  113 us
    dot_general x29, matrix products, product_right(): lax.dot_general(left, right, (((1,), (1,)), ((), ())), preferred_element_...  102 us
    dot_general x29, matrix products, product_left(): lax.dot_general(left, right, (((0,), (0,)), ((), ())), preferred_element_...  91.3 us
    unnamed x647, local copies, waits for them, and re-layouts  53.1 us
    all_gather x1, blocking collectives, on_device(): gain_part = lax.all_gather(gain_part, everywhere)  45.6 us
    dynamic_update_slice x2, local copies, waits for them, and re-layouts, scatter_unit(): lax.dynamic_update_slice(whole, plain(part), (y * rows, k * columns))  30.4 us
  transfers between devices with their start and end apart: 54, of which 25 were waited for; matrix products, arithmetic and copies ran while one was open for 38% of the time, Pallas kernels for 0%

profile of v3, /device:TPU:0, one launch (start us, length us, event | category | flops | bytes accessed | tf_op | source)
XLA Modules:
  0.0 1450.3 jit_solution(2826930776661276048)
XLA Ops:
  35.8 45.6 %all-gather = f32[256,48]{1,0:T(8,128)S(1)} all-gather(f32[8,48]{1,0:T(8,128)S(1)} %concatenate.127), channel_id=2, replica_groups=mesh['far'=4,'near'=2,'y'=2,'c'=2] {'near','far','y','c'}, dimensions={0}, use_global_device_ids=true | all-gather | bytes 50688 | tf_op jit(solution)/shard_map/all_gather | solution.py:309
  81.4 315.2 %all-gather.4.cloned.1.call-done = bf16[3072,5568]{1,0:T(8,128)(2,1)} async-done(((bf16[192,5568]{1,0:T(8,128)(2,1)}), bf16[3072,5568]{1,0:T(8,128)(2,1)}) %all-gather.4.cloned.1.call-update) | async-done | bytes 34209808 | tf_op jit(solution)/shard_map/all_gather | solution.py:44
  463.2 6.1 fusion.73
  469.4 6.8 fusion.85
  476.2 9.6 multiply_convert_fusion.5
  492.5 7.9 multiply_convert_fusion.4
  500.4 6.8 convolution_add_fusion.3
  556.2 52.2 %all-gather.6.cloned.1.call-done = bf16[3072,3072]{1,0:T(8,128)(2,1)} async-done(((bf16[192,3072]{1,0:T(8,128)(2,1)}), bf16[3072,3072]{1,0:T(8,128)(2,1)}) %all-gather.6.cloned.1.call-update) | async-done | bytes 18874384 | tf_op jit(solution)/shard_map/all_gather | solution.py:44
  650.3 15.2 %dynamic_update_slice.42 = bf16[3072,3072]{1,0:T(8,128)(2,1)} pad(bf16[1536,1024]{1,0:T(8,128)(2,1)S(1)} %convolution_convert_fusion.5, bf16[]{:T(256)} %constant.318.clone.1), padding=0_1536x0_2048 | pad | bytes 22020098 | tf_op jit(solution)/shard_map/dynamic_update_slice | solution.py:54
  804.2 8.2 multiply_convert_fusion.3
  816.3 15.2 %dynamic_update_slice.36 = bf16[3072,3072]{1,0:T(8,128)(2,1)} pad(bf16[1536,1024]{1,0:T(8,128)(2,1)S(1)} %convolution_convert_fusion.11, bf16[]{:T(256)} %constant.318.clone.1), padding=0_1536x0_2048 | pad | bytes 22020098 | tf_op jit(solution)/shard_map/dynamic_update_slice | solution.py:54
  831.5 8.1 multiply_convert_fusion.2
  927.5 7.5 fusion.83
  935.0 7.3 fusion.71
  942.3 7.4 fusion.79
  949.7 11.8 add_add_fusion
  966.3 29.8 %collective-permute-done.32 = bf16[1536,768]{0,1:T(8,128)(2,1)} collective-permute-done((bf16[1536,768]{0,1:T(8,128)(2,1)S(1)}, bf16[1536,768]{0,1:T(8,128)(2,1)}, u32[]{:S(2)}, u32[]{:S(2)}) %collective-permute-start.32) | collective-permute-done | bytes 2359328 | tf_op jit(solution)/shard_map/ppermute | solution.py:32
  999.2 5.9 collective-permute-done.38
  1012.3 11.6 collective-permute-done.33
  1031.8 37.9 %collective-permute-done.34 = bf16[384,768]{0,1:T(8,128)(2,1)} collective-permute-done((bf16[384,768]{0,1:T(8,128)(2,1)S(1)}, bf16[384,768]{0,1:T(8,128)(2,1)}, u32[]{:S(2)}, u32[]{:S(2)}) %collective-permute-start.34) | collective-permute-done | bytes 589856 | tf_op jit(solution)/shard_map/ppermute | solution.py:32
  1083.5 6.4 multiply_reduce_fusion.1
  1115.0 6.2 multiply_reduce_fusion
  1123.4 5.6 multiply_convert_fusion
  1176.6 5.9 fusion.42
  1196.1 7.3 collective-permute-done.41
  1204.8 43.0 %collective-permute-done.28 = bf16[1536,768]{0,1:T(8,128)(2,1)} collective-permute-done((bf16[1536,768]{0,1:T(8,128)(2,1)}, bf16[1536,768]{0,1:T(8,128)(2,1)}, u32[]{:S(2)}, u32[]{:S(2)}) %collective-permute-start.28) | collective-permute-done | bytes 2359328 | tf_op jit(solution)/shard_map/ppermute | solution.py:32
  1264.1 8.3 collective-permute-done.24
  1275.6 21.9 %collective-permute-done.29 = bf16[768,768]{0,1:T(8,128)(2,1)} collective-permute-done((bf16[768,768]{0,1:T(8,128)(2,1)}, bf16[768,768]{0,1:T(8,128)(2,1)}, u32[]{:S(2)}, u32[]{:S(2)}) %collective-permute-start.29) | collective-permute-done | bytes 1179680 | tf_op jit(solution)/shard_map/ppermute | solution.py:32
  1306.5 31.4 %collective-permute-done.26 = bf16[384,192]{1,0:T(8,128)(2,1)S(1)} collective-permute-done((bf16[384,192]{1,0:T(8,128)(2,1)S(1)}, bf16[384,192]{1,0:T(8,128)(2,1)S(1)}, u32[]{:S(2)}, u32[]{:S(2)}) %collective-permute-start.26) | collective-permute-done | bytes 147488 | tf_op jit(solution)/shard_map/ppermute | solution.py:32
  1345.0 5.8 collective-permute-done.31
  1360.5 17.8 %reduce-scatter.3.cloned.1.call-done = bf16[192,3072]{1,0:T(8,128)(2,1)} async-done(((bf16[3072,3072]{1,0:T(8,128)(2,1)}), bf16[192,3072]{1,0:T(8,128)(2,1)}) %reduce-scatter.3.cloned.1.call-update) | async-done | bytes 1179664 | tf_op jit(solution)/shard_map/reduce_scatter | solution.py:55
  1417.3 15.6 %multiply_subtract_fusion = (f32[2,192,2,992]{3,2,1,0:T(2,128)}, f32[2,192,2,992]{3,2,1,0:T(2,128)}, f32[2,192,2,992]{3,2,1,0:T(2,128)}) fusion(f32[2,192,2,992]{3,2,1,0:T(2,128)S(1)} %copy-done.34, f32[]{:T(128)S(6)} %min.3, f32[2,192,2,992]{3,1,2,0:T(8,128)} %pad_maximum_fusion.5, f32[2,192,2,992]{3,2,1,0:T(2,128)} %param.40, f32[2,192,2,992]{3,2,1,0:T(2,128)} %param.47), kind=kLoop, calls=%fused_computation.106 | loop fusion | flops 12189696 | bytes 21331972 | tf_op jit(solution)/shard_map/sub | solution.py:277
  (1098 shorter events, 632.8 us)
Async XLA Ops:
  7.2 389.4 %all-gather.4.cloned.1.call-start = ((), (), s32[]{:S(2)}) async-start(), calls=%async_computation.2 | async-start | bytes 36765696 | tf_op jit(solution)/shard_map/all_gather | solution.py:44
  33.2 575.3 %all-gather.6.cloned.1.call-start = ((), (), s32[]{:S(2)}) async-start(), calls=%async_computation.3 | async-start | bytes 20054016 | tf_op jit(solution)/shard_map/all_gather | solution.py:44
  34.4 1320.9 %reduce-scatter.5.cloned.1.call-start = ((), (), s32[]{:S(2)}) async-start(), calls=%async_computation.5 | async-start | bytes 20054016 | tf_op jit(solution)/shard_map/reduce_scatter | solution.py:55
  555.8 52.6 %collective-permute-start.10 = (bf16[128,1536]{1,0:T(8,128)(2,1)}, bf16[128,1536]{1,0:T(8,128)(2,1)}, u32[]{:S(2)}, u32[]{:S(2)}) collective-permute-start(bf16[128,1536]{1,0:T(8,128)(2,1)} %multiply_convert_fusion.18), channel_id=1, source_target_pairs={{0,1},{1,0},{2,3},{3,2},{4,5},{5,4},{6,7},{7,6},{8,9},{9,8},{10,11... | collective-permute-start | bytes 1179656 | tf_op jit(solution)/shard_map/ppermute | solution.py:27
  686.8 691.5 %reduce-scatter.3.cloned.1.call-start = ((), (), s32[]{:S(2)}) async-start(), calls=%async_computation.4 | async-start | bytes 20054016 | tf_op jit(solution)/shard_map/reduce_scatter | solution.py:55
  776.1 15.4 %collective-permute-start.15 = (bf16[512,1536]{1,0:T(8,128)(2,1)}, bf16[512,1536]{1,0:T(8,128)(2,1)}, u32[]{:S(2)}, u32[]{:S(2)}) collective-permute-start(bf16[512,1536]{1,0:T(8,128)(2,1)} %slice.957), channel_id=1, source_target_pairs={{0,1},{1,0},{2,3},{3,2},{4,5},{5,4},{6,7},{7,6},{8,9},{9,8},{10,11... | collective-permute-start | bytes 4718600 | tf_op jit(solution)/shard_map/ppermute | solution.py:27
  800.6 121.6 %collective-permute-start.36 = (bf16[1536,768]{0,1:T(8,128)(2,1)}, bf16[1536,768]{0,1:T(8,128)(2,1)}, u32[]{:S(2)}, u32[]{:S(2)}) collective-permute-start(bf16[1536,768]{0,1:T(8,128)(2,1)} %broadcast_select_fusion), channel_id=1, source_target_pairs={{0,2},{2,0},{1,3},{3,1},{4,6},{6,4},{5,7},{7,5},{8,10},{10,8},{9,1... | collective-permute-start | bytes 7077896 | tf_op jit(solution)/shard_map/ppermute | solution.py:32
  804.2 60.6 %collective-permute-start.21 = (bf16[128,1536]{1,0:T(8,128)(2,1)S(1)}, bf16[128,1536]{1,0:T(8,128)(2,1)}, u32[]{:S(2)}, u32[]{:S(2)}) collective-permute-start(bf16[128,1536]{1,0:T(8,128)(2,1)S(1)} %get-tuple-element.171), channel_id=1, source_target_pairs={{0,1},{1,0},{2,3},{3,2},{4,5},{5,4},{6,7},{7,6},{8,9},{9,8},{10,11... | collective-permute-start | bytes 1179656 | tf_op jit(solution)/shard_map/ppermute | solution.py:27
  889.9 32.0 %collective-permute-start.22 = (bf16[128,1536]{1,0:T(8,128)(2,1)}, bf16[128,1536]{1,0:T(8,128)(2,1)S(1)}, u32[]{:S(2)}, u32[]{:S(2)}) collective-permute-start(bf16[128,1536]{1,0:T(8,128)(2,1)} %slice.960), channel_id=1, source_target_pairs={{0,1},{1,0},{2,3},{3,2},{4,5},{5,4},{6,7},{7,6},{8,9},{9,8},{10,11... | collective-permute-start | bytes 1179656 | tf_op jit(solution)/shard_map/ppermute | solution.py:27
  921.4 74.7 %collective-permute-start.32 = (bf16[1536,768]{0,1:T(8,128)(2,1)S(1)}, bf16[1536,768]{0,1:T(8,128)(2,1)}, u32[]{:S(2)}, u32[]{:S(2)}) collective-permute-start(bf16[1536,768]{0,1:T(8,128)(2,1)S(1)} %broadcast_select_fusion.1), channel_id=1, source_target_pairs={{0,2},{2,0},{1,3},{3,1},{4,6},{6,4},{5,7},{7,5},{8,10},{10,8},{9,1... | collective-permute-start | bytes 7077896 | tf_op jit(solution)/shard_map/ppermute | solution.py:32
  927.0 35.9 %collective-permute-start.37 = (bf16[768,768]{0,1:T(8,128)(2,1)}, bf16[768,768]{0,1:T(8,128)(2,1)}, u32[]{:S(2)}, u32[]{:S(2)}) collective-permute-start(bf16[768,768]{0,1:T(8,128)(2,1)} %constant_dynamic-slice_fusion.8), channel_id=1, source_target_pairs={{0,4},{4,0},{1,5},{5,1},{2,6},{6,2},{3,7},{7,3},{8,12},{12,8},{9,1... | collective-permute-start | bytes 3538952 | tf_op jit(solution)/shard_map/ppermute | solution.py:32
  962.8 43.4 %collective-permute-start.17 = (bf16[512,1536]{1,0:T(8,128)(2,1)}, bf16[512,1536]{1,0:T(8,128)(2,1)S(1)}, u32[]{:S(2)}, u32[]{:S(2)}) collective-permute-start(bf16[512,1536]{1,0:T(8,128)(2,1)} %slice.956), channel_id=1, source_target_pairs={{0,1},{1,0},{2,3},{3,2},{4,5},{5,4},{6,7},{7,6},{8,9},{9,8},{10,11... | collective-permute-start | bytes 4718600 | tf_op jit(solution)/shard_map/ppermute | solution.py:27
  964.7 40.3 %collective-permute-start.38 = (bf16[384,768]{0,1:T(8,128)(2,1)S(1)}, bf16[384,768]{0,1:T(8,128)(2,1)S(1)}, u32[]{:S(2)}, u32[]{:S(2)}) collective-permute-start(bf16[384,768]{0,1:T(8,128)(2,1)S(1)} %constant_dynamic-slice_fusion.7), channel_id=1, source_target_pairs={{0,16},{8,24},{16,0},{24,8},{1,17},{9,25},{17,1},{25,9},{2,18},{10... | collective-permute-start | bytes 1769480 | tf_op jit(solution)/shard_map/ppermute | solution.py:32
  999.1 24.8 %collective-permute-start.33 = (bf16[768,768]{0,1:T(8,128)(2,1)S(1)}, bf16[768,768]{0,1:T(8,128)(2,1)S(1)}, u32[]{:S(2)}, u32[]{:S(2)}) collective-permute-start(bf16[768,768]{0,1:T(8,128)(2,1)S(1)} %constant_dynamic-slice_fusion.11), channel_id=1, source_target_pairs={{0,4},{4,0},{1,5},{5,1},{2,6},{6,2},{3,7},{7,3},{8,12},{12,8},{9,1... | collective-permute-start | bytes 3538952 | tf_op jit(solution)/shard_map/ppermute | solution.py:32
  1005.4 23.1 %collective-permute-start.39 = (bf16[192,768]{0,1:T(8,128)(2,1)S(1)}, bf16[192,768]{0,1:T(8,128)(2,1)S(1)}, u32[]{:S(2)}, u32[]{:S(2)}) collective-permute-start(bf16[192,768]{0,1:T(8,128)(2,1)S(1)} %constant_dynamic-slice_fusion.6), channel_id=1, source_target_pairs={{0,8},{8,0},{16,24},{24,16},{1,9},{9,1},{17,25},{25,17},{2,10},{10... | collective-permute-start | bytes 884744 | tf_op jit(solution)/shard_map/ppermute | solution.py:32
  1012.3 60.5 %collective-permute-start.18 = (bf16[512,1536]{1,0:T(8,128)(2,1)}, bf16[512,1536]{1,0:T(8,128)(2,1)}, u32[]{:S(2)}, u32[]{:S(2)}) collective-permute-start(bf16[512,1536]{1,0:T(8,128)(2,1)} %get-tuple-element.169), channel_id=1, source_target_pairs={{0,1},{1,0},{2,3},{3,2},{4,5},{5,4},{6,7},{7,6},{8,9},{9,8},{10,11... | collective-permute-start | bytes 4718600 | tf_op jit(solution)/shard_map/ppermute | solution.py:27
  1024.3 45.4 %collective-permute-start.34 = (bf16[384,768]{0,1:T(8,128)(2,1)S(1)}, bf16[384,768]{0,1:T(8,128)(2,1)}, u32[]{:S(2)}, u32[]{:S(2)}) collective-permute-start(bf16[384,768]{0,1:T(8,128)(2,1)S(1)} %constant_dynamic-slice_fusion.10), channel_id=1, source_target_pairs={{0,16},{8,24},{16,0},{24,8},{1,17},{9,25},{17,1},{25,9},{2,18},{10... | collective-permute-start | bytes 1769480 | tf_op jit(solution)/shard_map/ppermute | solution.py:32
  1072.7 120.7 %collective-permute-start.35 = (bf16[192,768]{0,1:T(8,128)(2,1)}, bf16[192,768]{0,1:T(8,128)(2,1)}, u32[]{:S(2)}, u32[]{:S(2)}) collective-permute-start(bf16[192,768]{0,1:T(8,128)(2,1)} %constant_dynamic-slice_fusion.9), channel_id=1, source_target_pairs={{0,8},{8,0},{16,24},{24,16},{1,9},{9,1},{17,25},{25,17},{2,10},{10... | collective-permute-start | bytes 884744 | tf_op jit(solution)/shard_map/ppermute | solution.py:32
  1150.4 20.8 %collective-permute-start.19 = (bf16[512,1536]{1,0:T(8,128)(2,1)}, bf16[512,1536]{1,0:T(8,128)(2,1)}, u32[]{:S(2)}, u32[]{:S(2)}) collective-permute-start(bf16[512,1536]{1,0:T(8,128)(2,1)} %slice.955), channel_id=1, source_target_pairs={{0,1},{1,0},{2,3},{3,2},{4,5},{5,4},{6,7},{7,6},{8,9},{9,8},{10,11... | collective-permute-start | bytes 4718600 | tf_op jit(solution)/shard_map/ppermute | solution.py:27
  1169.2 78.6 %collective-permute-start.28 = (bf16[1536,768]{0,1:T(8,128)(2,1)}, bf16[1536,768]{0,1:T(8,128)(2,1)}, u32[]{:S(2)}, u32[]{:S(2)}) collective-permute-start(bf16[1536,768]{0,1:T(8,128)(2,1)} %broadcast_select_fusion.2), channel_id=1, source_target_pairs={{0,2},{2,0},{1,3},{3,1},{4,6},{6,4},{5,7},{7,5},{8,10},{10,8},{9,1... | collective-permute-start | bytes 7077896 | tf_op jit(solution)/shard_map/ppermute | solution.py:32
  1176.0 14.7 %collective-permute-start.40 = (f32[768,7]{1,0:T(8,128)}, f32[768,7]{1,0:T(8,128)}, u32[]{:S(2)}, u32[]{:S(2)}) collective-permute-start(f32[768,7]{1,0:T(8,128)} %bitcast.106), channel_id=1, source_target_pairs={{0,4},{4,0},{1,5},{5,1},{2,6},{6,2},{3,7},{7,3},{8,12},{12,8},{9,1... | collective-permute-start | bytes 64520 | tf_op jit(solution)/shard_map/ppermute | solution.py:32
  1188.5 63.9 %collective-permute-start.23 = (bf16[3072,192]{0,1:T(8,128)(2,1)}, bf16[3072,192]{0,1:T(8,128)(2,1)}, u32[]{:S(2)}, u32[]{:S(2)}) collective-permute-start(bf16[3072,192]{0,1:T(8,128)(2,1)} %copy.365), channel_id=1, source_target_pairs={{0,1},{1,0},{2,3},{3,2},{4,5},{5,4},{6,7},{7,6},{8,9},{9,8},{10,11... | collective-permute-start | bytes 3538952 | tf_op jit(solution)/shard_map/ppermute | solution.py:32
  1191.8 11.6 collective-permute-start.41
  1204.8 57.9 %collective-permute-start.42 = (f32[192,7]{1,0:T(8,128)}, f32[192,7]{1,0:T(8,128)}, u32[]{:S(2)}, u32[]{:S(2)}) collective-permute-start(f32[192,7]{1,0:T(8,128)} %constant_dynamic-slice_fusion.2), channel_id=1, source_target_pairs={{0,8},{8,0},{16,24},{24,16},{1,9},{9,1},{17,25},{25,17},{2,10},{10... | collective-permute-start | bytes 16136 | tf_op jit(solution)/shard_map/ppermute | solution.py:32
  1257.5 14.8 %collective-permute-start.24 = (bf16[1536,192]{0,1:T(8,128)(2,1)}, bf16[1536,192]{0,1:T(8,128)(2,1)}, u32[]{:S(2)}, u32[]{:S(2)}) collective-permute-start(bf16[1536,192]{0,1:T(8,128)(2,1)} %copy.367), channel_id=1, source_target_pairs={{0,2},{2,0},{1,3},{3,1},{4,6},{6,4},{5,7},{7,5},{8,10},{10,8},{9,1... | collective-permute-start | bytes 1769480 | tf_op jit(solution)/shard_map/ppermute | solution.py:32
  1259.9 37.6 %collective-permute-start.29 = (bf16[768,768]{0,1:T(8,128)(2,1)}, bf16[768,768]{0,1:T(8,128)(2,1)}, u32[]{:S(2)}, u32[]{:S(2)}) collective-permute-start(bf16[768,768]{0,1:T(8,128)(2,1)} %constant_dynamic-slice_fusion.14), channel_id=1, source_target_pairs={{0,4},{4,0},{1,5},{5,1},{2,6},{6,2},{3,7},{7,3},{8,12},{12,8},{9,1... | collective-permute-start | bytes 3538952 | tf_op jit(solution)/shard_map/ppermute | solution.py:32
  1263.6 42.8 %collective-permute-start.43 = (f32[96,7]{1,0:T(8,128)S(1)}, f32[96,7]{1,0:T(8,128)S(1)}, u32[]{:S(2)}, u32[]{:S(2)}) collective-permute-start(f32[96,7]{1,0:T(8,128)S(1)} %constant_dynamic-slice_fusion.1), channel_id=1, source_target_pairs={{0,2},{2,0},{1,3},{3,1},{4,6},{6,4},{5,7},{7,5},{8,10},{10,8},{9,1... | collective-permute-start | bytes 8072 | tf_op jit(solution)/shard_map/ppermute | solution.py:32
  1274.1 29.5 %collective-permute-start.25 = (bf16[768,192]{1,0:T(8,128)(2,1)S(1)}, bf16[768,192]{1,0:T(8,128)(2,1)S(1)}, u32[]{:S(2)}, u32[]{:S(2)}) collective-permute-start(bf16[768,192]{1,0:T(8,128)(2,1)S(1)} %constant_dynamic-slice_fusion.17), channel_id=1, source_target_pairs={{0,4},{4,0},{1,5},{5,1},{2,6},{6,2},{3,7},{7,3},{8,12},{12,8},{9,1... | collective-permute-start | bytes 884744 | tf_op jit(solution)/shard_map/ppermute | solution.py:32
  1299.2 38.8 %collective-permute-start.30 = (bf16[384,768]{0,1:T(8,128)(2,1)S(1)}, bf16[384,768]{0,1:T(8,128)(2,1)S(1)}, u32[]{:S(2)}, u32[]{:S(2)}) collective-permute-start(bf16[384,768]{0,1:T(8,128)(2,1)S(1)} %constant_dynamic-slice_fusion.13), channel_id=1, source_target_pairs={{0,16},{8,24},{16,0},{24,8},{1,17},{9,25},{17,1},{25,9},{2,18},{10... | collective-permute-start | bytes 1769480 | tf_op jit(solution)/shard_map/ppermute | solution.py:32
  1303.8 34.1 %collective-permute-start.26 = (bf16[384,192]{1,0:T(8,128)(2,1)S(1)}, bf16[384,192]{1,0:T(8,128)(2,1)S(1)}, u32[]{:S(2)}, u32[]{:S(2)}) collective-permute-start(bf16[384,192]{1,0:T(8,128)(2,1)S(1)} %constant_dynamic-slice_fusion.16), channel_id=1, source_target_pairs={{0,16},{8,24},{16,0},{24,8},{1,17},{9,25},{17,1},{25,9},{2,18},{10... | collective-permute-start | bytes 442376 | tf_op jit(solution)/shard_map/ppermute | solution.py:32
  1306.4 34.1 %collective-permute-start.44 = (f32[48,7]{1,0:T(8,128)S(1)}, f32[48,7]{1,0:T(8,128)S(1)}, u32[]{:S(2)}, u32[]{:S(2)}) collective-permute-start(f32[48,7]{1,0:T(8,128)S(1)} %constant_dynamic-slice_fusion), channel_id=1, source_target_pairs={{0,1},{1,0},{2,3},{3,2},{4,5},{5,4},{6,7},{7,6},{8,9},{9,8},{10,11... | collective-permute-start | bytes 4040 | tf_op jit(solution)/shard_map/ppermute | solution.py:32
  1338.4 12.3 collective-permute-start.31
  (341 other events, 3040.8 us)
Sparse Core Ops, SparseCore 0:
  33.3 363.2 all-gather.3
  399.3 209.0 all-gather.5
  686.9 339.5 reduce-scatter.4
  1032.1 346.1 reduce-scatter.2

commit v4 on v3

--- a/solution.py
+++ b/solution.py
@@ -41,14 +41,41 @@
 
 
 def gather_unit(part):
-    whole = lax.all_gather(plain(part), ("y", "near", "far"), axis=0, tiled=True)
+    return lax.all_gather(plain(part), ("y", "near", "far"), axis=0, tiled=True)
+
+
+def halves(whole):
     rows = whole.shape[0] // 2
     return [whole[:rows], whole[rows:]]
 
 
-def scatter_unit(blocks):
+def place(part, other, axis, bit):
+    first = (lax.axis_index(axis) // bit) % 2 == 0
+    return [jnp.where(first, part, other), jnp.where(first, other, part)]
+
+
+def join_rows(part, axis, bit):
+    part = plain(part)
+    return jnp.concatenate(place(part, flip(part, axis, bit), axis, bit), axis=0)
+
+
+def gather_pairs(part, row_first):
+    bit = 1
+    while bit < lax.axis_size("far"):
+        part = join_rows(part, "far", bit)
+        bit *= 2
+    if not row_first:
+        part = plain(join_rows(part, "near", 1))
+        return place(part, flip(part, "y", 1), "y", 1)
+    part = plain(part)
+    both = plain(jnp.concatenate([part, flip(part, "y", 1)], axis=0))
+    pairs = zip(halves(both), halves(flip(both, "near", 1)))
+    own, other = [jnp.concatenate(place(p, q, "near", 1), axis=0) for p, q in pairs]
+    return place(own, other, "y", 1)
+
+
+def scatter_unit(blocks, whole):
     rows, columns = blocks[0][0].shape
-    whole = jnp.zeros((2 * rows, len(blocks) * columns), half)
     for k, pair in enumerate(blocks):
         for y, part in enumerate(pair):
             whole = lax.dynamic_update_slice(whole, plain(part), (y * rows, k * columns))
@@ -331,13 +358,18 @@
             [b[:, start + k * third : start + (k + 1) * third] for b in blocks] for k in range(3)
         ]
 
-    first = [u for layer in range(3) for u in attention_unit(layer)]
-    first = gather_unit(jnp.concatenate(first + feed_units(0) + [table_pair], axis=1))
-    second = gather_unit(jnp.concatenate(feed_units(1), axis=1))
-    span = 4 * attention_out.shape[1]
+    first = gather_unit(jnp.concatenate(feed_units(0) + [table_pair], axis=1))
+    second = halves(gather_unit(jnp.concatenate(feed_units(1), axis=1)))
+    attn = [
+        gather_pairs(jnp.concatenate(attention_unit(layer), axis=1), row_first)
+        for layer, row_first in enumerate((False, True, False))
+    ]
+    fills = (jnp.minimum(jnp.sum(target_lengths), 0), jnp.minimum(jnp.sum(source_lengths), 0))
+    blanks = [jnp.full((2 * b.shape[0], b.shape[1]), f.astype(half)) for b, f in zip(second, fills)]
+    first, attn, blanks = lax.optimization_barrier((first, attn, blanks))
+    first = halves(first)
     edge = first[0].shape[1] - 2 * vocab_rows
-    attn = [[b[:, k * span : (k + 1) * span] for b in first] for k in range(3)]
-    feed = (thirds(first, 3 * span), thirds(second, 0))
+    feed = (thirds(first, 0), thirds(second, 0))
     near_pair = jnp.concatenate([b[:, edge:] for b in first], axis=1)
     table_pairs = [near_pair, flip(plain(near_pair), "c", 1)]
     table_pairs = [p[:, k * vocab_rows :][:, :vocab_rows] for p in table_pairs for k in range(4)]
@@ -391,7 +423,7 @@
 
     d_tgt, gain_six = norm_back(tgt_top, gains[6], product_right(d_logits, w_head))
     *feed_one, d_in = expand_back(tgt_norm_c, *feed[1], keep_tgt_c, collect(d_tgt.astype(half)))
-    feed_one = scatter_unit(feed_one)
+    feed_one = scatter_unit(feed_one, blanks[1])
     d_more, gain_five = norm_back(tgt_cross, gains[5], fold(d_in))
     d_tgt = d_tgt + d_more
     attn_two, d_query, d_keys = cross_attention_back(
@@ -410,7 +442,7 @@
 
     d_src, gain_two = norm_back(src_top, gains[2], d_encoded)
     *feed_zero, d_in = expand_back(src_norm_b, *feed[0], keep_src_b, collect(d_src.astype(half)))
-    feed_zero = scatter_unit(feed_zero)
+    feed_zero = scatter_unit(feed_zero, blanks[0])
     d_more, gain_one = norm_back(src_mid, gains[1], fold(d_in))
     d_src = d_src + d_more
     attn_zero, d_in = self_attention_back(

time: 1460 us -> 1450 us (level)
  waiting for transfers between devices: 612 us -> 462 us
  blocking collectives: 45.6 us -> 154 us
  other arithmetic: 165 us -> 204 us
  starting transfers between devices: 33.5 us -> 64.4 us
  local copies, waits for them, and re-layouts: 203 us -> 176 us
  matrix products: 365 us -> 345 us
    all_gather x2, waiting for transfers between devices: 367 us -> 6.51 us  [gather_unit(): return lax.all_gather(plain(part), ('y', 'near', 'far'), axis=0, tiled=True)]
    ppermute x28 -> x40, waiting for transfers between devices: 218 us -> 422 us  [flip(): return lax.ppermute(part, axis, [(i, i ^ bit) for i in range(size)])]
    all_gather x1, blocking collectives: 45.6 us -> 154 us  [on_device(): gain_part = lax.all_gather(gain_part, everywhere)]
    ppermute x28 -> x40, starting transfers between devices: 26.6 us -> 58.5 us  [flip(): return lax.ppermute(part, axis, [(i, i ^ bit) for i in range(size)])]
    dynamic_update_slice x2 -> x0, local copies, waits for them, and re-layouts: 30.4 us -> none  [scatter_unit(): lax.dynamic_update_slice(whole, plain(part), (y * rows, k * columns))]
    select_n x0 -> x11, other arithmetic: none -> 21.8 us  [place(): return [jnp.where(first, part, other), jnp.where(first, other, part)]]
    unnamed x647 -> x687, local copies, waits for them, and re-layouts: 53.1 us -> 52.7 us
  transfers between devices with their start and end apart: 54 -> 66, of which waited for: 25 -> 30; matrix products, arithmetic and copies ran while one was open for 38% -> 41% of each run, Pallas kernels for 0% -> 0%
where the time goes in v4:
time: 1450 us; the launch traced here: 1430 us
  waiting for transfers between devices  462 us (32%)
  matrix products  345 us (24%)
  other arithmetic  204 us (14%)
  local copies, waits for them, and re-layouts  176 us (12%)
  blocking collectives  154 us (11%)
  starting transfers between devices  64.4 us (4%)
  between operations  27.7 us (2%)
    ppermute x40, waiting for transfers between devices, flip(): return lax.ppermute(part, axis, [(i, i ^ bit) for i in range(size)])  422 us
    all_gather x1, blocking collectives, on_device(): gain_part = lax.all_gather(gain_part, everywhere)  154 us
    dot_general x27, matrix products, product(): return jnp.dot(left, right, preferred_element_type=jnp.float32)  98.7 us
    dot_general x29, matrix products, product_left(): lax.dot_general(left, right, (((0,), (0,)), ((), ())), preferred_element_...  97.1 us
    dot_general x29, matrix products, product_right(): lax.dot_general(left, right, (((1,), (1,)), ((), ())), preferred_element_...  90.8 us
    ppermute x40, starting transfers between devices, flip(): return lax.ppermute(part, axis, [(i, i ^ bit) for i in range(size)])  58.5 us
    unnamed x687, local copies, waits for them, and re-layouts  52.7 us
  transfers between devices with their start and end apart: 66, of which 30 were waited for; matrix products, arithmetic and copies ran while one was open for 41% of the time, Pallas kernels for 0%

profile of v4, /device:TPU:0, one launch (start us, length us, event | category | flops | bytes accessed | tf_op | source)
XLA Modules:
  0.0 1433.0 jit_solution(8776054447622599108)
XLA Ops:
  19.6 7.3 collective-permute-done.4
  27.7 14.3 %collective-permute-done.8 = bf16[192,768]{1,0:T(8,128)(2,1)S(1)} collective-permute-done((bf16[192,768]{1,0:T(8,128)(2,1)S(1)}, bf16[192,768]{1,0:T(8,128)(2,1)S(1)}, u32[]{:S(2)}, u32[]{:S(2)}) %collective-permute-start.8) | collective-permute-done | bytes 294944 | tf_op jit(solution)/shard_map/ppermute | solution.py:32
  55.7 56.0 %collective-permute-done.9 = bf16[384,768]{1,0:T(8,128)(2,1)S(1)} collective-permute-done((bf16[384,768]{1,0:T(8,128)(2,1)}, bf16[384,768]{1,0:T(8,128)(2,1)S(1)}, u32[]{:S(2)}, u32[]{:S(2)}) %collective-permute-start.9) | collective-permute-done | bytes 589856 | tf_op jit(solution)/shard_map/ppermute | solution.py:32
  116.9 48.8 %collective-permute-done.5 = bf16[384,768]{1,0:T(8,128)(2,1)} collective-permute-done((bf16[384,768]{1,0:T(8,128)(2,1)}, bf16[384,768]{1,0:T(8,128)(2,1)}, u32[]{:S(2)}, u32[]{:S(2)}) %collective-permute-start.5) | collective-permute-done | bytes 589856 | tf_op jit(solution)/shard_map/ppermute | solution.py:32
  169.5 20.4 %collective-permute-done.1 = bf16[384,768]{1,0:T(8,128)(2,1)S(1)} collective-permute-done((bf16[384,768]{1,0:T(8,128)(2,1)}, bf16[384,768]{1,0:T(8,128)(2,1)S(1)}, u32[]{:S(2)}, u32[]{:S(2)}) %collective-permute-start.1) | collective-permute-done | bytes 589856 | tf_op jit(solution)/shard_map/ppermute | solution.py:32
  199.6 43.4 %collective-permute-done.2 = bf16[768,768]{1,0:T(8,128)(2,1)S(1)} collective-permute-done((bf16[768,768]{1,0:T(8,128)(2,1)S(1)}, bf16[768,768]{1,0:T(8,128)(2,1)S(1)}, u32[]{:S(2)}, u32[]{:S(2)}) %collective-permute-start.2) | collective-permute-done | bytes 1179680 | tf_op jit(solution)/shard_map/ppermute | solution.py:32
  251.7 154.5 %all-gather = f32[256,48]{1,0:T(8,128)} all-gather(f32[8,48]{1,0:T(8,128)S(1)} %concatenate.183), channel_id=2, replica_groups=mesh['far'=4,'near'=2,'y'=2,'c'=2] {'near','far','y','c'}, dimensions={0}, use_global_device_ids=true | all-gather | bytes 50688 | tf_op jit(solution)/shard_map/all_gather | solution.py:336
  421.6 7.1 broadcast_in_dim.37
  428.7 7.1 broadcast_in_dim.38
  503.4 8.5 fusion.75
  516.9 8.2 multiply_convert_fusion.5
  532.2 8.6 multiply_convert_fusion.4
  540.8 7.9 convolution_add_fusion.3
  755.4 8.1 multiply_convert_fusion.3
  769.7 8.0 multiply_convert_fusion.2
  862.5 7.4 fusion.81
  869.9 7.4 fusion.85
  877.3 7.2 fusion.73
  884.5 12.2 add_add_fusion
  901.7 23.3 %collective-permute-done.44 = bf16[1536,768]{0,1:T(8,128)(2,1)} collective-permute-done((bf16[1536,768]{0,1:T(8,128)(2,1)S(1)}, bf16[1536,768]{0,1:T(8,128)(2,1)}, u32[]{:S(2)}, u32[]{:S(2)}) %collective-permute-start.44) | collective-permute-done | bytes 2359328 | tf_op jit(solution)/shard_map/ppermute | solution.py:32
  929.5 9.3 collective-permute-done.50
  946.0 9.8 collective-permute-done.45
  971.0 40.8 %collective-permute-done.46 = bf16[384,768]{0,1:T(8,128)(2,1)} collective-permute-done((bf16[384,768]{0,1:T(8,128)(2,1)}, bf16[384,768]{0,1:T(8,128)(2,1)}, u32[]{:S(2)}, u32[]{:S(2)}) %collective-permute-start.46) | collective-permute-done | bytes 589856 | tf_op jit(solution)/shard_map/ppermute | solution.py:32
  1022.4 10.9 multiply_reduce_fusion
  1035.9 11.0 multiply_convert_fusion
  1061.7 9.3 multiply_convert_fusion.1
  1160.4 50.8 %collective-permute-done.40 = bf16[1536,768]{0,1:T(8,128)(2,1)} collective-permute-done((bf16[1536,768]{0,1:T(8,128)(2,1)}, bf16[1536,768]{0,1:T(8,128)(2,1)}, u32[]{:S(2)}, u32[]{:S(2)}) %collective-permute-start.40) | collective-permute-done | bytes 2359328 | tf_op jit(solution)/shard_map/ppermute | solution.py:32
  1228.6 16.2 %collective-permute-done.36 = bf16[1536,192]{0,1:T(8,128)(2,1)} collective-permute-done((bf16[1536,192]{0,1:T(8,128)(2,1)}, bf16[1536,192]{0,1:T(8,128)(2,1)}, u32[]{:S(2)}, u32[]{:S(2)}) %collective-permute-start.36) | collective-permute-done | bytes 589856 | tf_op jit(solution)/shard_map/ppermute | solution.py:32
  1248.3 16.1 %collective-permute-done.41 = bf16[768,768]{0,1:T(8,128)(2,1)} collective-permute-done((bf16[768,768]{0,1:T(8,128)(2,1)}, bf16[768,768]{0,1:T(8,128)(2,1)}, u32[]{:S(2)}, u32[]{:S(2)}) %collective-permute-start.41) | collective-permute-done | bytes 1179680 | tf_op jit(solution)/shard_map/ppermute | solution.py:32
  1277.8 37.4 %collective-permute-done.38 = bf16[384,192]{1,0:T(8,128)(2,1)S(1)} collective-permute-done((bf16[384,192]{1,0:T(8,128)(2,1)S(1)}, bf16[384,192]{1,0:T(8,128)(2,1)S(1)}, u32[]{:S(2)}, u32[]{:S(2)}) %collective-permute-start.38) | collective-permute-done | bytes 147488 | tf_op jit(solution)/shard_map/ppermute | solution.py:32
  1338.3 23.4 %reduce-scatter.3.cloned.1.call-done = bf16[192,3072]{1,0:T(8,128)(2,1)} async-done(((bf16[3072,3072]{1,0:T(8,128)(2,1)}), bf16[192,3072]{1,0:T(8,128)(2,1)}) %reduce-scatter.3.cloned.1.call-update) | async-done | bytes 1179664 | tf_op jit(solution)/shard_map/reduce_scatter | solution.py:82
  1399.4 15.5 %multiply_subtract_fusion = (f32[2,192,2,992]{3,2,1,0:T(2,128)}, f32[2,192,2,992]{3,2,1,0:T(2,128)}, f32[2,192,2,992]{3,2,1,0:T(2,128)}) fusion(f32[2,192,2,992]{3,2,1,0:T(2,128)S(1)} %copy-done.33, f32[]{:T(128)S(6)} %min.11, f32[2,192,2,992]{3,1,2,0:T(8,128)} %pad_maximum_fusion.5, f32[2,192,2,992]{3,2,1,0:T(2,128)} %param.40, f32[2,192,2,992]{3,2,1,0:T(2,128)} %param.47), kind=kLoop, calls=%fused_computation.108 | loop fusion | flops 12189696 | bytes 21331972 | tf_op jit(solution)/shard_map/sub | solution.py:304
  (1186 shorter events, 688.9 us)
Async XLA Ops:
  7.2 414.4 %all-gather.4.cloned.1.call-start = ((), (), s32[]{:S(2)}) async-start(), calls=%async_computation.2 | async-start | bytes 21725184 | tf_op jit(solution)/shard_map/all_gather | solution.py:44
  14.6 580.0 %all-gather.6.cloned.1.call-start = ((), (), s32[]{:S(2)}) async-start(), calls=%async_computation.3 | async-start | bytes 20054016 | tf_op jit(solution)/shard_map/all_gather | solution.py:44
  44.2 67.5 %collective-permute-start.9 = (bf16[384,768]{1,0:T(8,128)(2,1)}, bf16[384,768]{1,0:T(8,128)(2,1)S(1)}, u32[]{:S(2)}, u32[]{:S(2)}) collective-permute-start(bf16[384,768]{1,0:T(8,128)(2,1)} %pad_maximum_fusion.35), channel_id=1, source_target_pairs={{0,16},{8,24},{16,0},{24,8},{1,17},{9,25},{17,1},{25,9},{2,18},{10... | collective-permute-start | bytes 1769480 | tf_op jit(solution)/shard_map/ppermute | solution.py:32
  52.0 62.9 %collective-permute-start = (bf16[192,768]{1,0:T(8,128)(2,1)}, bf16[192,768]{1,0:T(8,128)(2,1)}, u32[]{:S(2)}, u32[]{:S(2)}) collective-permute-start(bf16[192,768]{1,0:T(8,128)(2,1)} %pad_maximum_fusion.44), channel_id=1, source_target_pairs={{0,8},{8,0},{16,24},{24,16},{1,9},{9,1},{17,25},{25,17},{2,10},{10... | collective-permute-start | bytes 884744 | tf_op jit(solution)/shard_map/ppermute | solution.py:32
  55.7 110.1 %collective-permute-start.5 = (bf16[384,768]{1,0:T(8,128)(2,1)}, bf16[384,768]{1,0:T(8,128)(2,1)}, u32[]{:S(2)}, u32[]{:S(2)}) collective-permute-start(bf16[384,768]{1,0:T(8,128)(2,1)} %pad_maximum_fusion.34), channel_id=1, source_target_pairs={{0,16},{8,24},{16,0},{24,8},{1,17},{9,25},{17,1},{25,9},{2,18},{10... | collective-permute-start | bytes 1769480 | tf_op jit(solution)/shard_map/ppermute | solution.py:32
  113.0 78.8 %collective-permute-start.10 = (bf16[768,768]{1,0:T(8,128)(2,1)}, bf16[768,768]{1,0:T(8,128)(2,1)}, u32[]{:S(2)}, u32[]{:S(2)}) collective-permute-start(bf16[768,768]{1,0:T(8,128)(2,1)} %pad_maximum_fusion.19), channel_id=1, source_target_pairs={{0,4},{4,0},{1,5},{5,1},{2,6},{6,2},{3,7},{7,3},{8,12},{12,8},{9,1... | collective-permute-start | bytes 3538952 | tf_op jit(solution)/shard_map/ppermute | solution.py:32
  116.9 73.0 %collective-permute-start.1 = (bf16[384,768]{1,0:T(8,128)(2,1)}, bf16[384,768]{1,0:T(8,128)(2,1)S(1)}, u32[]{:S(2)}, u32[]{:S(2)}) collective-permute-start(bf16[384,768]{1,0:T(8,128)(2,1)} %pad_maximum_fusion.33), channel_id=1, source_target_pairs={{0,16},{8,24},{16,0},{24,8},{1,17},{9,25},{17,1},{25,9},{2,18},{10... | collective-permute-start | bytes 1769480 | tf_op jit(solution)/shard_map/ppermute | solution.py:32
  190.3 52.7 %collective-permute-start.2 = (bf16[768,768]{1,0:T(8,128)(2,1)S(1)}, bf16[768,768]{1,0:T(8,128)(2,1)S(1)}, u32[]{:S(2)}, u32[]{:S(2)}) collective-permute-start(bf16[768,768]{1,0:T(8,128)(2,1)S(1)} %pad_maximum_fusion.17), channel_id=1, source_target_pairs={{0,4},{4,0},{1,5},{5,1},{2,6},{6,2},{3,7},{7,3},{8,12},{12,8},{9,1... | collective-permute-start | bytes 3538952 | tf_op jit(solution)/shard_map/ppermute | solution.py:32
  195.9 210.3 %collective-permute-start.11 = (bf16[1536,768]{1,0:T(8,128)(2,1)}, bf16[1536,768]{1,0:T(8,128)(2,1)}, u32[]{:S(2)}, u32[]{:S(2)}) collective-permute-start(bf16[1536,768]{1,0:T(8,128)(2,1)} %pad_maximum_fusion.10), channel_id=1, source_target_pairs={{0,2},{2,0},{1,3},{3,1},{4,6},{6,4},{5,7},{7,5},{8,10},{10,8},{9,1... | collective-permute-start | bytes 7077896 | tf_op jit(solution)/shard_map/ppermute | solution.py:32
  199.3 212.2 %collective-permute-start.7 = (bf16[1536,768]{1,0:T(8,128)(2,1)}, bf16[1536,768]{1,0:T(8,128)(2,1)}, u32[]{:S(2)}, u32[]{:S(2)}) collective-permute-start(bf16[1536,768]{1,0:T(8,128)(2,1)} %pad_maximum_fusion.7), channel_id=1, source_target_pairs={{0,4},{4,0},{1,5},{5,1},{2,6},{6,2},{3,7},{7,3},{8,12},{12,8},{9,1... | collective-permute-start | bytes 7077896 | tf_op jit(solution)/shard_map/ppermute | solution.py:32
  245.1 171.8 %collective-permute-start.3 = (bf16[1536,768]{1,0:T(8,128)(2,1)}, bf16[1536,768]{1,0:T(8,128)(2,1)}, u32[]{:S(2)}, u32[]{:S(2)}) collective-permute-start(bf16[1536,768]{1,0:T(8,128)(2,1)} %pad_maximum_fusion.6), channel_id=1, source_target_pairs={{0,2},{2,0},{1,3},{3,1},{4,6},{6,4},{5,7},{7,5},{8,10},{10,8},{9,1... | collective-permute-start | bytes 7077896 | tf_op jit(solution)/shard_map/ppermute | solution.py:32
  247.7 1084.9 %reduce-scatter.5.cloned.1.call-start = ((), (), s32[]{:S(2)}) async-start(), calls=%async_computation.5 | async-start | bytes 20054016 | tf_op jit(solution)/shard_map/reduce_scatter | solution.py:82
  658.1 703.6 %reduce-scatter.3.cloned.1.call-start = ((), (), s32[]{:S(2)}) async-start(), calls=%async_computation.4 | async-start | bytes 20054016 | tf_op jit(solution)/shard_map/reduce_scatter | solution.py:82
  710.0 42.7 %collective-permute-start.32 = (bf16[128,1536]{1,0:T(8,128)(2,1)}, bf16[128,1536]{1,0:T(8,128)(2,1)S(1)}, u32[]{:S(2)}, u32[]{:S(2)}) collective-permute-start(bf16[128,1536]{1,0:T(8,128)(2,1)} %slice.931), channel_id=1, source_target_pairs={{0,1},{1,0},{2,3},{3,2},{4,5},{5,4},{6,7},{7,6},{8,9},{9,8},{10,11... | collective-permute-start | bytes 1179656 | tf_op jit(solution)/shard_map/ppermute | solution.py:27
  751.2 105.5 %collective-permute-start.48 = (bf16[1536,768]{0,1:T(8,128)(2,1)}, bf16[1536,768]{0,1:T(8,128)(2,1)}, u32[]{:S(2)}, u32[]{:S(2)}) collective-permute-start(bf16[1536,768]{0,1:T(8,128)(2,1)} %broadcast_select_fusion), channel_id=1, source_target_pairs={{0,2},{2,0},{1,3},{3,1},{4,6},{6,4},{5,7},{7,5},{8,10},{10,8},{9,1... | collective-permute-start | bytes 7077896 | tf_op jit(solution)/shard_map/ppermute | solution.py:32
  754.2 48.3 %collective-permute-start.33 = (bf16[128,1536]{1,0:T(8,128)(2,1)}, bf16[128,1536]{1,0:T(8,128)(2,1)S(1)}, u32[]{:S(2)}, u32[]{:S(2)}) collective-permute-start(bf16[128,1536]{1,0:T(8,128)(2,1)} %get-tuple-element.189), channel_id=1, source_target_pairs={{0,1},{1,0},{2,3},{3,2},{4,5},{5,4},{6,7},{7,6},{8,9},{9,8},{10,11... | collective-permute-start | bytes 1179656 | tf_op jit(solution)/shard_map/ppermute | solution.py:27
  814.8 41.5 %collective-permute-start.34 = (bf16[128,1536]{1,0:T(8,128)(2,1)}, bf16[128,1536]{1,0:T(8,128)(2,1)S(1)}, u32[]{:S(2)}, u32[]{:S(2)}) collective-permute-start(bf16[128,1536]{1,0:T(8,128)(2,1)} %slice.930), channel_id=1, source_target_pairs={{0,1},{1,0},{2,3},{3,2},{4,5},{5,4},{6,7},{7,6},{8,9},{9,8},{10,11... | collective-permute-start | bytes 1179656 | tf_op jit(solution)/shard_map/ppermute | solution.py:27
  855.0 70.0 %collective-permute-start.44 = (bf16[1536,768]{0,1:T(8,128)(2,1)S(1)}, bf16[1536,768]{0,1:T(8,128)(2,1)}, u32[]{:S(2)}, u32[]{:S(2)}) collective-permute-start(bf16[1536,768]{0,1:T(8,128)(2,1)S(1)} %broadcast_select_fusion.1), channel_id=1, source_target_pairs={{0,2},{2,0},{1,3},{3,1},{4,6},{6,4},{5,7},{7,5},{8,10},{10,8},{9,1... | collective-permute-start | bytes 7077896 | tf_op jit(solution)/shard_map/ppermute | solution.py:32
  861.1 36.9 %collective-permute-start.49 = (bf16[768,768]{0,1:T(8,128)(2,1)}, bf16[768,768]{0,1:T(8,128)(2,1)}, u32[]{:S(2)}, u32[]{:S(2)}) collective-permute-start(bf16[768,768]{0,1:T(8,128)(2,1)} %constant_dynamic-slice_fusion.8), channel_id=1, source_target_pairs={{0,4},{4,0},{1,5},{5,1},{2,6},{6,2},{3,7},{7,3},{8,12},{12,8},{9,1... | collective-permute-start | bytes 3538952 | tf_op jit(solution)/shard_map/ppermute | solution.py:32
  898.1 41.2 %collective-permute-start.29 = (bf16[512,1536]{1,0:T(8,128)(2,1)}, bf16[512,1536]{1,0:T(8,128)(2,1)S(1)}, u32[]{:S(2)}, u32[]{:S(2)}) collective-permute-start(bf16[512,1536]{1,0:T(8,128)(2,1)} %slice.926), channel_id=1, source_target_pairs={{0,1},{1,0},{2,3},{3,2},{4,5},{5,4},{6,7},{7,6},{8,9},{9,8},{10,11... | collective-permute-start | bytes 4718600 | tf_op jit(solution)/shard_map/ppermute | solution.py:27
  899.9 38.9 %collective-permute-start.50 = (bf16[384,768]{0,1:T(8,128)(2,1)S(1)}, bf16[384,768]{0,1:T(8,128)(2,1)S(1)}, u32[]{:S(2)}, u32[]{:S(2)}) collective-permute-start(bf16[384,768]{0,1:T(8,128)(2,1)S(1)} %constant_dynamic-slice_fusion.7), channel_id=1, source_target_pairs={{0,16},{8,24},{16,0},{24,8},{1,17},{9,25},{17,1},{25,9},{2,18},{10... | collective-permute-start | bytes 1769480 | tf_op jit(solution)/shard_map/ppermute | solution.py:32
  945.8 68.9 %collective-permute-start.30 = (bf16[512,1536]{1,0:T(8,128)(2,1)}, bf16[512,1536]{1,0:T(8,128)(2,1)}, u32[]{:S(2)}, u32[]{:S(2)}) collective-permute-start(bf16[512,1536]{1,0:T(8,128)(2,1)} %get-tuple-element.187), channel_id=1, source_target_pairs={{0,1},{1,0},{2,3},{3,2},{4,5},{5,4},{6,7},{7,6},{8,9},{9,8},{10,11... | collective-permute-start | bytes 4718600 | tf_op jit(solution)/shard_map/ppermute | solution.py:27
  957.0 54.7 %collective-permute-start.46 = (bf16[384,768]{0,1:T(8,128)(2,1)}, bf16[384,768]{0,1:T(8,128)(2,1)}, u32[]{:S(2)}, u32[]{:S(2)}) collective-permute-start(bf16[384,768]{0,1:T(8,128)(2,1)} %constant_dynamic-slice_fusion.10), channel_id=1, source_target_pairs={{0,16},{8,24},{16,0},{24,8},{1,17},{9,25},{17,1},{25,9},{2,18},{10... | collective-permute-start | bytes 1769480 | tf_op jit(solution)/shard_map/ppermute | solution.py:32
  1014.7 134.7 %collective-permute-start.47 = (bf16[192,768]{0,1:T(8,128)(2,1)}, bf16[192,768]{0,1:T(8,128)(2,1)}, u32[]{:S(2)}, u32[]{:S(2)}) collective-permute-start(bf16[192,768]{0,1:T(8,128)(2,1)} %constant_dynamic-slice_fusion.9), channel_id=1, source_target_pairs={{0,8},{8,0},{16,24},{24,16},{1,9},{9,1},{17,25},{25,17},{2,10},{10... | collective-permute-start | bytes 884744 | tf_op jit(solution)/shard_map/ppermute | solution.py:32
  1126.2 85.0 %collective-permute-start.40 = (bf16[1536,768]{0,1:T(8,128)(2,1)}, bf16[1536,768]{0,1:T(8,128)(2,1)}, u32[]{:S(2)}, u32[]{:S(2)}) collective-permute-start(bf16[1536,768]{0,1:T(8,128)(2,1)} %broadcast_select_fusion.2), channel_id=1, source_target_pairs={{0,2},{2,0},{1,3},{3,1},{4,6},{6,4},{5,7},{7,5},{8,10},{10,8},{9,1... | collective-permute-start | bytes 7077896 | tf_op jit(solution)/shard_map/ppermute | solution.py:32
  1144.8 70.5 %collective-permute-start.35 = (bf16[3072,192]{0,1:T(8,128)(2,1)}, bf16[3072,192]{0,1:T(8,128)(2,1)}, u32[]{:S(2)}, u32[]{:S(2)}) collective-permute-start(bf16[3072,192]{0,1:T(8,128)(2,1)} %copy.365), channel_id=1, source_target_pairs={{0,1},{1,0},{2,3},{3,2},{4,5},{5,4},{6,7},{7,6},{8,9},{9,8},{10,11... | collective-permute-start | bytes 3538952 | tf_op jit(solution)/shard_map/ppermute | solution.py:32
  1160.4 65.8 %collective-permute-start.54 = (f32[192,7]{1,0:T(8,128)}, f32[192,7]{1,0:T(8,128)}, u32[]{:S(2)}, u32[]{:S(2)}) collective-permute-start(f32[192,7]{1,0:T(8,128)} %constant_dynamic-slice_fusion.2), channel_id=1, source_target_pairs={{0,8},{8,0},{16,24},{24,16},{1,9},{9,1},{17,25},{25,17},{2,10},{10... | collective-permute-start | bytes 16136 | tf_op jit(solution)/shard_map/ppermute | solution.py:32
  1223.6 40.7 %collective-permute-start.41 = (bf16[768,768]{0,1:T(8,128)(2,1)}, bf16[768,768]{0,1:T(8,128)(2,1)}, u32[]{:S(2)}, u32[]{:S(2)}) collective-permute-start(bf16[768,768]{0,1:T(8,128)(2,1)} %constant_dynamic-slice_fusion.14), channel_id=1, source_target_pairs={{0,4},{4,0},{1,5},{5,1},{2,6},{6,2},{3,7},{7,3},{8,12},{12,8},{9,1... | collective-permute-start | bytes 3538952 | tf_op jit(solution)/shard_map/ppermute | solution.py:32
  1227.1 50.5 %collective-permute-start.55 = (f32[96,7]{1,0:T(8,128)S(1)}, f32[96,7]{1,0:T(8,128)S(1)}, u32[]{:S(2)}, u32[]{:S(2)}) collective-permute-start(f32[96,7]{1,0:T(8,128)S(1)} %constant_dynamic-slice_fusion.1), channel_id=1, source_target_pairs={{0,2},{2,0},{1,3},{3,1},{4,6},{6,4},{5,7},{7,5},{8,10},{10,8},{9,1... | collective-permute-start | bytes 8072 | tf_op jit(solution)/shard_map/ppermute | solution.py:32
  1266.0 49.4 %collective-permute-start.42 = (bf16[384,768]{0,1:T(8,128)(2,1)S(1)}, bf16[384,768]{0,1:T(8,128)(2,1)S(1)}, u32[]{:S(2)}, u32[]{:S(2)}) collective-permute-start(bf16[384,768]{0,1:T(8,128)(2,1)S(1)} %constant_dynamic-slice_fusion.13), channel_id=1, source_target_pairs={{0,16},{8,24},{16,0},{24,8},{1,17},{9,25},{17,1},{25,9},{2,18},{10... | collective-permute-start | bytes 1769480 | tf_op jit(solution)/shard_map/ppermute | solution.py:32
  1275.2 40.0 %collective-permute-start.38 = (bf16[384,192]{1,0:T(8,128)(2,1)S(1)}, bf16[384,192]{1,0:T(8,128)(2,1)S(1)}, u32[]{:S(2)}, u32[]{:S(2)}) collective-permute-start(bf16[384,192]{1,0:T(8,128)(2,1)S(1)} %constant_dynamic-slice_fusion.16), channel_id=1, source_target_pairs={{0,16},{8,24},{16,0},{24,8},{1,17},{9,25},{17,1},{25,9},{2,18},{10... | collective-permute-start | bytes 442376 | tf_op jit(solution)/shard_map/ppermute | solution.py:32
  1277.7 40.1 %collective-permute-start.56 = (f32[48,7]{1,0:T(8,128)S(1)}, f32[48,7]{1,0:T(8,128)S(1)}, u32[]{:S(2)}, u32[]{:S(2)}) collective-permute-start(f32[48,7]{1,0:T(8,128)S(1)} %constant_dynamic-slice_fusion), channel_id=1, source_target_pairs={{0,1},{1,0},{2,3},{3,2},{4,5},{5,4},{6,7},{7,6},{8,9},{9,8},{10,11... | collective-permute-start | bytes 4040 | tf_op jit(solution)/shard_map/ppermute | solution.py:32
  (373 other events, 3085.8 us)
Sparse Core Ops, SparseCore 0:
  14.7 367.8 all-gather.3
  385.3 209.2 all-gather.5
  658.3 354.7 reduce-scatter.4
  1018.7 343.0 reduce-scatter.2

commit v5 on v4

--- a/solution.py
+++ b/solution.py
@@ -352,20 +352,21 @@
             jnp.pad(feed_out[layer].T.astype(half), spare),
         ]
 
+    third = hidden_rows + spare[1][1]
+
     def thirds(blocks, start):
-        third = hidden_rows + spare[1][1]
         return [
             [b[:, start + k * third : start + (k + 1) * third] for b in blocks] for k in range(3)
         ]
 
-    first = gather_unit(jnp.concatenate(feed_units(0) + [table_pair], axis=1))
+    first = plain(jnp.concatenate(feed_units(0) + [table_pair], axis=1))
+    attn = [plain(jnp.concatenate(attention_unit(layer), axis=1)) for layer in range(3)]
+    attn, gains = lax.optimization_barrier((attn, gains))
+    first = gather_unit(first)
     second = halves(gather_unit(jnp.concatenate(feed_units(1), axis=1)))
-    attn = [
-        gather_pairs(jnp.concatenate(attention_unit(layer), axis=1), row_first)
-        for layer, row_first in enumerate((False, True, False))
-    ]
+    attn = [gather_pairs(a, row_first) for a, row_first in zip(attn, (False, True, False))]
     fills = (jnp.minimum(jnp.sum(target_lengths), 0), jnp.minimum(jnp.sum(source_lengths), 0))
-    blanks = [jnp.full((2 * b.shape[0], b.shape[1]), f.astype(half)) for b, f in zip(second, fills)]
+    blanks = [jnp.full((first.shape[0], 2 * third), f.astype(half)) for f in fills]
     first, attn, blanks = lax.optimization_barrier((first, attn, blanks))
     first = halves(first)
     edge = first[0].shape[1] - 2 * vocab_rows
@@ -423,7 +424,8 @@
 
     d_tgt, gain_six = norm_back(tgt_top, gains[6], product_right(d_logits, w_head))
     *feed_one, d_in = expand_back(tgt_norm_c, *feed[1], keep_tgt_c, collect(d_tgt.astype(half)))
-    feed_one = scatter_unit(feed_one, blanks[1])
+    down_one = scatter_pairs(feed_one[2])
+    feed_one = scatter_unit(feed_one[:2], blanks[1])
     d_more, gain_five = norm_back(tgt_cross, gains[5], fold(d_in))
     d_tgt = d_tgt + d_more
     attn_two, d_query, d_keys = cross_attention_back(
@@ -442,7 +444,8 @@
 
     d_src, gain_two = norm_back(src_top, gains[2], d_encoded)
     *feed_zero, d_in = expand_back(src_norm_b, *feed[0], keep_src_b, collect(d_src.astype(half)))
-    feed_zero = scatter_unit(feed_zero, blanks[0])
+    down_zero = scatter_pairs(feed_zero[2])
+    feed_zero = scatter_unit(feed_zero[:2], blanks[0])
     d_more, gain_one = norm_back(src_mid, gains[1], fold(d_in))
     d_src = d_src + d_more
     attn_zero, d_in = self_attention_back(
@@ -468,16 +471,14 @@
 
     width = attention_out.shape[1]
     attn_grads = [attn_zero, attn_one, attn_two]
-    units = [pair_grad, *attn_grads, feed_zero, feed_one]
+    units = [pair_grad, *attn_grads, feed_zero, feed_one, down_zero, down_one]
     squares = sum(jnp.sum(g * g) for g in units) + jnp.sum(g_gains * g_gains)
-    feed_grads = [thirds([g], 0) for g in (feed_zero, feed_one)]
     squares, loss = total_over(jnp.stack([squares, own_loss]), everywhere)
     attn_in = [g[:, : 3 * width].reshape(-1, 3, width) for g in attn_grads]
     gates_uppers = [
-        jnp.stack([gate[0][:, :hidden_rows], upper[0][:, :hidden_rows]], axis=1)
-        for gate, upper, _ in feed_grads
+        g.reshape(-1, 2, third)[..., :hidden_rows] for g in (feed_zero, feed_one)
     ]
-    downs = [down[0][:, :hidden_rows].T for _, _, down in feed_grads]
+    downs = [g[:, :hidden_rows].T for g in (down_zero, down_one)]
     grads = (
         plain(pair_grad[:, :vocab_rows].T),
         plain(pair_grad[:, vocab_rows:]),

time: 1450 us -> 1490 us (1.028)
  waiting for transfers between devices: 462 us -> 626 us
  blocking collectives: 154 us -> 45.3 us
    ppermute x40 -> x48, waiting for transfers between devices: 422 us -> 598 us  [flip(): return lax.ppermute(part, axis, [(i, i ^ bit) for i in range(size)])]
    all_gather x1, blocking collectives: 154 us -> 45.3 us  [on_device(): gain_part = lax.all_gather(gain_part, everywhere)]
    reduce_scatter x2, waiting for transfers between devices: 23.4 us -> 0.04 us  [scatter_unit(): lax.psum_scatter(plain(whole), ('y', 'near', 'far'), scatter_dimension=0,...]
    all_gather x2, waiting for transfers between devices: 6.51 us -> 25.6 us  [gather_unit(): return lax.all_gather(plain(part), ('y', 'near', 'far'), axis=0, tiled=True)]
    ppermute x40 -> x48, starting transfers between devices: 58.5 us -> 49.4 us  [flip(): return lax.ppermute(part, axis, [(i, i ^ bit) for i in range(size)])]
    unnamed x687 -> x662, local copies, waits for them, and re-layouts: 52.7 us -> 55.1 us
  transfers between devices with their start and end apart: 66 -> 74, of which waited for: 30 -> 35; matrix products, arithmetic and copies ran while one was open for 41% -> 41% of each run, Pallas kernels for 0% -> 0%
where the time goes in v5:
time: 1490 us; the launch traced here: 1480 us
  waiting for transfers between devices  626 us (42%)
  matrix products  342 us (23%)
  other arithmetic  207 us (14%)
  local copies, waits for them, and re-layouts  177 us (12%)
  starting transfers between devices  55.8 us (4%)
  blocking collectives  45.3 us (3%)
  between operations  29.3 us (2%)
    ppermute x48, waiting for transfers between devices, flip(): return lax.ppermute(part, axis, [(i, i ^ bit) for i in range(size)])  598 us
    dot_general x29, matrix products, product_left(): lax.dot_general(left, right, (((0,), (0,)), ((), ())), preferred_element_...  100 us
    dot_general x27, matrix products, product(): return jnp.dot(left, right, preferred_element_type=jnp.float32)  99.4 us
    dot_general x29, matrix products, product_right(): lax.dot_general(left, right, (((1,), (1,)), ((), ())), preferred_element_...  81.1 us
    unnamed x662, local copies, waits for them, and re-layouts  55.1 us
    ppermute x48, starting transfers between devices, flip(): return lax.ppermute(part, axis, [(i, i ^ bit) for i in range(size)])  49.4 us
    all_gather x1, blocking collectives, on_device(): gain_part = lax.all_gather(gain_part, everywhere)  45.3 us
  transfers between devices with their start and end apart: 74, of which 35 were waited for; matrix products, arithmetic and copies ran while one was open for 41% of the time, Pallas kernels for 0%

profile of v5, /device:TPU:0, one launch (start us, length us, event | category | flops | bytes accessed | tf_op | source)
XLA Modules:
  0.0 1482.1 jit_solution(16092234764376902002)
XLA Ops:
  17.7 45.3 %all-gather = f32[256,48]{1,0:T(8,128)S(1)} all-gather(f32[8,48]{1,0:T(8,128)S(1)} %concatenate.170), channel_id=2, replica_groups=mesh['far'=4,'near'=2,'y'=2,'c'=2] {'near','far','y','c'}, dimensions={0}, use_global_device_ids=true | all-gather | bytes 50688 | tf_op jit(solution)/shard_map/all_gather | solution.py:336
  66.2 26.8 %collective-permute-done.4 = bf16[192,768]{1,0:T(8,128)(2,1)S(1)} collective-permute-done((bf16[192,768]{1,0:T(8,128)(2,1)S(1)}, bf16[192,768]{1,0:T(8,128)(2,1)S(1)}, u32[]{:S(2)}, u32[]{:S(2)}) %collective-permute-start.4) | collective-permute-done | bytes 294944 | tf_op jit(solution)/shard_map/ppermute | solution.py:32
  93.2 15.1 %collective-permute-done.8 = bf16[192,768]{1,0:T(8,128)(2,1)S(1)} collective-permute-done((bf16[192,768]{1,0:T(8,128)(2,1)S(1)}, bf16[192,768]{1,0:T(8,128)(2,1)S(1)}, u32[]{:S(2)}, u32[]{:S(2)}) %collective-permute-start.8) | collective-permute-done | bytes 294944 | tf_op jit(solution)/shard_map/ppermute | solution.py:32
  108.5 16.7 %collective-permute-done = bf16[192,768]{1,0:T(8,128)(2,1)S(1)} collective-permute-done((bf16[192,768]{1,0:T(8,128)(2,1)S(1)}, bf16[192,768]{1,0:T(8,128)(2,1)S(1)}, u32[]{:S(2)}, u32[]{:S(2)}) %collective-permute-start) | collective-permute-done | bytes 294944 | tf_op jit(solution)/shard_map/ppermute | solution.py:32
  126.3 52.6 %collective-permute-done.5 = bf16[384,768]{1,0:T(8,128)(2,1)S(1)} collective-permute-done((bf16[384,768]{1,0:T(8,128)(2,1)S(1)}, bf16[384,768]{1,0:T(8,128)(2,1)S(1)}, u32[]{:S(2)}, u32[]{:S(2)}) %collective-permute-start.5) | collective-permute-done | bytes 589856 | tf_op jit(solution)/shard_map/ppermute | solution.py:32
  180.3 19.8 %collective-permute-done.9 = bf16[384,768]{1,0:T(8,128)(2,1)S(1)} collective-permute-done((bf16[384,768]{1,0:T(8,128)(2,1)S(1)}, bf16[384,768]{1,0:T(8,128)(2,1)S(1)}, u32[]{:S(2)}, u32[]{:S(2)}) %collective-permute-start.9) | collective-permute-done | bytes 589856 | tf_op jit(solution)/shard_map/ppermute | solution.py:32
  202.9 45.4 %collective-permute-done.1 = bf16[384,768]{1,0:T(8,128)(2,1)} collective-permute-done((bf16[384,768]{1,0:T(8,128)(2,1)}, bf16[384,768]{1,0:T(8,128)(2,1)}, u32[]{:S(2)}, u32[]{:S(2)}) %collective-permute-start.1) | collective-permute-done | bytes 589856 | tf_op jit(solution)/shard_map/ppermute | solution.py:32
  259.4 46.9 %collective-permute-done.2 = bf16[768,768]{1,0:T(8,128)(2,1)S(1)} collective-permute-done((bf16[768,768]{1,0:T(8,128)(2,1)S(1)}, bf16[768,768]{1,0:T(8,128)(2,1)S(1)}, u32[]{:S(2)}, u32[]{:S(2)}) %collective-permute-start.2) | collective-permute-done | bytes 1179680 | tf_op jit(solution)/shard_map/ppermute | solution.py:32
  311.6 51.5 %collective-permute-done.7 = bf16[1536,768]{1,0:T(8,128)(2,1)} collective-permute-done((bf16[1536,768]{1,0:T(8,128)(2,1)}, bf16[1536,768]{1,0:T(8,128)(2,1)}, u32[]{:S(2)}, u32[]{:S(2)}) %collective-permute-start.7) | collective-permute-done | bytes 2359328 | tf_op jit(solution)/shard_map/ppermute | solution.py:32
  373.9 8.9 collective-permute-done.3
  467.4 8.2 fusion.71
  480.6 8.9 multiply_convert_fusion.5
  496.5 8.7 multiply_convert_fusion.4
  560.0 25.6 %all-gather.6.cloned.1.call-done = bf16[3072,3072]{1,0:T(8,128)(2,1)} async-done(((bf16[192,3072]{1,0:T(8,128)(2,1)}), bf16[3072,3072]{1,0:T(8,128)(2,1)}) %all-gather.6.cloned.1.call-update) | async-done | bytes 18874384 | tf_op jit(solution)/shard_map/all_gather | solution.py:44
  764.3 25.0 %collective-permute-done.48 = bf16[1536,768]{0,1:T(8,128)(2,1)} collective-permute-done((bf16[1536,768]{0,1:T(8,128)(2,1)}, bf16[1536,768]{0,1:T(8,128)(2,1)}, u32[]{:S(2)}, u32[]{:S(2)}) %collective-permute-start.48) | collective-permute-done | bytes 2359328 | tf_op jit(solution)/shard_map/ppermute | solution.py:32
  801.0 61.0 %collective-permute-done.44 = bf16[1536,768]{0,1:T(8,128)(2,1)S(1)} collective-permute-done((bf16[1536,768]{0,1:T(8,128)(2,1)S(1)}, bf16[1536,768]{0,1:T(8,128)(2,1)S(1)}, u32[]{:S(2)}, u32[]{:S(2)}) %collective-permute-start.44) | collective-permute-done | bytes 2359328 | tf_op jit(solution)/shard_map/ppermute | solution.py:32
  866.1 9.4 multiply_convert_fusion.3
  890.0 9.7 multiply_convert_fusion.2
  899.7 8.4 fusion.69
  908.2 9.7 add_add_fusion
  927.4 8.1 broadcast_select_fusion.1
  965.3 58.1 %collective-permute-done.50 = bf16[384,768]{0,1:T(8,128)(2,1)} collective-permute-done((bf16[384,768]{0,1:T(8,128)(2,1)}, bf16[384,768]{0,1:T(8,128)(2,1)}, u32[]{:S(2)}, u32[]{:S(2)}) %collective-permute-start.50) | collective-permute-done | bytes 589856 | tf_op jit(solution)/shard_map/ppermute | solution.py:32
  1035.9 24.7 %collective-permute-done.51 = bf16[192,768]{0,1:T(8,128)(2,1)S(1)} collective-permute-done((bf16[192,768]{0,1:T(8,128)(2,1)S(1)}, bf16[192,768]{0,1:T(8,128)(2,1)S(1)}, u32[]{:S(2)}, u32[]{:S(2)}) %collective-permute-start.51) | collective-permute-done | bytes 294944 | tf_op jit(solution)/shard_map/ppermute | solution.py:32
  1069.8 16.5 %collective-permute-done.58 = bf16[384,1024]{1,0:T(8,128)(2,1)S(1)} collective-permute-done((bf16[384,1024]{1,0:T(8,128)(2,1)S(1)}, bf16[384,1024]{1,0:T(8,128)(2,1)S(1)}, u32[]{:S(2)}, u32[]{:S(2)}) %collective-permute-start.58) | collective-permute-done | bytes 786464 | tf_op jit(solution)/shard_map/ppermute | solution.py:32
  1092.3 16.0 %collective-permute-done.46 = bf16[384,768]{0,1:T(8,128)(2,1)} collective-permute-done((bf16[384,768]{0,1:T(8,128)(2,1)}, bf16[384,768]{0,1:T(8,128)(2,1)}, u32[]{:S(2)}, u32[]{:S(2)}) %collective-permute-start.46) | collective-permute-done | bytes 589856 | tf_op jit(solution)/shard_map/ppermute | solution.py:32
  1137.0 10.9 multiply_reduce_fusion
  1149.7 10.8 multiply_convert_fusion
  1175.7 9.1 multiply_convert_fusion.1
  1273.4 32.6 %collective-permute-done.61 = f32[384,7]{1,0:T(8,128)S(1)} collective-permute-done((f32[384,7]{1,0:T(8,128)S(1)}, f32[384,7]{1,0:T(8,128)S(1)}, u32[]{:S(2)}, u32[]{:S(2)}) %collective-permute-start.61) | collective-permute-done | bytes 10784 | tf_op jit(solution)/shard_map/ppermute | solution.py:32
  1336.3 9.3 collective-permute-done.36
  1362.2 26.8 %collective-permute-done.38 = bf16[384,192]{1,0:T(8,128)(2,1)S(1)} collective-permute-done((bf16[384,192]{1,0:T(8,128)(2,1)S(1)}, bf16[384,192]{1,0:T(8,128)(2,1)S(1)}, u32[]{:S(2)}, u32[]{:S(2)}) %collective-permute-start.38) | collective-permute-done | bytes 147488 | tf_op jit(solution)/shard_map/ppermute | solution.py:32
  1455.8 12.2 multiply_subtract_fusion
  (1185 shorter events, 714.0 us)
Async XLA Ops:
  7.2 380.8 %all-gather.4.cloned.1.call-start = ((), (), s32[]{:S(2)}) async-start(), calls=%async_computation.2 | async-start | bytes 21725184 | tf_op jit(solution)/shard_map/all_gather | solution.py:44
  14.6 571.0 %all-gather.6.cloned.1.call-start = ((), (), s32[]{:S(2)}) async-start(), calls=%async_computation.3 | async-start | bytes 20054016 | tf_op jit(solution)/shard_map/all_gather | solution.py:44
  64.1 44.2 %collective-permute-start.8 = (bf16[192,768]{1,0:T(8,128)(2,1)S(1)}, bf16[192,768]{1,0:T(8,128)(2,1)S(1)}, u32[]{:S(2)}, u32[]{:S(2)}) collective-permute-start(bf16[192,768]{1,0:T(8,128)(2,1)S(1)} %pad_maximum_fusion.45), channel_id=1, source_target_pairs={{0,8},{8,0},{16,24},{24,16},{1,9},{9,1},{17,25},{25,17},{2,10},{10... | collective-permute-start | bytes 884744 | tf_op jit(solution)/shard_map/ppermute | solution.py:32
  66.1 59.1 %collective-permute-start = (bf16[192,768]{1,0:T(8,128)(2,1)S(1)}, bf16[192,768]{1,0:T(8,128)(2,1)S(1)}, u32[]{:S(2)}, u32[]{:S(2)}) collective-permute-start(bf16[192,768]{1,0:T(8,128)(2,1)S(1)} %get-tuple-element.36), channel_id=1, source_target_pairs={{0,8},{8,0},{16,24},{24,16},{1,9},{9,1},{17,25},{25,17},{2,10},{10... | collective-permute-start | bytes 884744 | tf_op jit(solution)/shard_map/ppermute | solution.py:32
  93.1 85.7 %collective-permute-start.5 = (bf16[384,768]{1,0:T(8,128)(2,1)S(1)}, bf16[384,768]{1,0:T(8,128)(2,1)S(1)}, u32[]{:S(2)}, u32[]{:S(2)}) collective-permute-start(bf16[384,768]{1,0:T(8,128)(2,1)S(1)} %pad_maximum_fusion.33), channel_id=1, source_target_pairs={{0,16},{8,24},{16,0},{24,8},{1,17},{9,25},{17,1},{25,9},{2,18},{10... | collective-permute-start | bytes 1769480 | tf_op jit(solution)/shard_map/ppermute | solution.py:32
  108.4 91.7 %collective-permute-start.9 = (bf16[384,768]{1,0:T(8,128)(2,1)S(1)}, bf16[384,768]{1,0:T(8,128)(2,1)S(1)}, u32[]{:S(2)}, u32[]{:S(2)}) collective-permute-start(bf16[384,768]{1,0:T(8,128)(2,1)S(1)} %pad_maximum_fusion.34), channel_id=1, source_target_pairs={{0,16},{8,24},{16,0},{24,8},{1,17},{9,25},{17,1},{25,9},{2,18},{10... | collective-permute-start | bytes 1769480 | tf_op jit(solution)/shard_map/ppermute | solution.py:32
  126.2 122.0 %collective-permute-start.1 = (bf16[384,768]{1,0:T(8,128)(2,1)}, bf16[384,768]{1,0:T(8,128)(2,1)}, u32[]{:S(2)}, u32[]{:S(2)}) collective-permute-start(bf16[384,768]{1,0:T(8,128)(2,1)} %pad_maximum_fusion.32), channel_id=1, source_target_pairs={{0,16},{8,24},{16,0},{24,8},{1,17},{9,25},{17,1},{25,9},{2,18},{10... | collective-permute-start | bytes 1769480 | tf_op jit(solution)/shard_map/ppermute | solution.py:32
  180.3 70.9 %collective-permute-start.6 = (bf16[768,768]{1,0:T(8,128)(2,1)}, bf16[768,768]{1,0:T(8,128)(2,1)S(1)}, u32[]{:S(2)}, u32[]{:S(2)}) collective-permute-start(bf16[768,768]{1,0:T(8,128)(2,1)} %pad_maximum_fusion.17), channel_id=1, source_target_pairs={{0,2},{2,0},{1,3},{3,1},{4,6},{6,4},{5,7},{7,5},{8,10},{10,8},{9,1... | collective-permute-start | bytes 3538952 | tf_op jit(solution)/shard_map/ppermute | solution.py:32
  201.4 54.4 %collective-permute-start.10 = (bf16[768,768]{1,0:T(8,128)(2,1)}, bf16[768,768]{1,0:T(8,128)(2,1)}, u32[]{:S(2)}, u32[]{:S(2)}) collective-permute-start(bf16[768,768]{1,0:T(8,128)(2,1)} %pad_maximum_fusion.18), channel_id=1, source_target_pairs={{0,4},{4,0},{1,5},{5,1},{2,6},{6,2},{3,7},{7,3},{8,12},{12,8},{9,1... | collective-permute-start | bytes 3538952 | tf_op jit(solution)/shard_map/ppermute | solution.py:32
  249.8 56.5 %collective-permute-start.2 = (bf16[768,768]{1,0:T(8,128)(2,1)S(1)}, bf16[768,768]{1,0:T(8,128)(2,1)S(1)}, u32[]{:S(2)}, u32[]{:S(2)}) collective-permute-start(bf16[768,768]{1,0:T(8,128)(2,1)S(1)} %pad_maximum_fusion.16), channel_id=1, source_target_pairs={{0,4},{4,0},{1,5},{5,1},{2,6},{6,2},{3,7},{7,3},{8,12},{12,8},{9,1... | collective-permute-start | bytes 3538952 | tf_op jit(solution)/shard_map/ppermute | solution.py:32
  253.0 110.1 %collective-permute-start.7 = (bf16[1536,768]{1,0:T(8,128)(2,1)}, bf16[1536,768]{1,0:T(8,128)(2,1)}, u32[]{:S(2)}, u32[]{:S(2)}) collective-permute-start(bf16[1536,768]{1,0:T(8,128)(2,1)} %pad_maximum_fusion.6), channel_id=1, source_target_pairs={{0,4},{4,0},{1,5},{5,1},{2,6},{6,2},{3,7},{7,3},{8,12},{12,8},{9,1... | collective-permute-start | bytes 7077896 | tf_op jit(solution)/shard_map/ppermute | solution.py:32
  259.4 106.9 %collective-permute-start.11 = (bf16[1536,768]{1,0:T(8,128)(2,1)}, bf16[1536,768]{1,0:T(8,128)(2,1)}, u32[]{:S(2)}, u32[]{:S(2)}) collective-permute-start(bf16[1536,768]{1,0:T(8,128)(2,1)} %pad_maximum_fusion.9), channel_id=1, source_target_pairs={{0,2},{2,0},{1,3},{3,1},{4,6},{6,4},{5,7},{7,5},{8,10},{10,8},{9,1... | collective-permute-start | bytes 7077896 | tf_op jit(solution)/shard_map/ppermute | solution.py:32
  308.4 74.4 %collective-permute-start.3 = (bf16[1536,768]{1,0:T(8,128)(2,1)}, bf16[1536,768]{1,0:T(8,128)(2,1)}, u32[]{:S(2)}, u32[]{:S(2)}) collective-permute-start(bf16[1536,768]{1,0:T(8,128)(2,1)} %pad_maximum_fusion.5), channel_id=1, source_target_pairs={{0,2},{2,0},{1,3},{3,1},{4,6},{6,4},{5,7},{7,5},{8,10},{10,8},{9,1... | collective-permute-start | bytes 7077896 | tf_op jit(solution)/shard_map/ppermute | solution.py:32
  309.6 1097.0 %reduce-scatter.5.cloned.1.call-start = ((), (), s32[]{:S(2)}) async-start(), calls=%async_computation.5 | async-start | bytes 13369344 | tf_op jit(solution)/shard_map/reduce_scatter | solution.py:82
  623.0 171.6 %collective-permute-start.56 = (bf16[1536,1024]{1,0:T(8,128)(2,1)}, bf16[1536,1024]{1,0:T(8,128)(2,1)}, u32[]{:S(2)}, u32[]{:S(2)}) collective-permute-start(bf16[1536,1024]{1,0:T(8,128)(2,1)} %get-tuple-element.346), channel_id=1, source_target_pairs={{0,2},{2,0},{1,3},{3,1},{4,6},{6,4},{5,7},{7,5},{8,10},{10,8},{9,1... | collective-permute-start | bytes 9437192 | tf_op jit(solution)/shard_map/ppermute | solution.py:32
  642.4 768.3 %reduce-scatter.3.cloned.1.call-start = ((), (), s32[]{:S(2)}) async-start(), calls=%async_computation.4 | async-start | bytes 13369344 | tf_op jit(solution)/shard_map/reduce_scatter | solution.py:82
  666.7 90.2 %collective-permute-start.27 = (bf16[512,1536]{1,0:T(8,128)(2,1)}, bf16[512,1536]{1,0:T(8,128)(2,1)}, u32[]{:S(2)}, u32[]{:S(2)}) collective-permute-start(bf16[512,1536]{1,0:T(8,128)(2,1)} %slice.888), channel_id=1, source_target_pairs={{0,1},{1,0},{2,3},{3,2},{4,5},{5,4},{6,7},{7,6},{8,9},{9,8},{10,11... | collective-permute-start | bytes 4718600 | tf_op jit(solution)/shard_map/ppermute | solution.py:27
  710.2 79.1 %collective-permute-start.48 = (bf16[1536,768]{0,1:T(8,128)(2,1)}, bf16[1536,768]{0,1:T(8,128)(2,1)}, u32[]{:S(2)}, u32[]{:S(2)}) collective-permute-start(bf16[1536,768]{0,1:T(8,128)(2,1)} %broadcast_select_fusion.2), channel_id=1, source_target_pairs={{0,2},{2,0},{1,3},{3,1},{4,6},{6,4},{5,7},{7,5},{8,10},{10,8},{9,1... | collective-permute-start | bytes 7077896 | tf_op jit(solution)/shard_map/ppermute | solution.py:32
  751.4 110.6 %collective-permute-start.44 = (bf16[1536,768]{0,1:T(8,128)(2,1)S(1)}, bf16[1536,768]{0,1:T(8,128)(2,1)S(1)}, u32[]{:S(2)}, u32[]{:S(2)}) collective-permute-start(bf16[1536,768]{0,1:T(8,128)(2,1)S(1)} %broadcast_select_fusion.3), channel_id=1, source_target_pairs={{0,2},{2,0},{1,3},{3,1},{4,6},{6,4},{5,7},{7,5},{8,10},{10,8},{9,1... | collective-permute-start | bytes 7077896 | tf_op jit(solution)/shard_map/ppermute | solution.py:32
  763.0 103.1 %collective-permute-start.28 = (bf16[512,1536]{1,0:T(8,128)(2,1)S(1)}, bf16[512,1536]{1,0:T(8,128)(2,1)}, u32[]{:S(2)}, u32[]{:S(2)}) collective-permute-start(bf16[512,1536]{1,0:T(8,128)(2,1)S(1)} %fusion.275), channel_id=1, source_target_pairs={{0,1},{1,0},{2,3},{3,2},{4,5},{5,4},{6,7},{7,6},{8,9},{9,8},{10,11... | collective-permute-start | bytes 4718600 | tf_op jit(solution)/shard_map/ppermute | solution.py:27
  793.2 157.7 %collective-permute-start.49 = (bf16[768,768]{0,1:T(8,128)(2,1)}, bf16[768,768]{0,1:T(8,128)(2,1)}, u32[]{:S(2)}, u32[]{:S(2)}) collective-permute-start(bf16[768,768]{0,1:T(8,128)(2,1)} %constant_dynamic-slice_fusion.14), channel_id=1, source_target_pairs={{0,4},{4,0},{1,5},{5,1},{2,6},{6,2},{3,7},{7,3},{8,12},{12,8},{9,1... | collective-permute-start | bytes 3538952 | tf_op jit(solution)/shard_map/ppermute | solution.py:32
  800.3 160.7 %collective-permute-start.57 = (bf16[768,1024]{1,0:T(8,128)(2,1)}, bf16[768,1024]{1,0:T(8,128)(2,1)}, u32[]{:S(2)}, u32[]{:S(2)}) collective-permute-start(bf16[768,1024]{1,0:T(8,128)(2,1)} %constant_dynamic-slice_fusion.8), channel_id=1, source_target_pairs={{0,4},{4,0},{1,5},{5,1},{2,6},{6,2},{3,7},{7,3},{8,12},{12,8},{9,1... | collective-permute-start | bytes 4718600 | tf_op jit(solution)/shard_map/ppermute | solution.py:32
  864.7 163.7 %collective-permute-start.45 = (bf16[768,768]{0,1:T(8,128)(2,1)}, bf16[768,768]{0,1:T(8,128)(2,1)}, u32[]{:S(2)}, u32[]{:S(2)}) collective-permute-start(bf16[768,768]{0,1:T(8,128)(2,1)} %constant_dynamic-slice_fusion.17), channel_id=1, source_target_pairs={{0,4},{4,0},{1,5},{5,1},{2,6},{6,2},{3,7},{7,3},{8,12},{12,8},{9,1... | collective-permute-start | bytes 3538952 | tf_op jit(solution)/shard_map/ppermute | solution.py:32
  919.3 142.2 %collective-permute-start.29 = (bf16[512,1536]{1,0:T(8,128)(2,1)}, bf16[512,1536]{1,0:T(8,128)(2,1)}, u32[]{:S(2)}, u32[]{:S(2)}) collective-permute-start(bf16[512,1536]{1,0:T(8,128)(2,1)} %slice.887), channel_id=1, source_target_pairs={{0,1},{1,0},{2,3},{3,2},{4,5},{5,4},{6,7},{7,6},{8,9},{9,8},{10,11... | collective-permute-start | bytes 4718600 | tf_op jit(solution)/shard_map/ppermute | solution.py:27
  935.5 270.3 %collective-permute-start.52 = (bf16[1536,1024]{1,0:T(8,128)(2,1)}, bf16[1536,1024]{1,0:T(8,128)(2,1)}, u32[]{:S(2)}, u32[]{:S(2)}) collective-permute-start(bf16[1536,1024]{1,0:T(8,128)(2,1)} %get-tuple-element.344), channel_id=1, source_target_pairs={{0,2},{2,0},{1,3},{3,1},{4,6},{6,4},{5,7},{7,5},{8,10},{10,8},{9,1... | collective-permute-start | bytes 9437192 | tf_op jit(solution)/shard_map/ppermute | solution.py:32
  954.5 68.8 %collective-permute-start.50 = (bf16[384,768]{0,1:T(8,128)(2,1)}, bf16[384,768]{0,1:T(8,128)(2,1)}, u32[]{:S(2)}, u32[]{:S(2)}) collective-permute-start(bf16[384,768]{0,1:T(8,128)(2,1)} %constant_dynamic-slice_fusion.13), channel_id=1, source_target_pairs={{0,16},{8,24},{16,0},{24,8},{1,17},{9,25},{17,1},{25,9},{2,18},{10... | collective-permute-start | bytes 1769480 | tf_op jit(solution)/shard_map/ppermute | solution.py:32
  963.9 122.5 %collective-permute-start.58 = (bf16[384,1024]{1,0:T(8,128)(2,1)S(1)}, bf16[384,1024]{1,0:T(8,128)(2,1)S(1)}, u32[]{:S(2)}, u32[]{:S(2)}) collective-permute-start(bf16[384,1024]{1,0:T(8,128)(2,1)S(1)} %constant_dynamic-slice_fusion.7), channel_id=1, source_target_pairs={{0,16},{8,24},{16,0},{24,8},{1,17},{9,25},{17,1},{25,9},{2,18},{10... | collective-permute-start | bytes 2359304 | tf_op jit(solution)/shard_map/ppermute | solution.py:32
  1031.9 76.5 %collective-permute-start.46 = (bf16[384,768]{0,1:T(8,128)(2,1)}, bf16[384,768]{0,1:T(8,128)(2,1)}, u32[]{:S(2)}, u32[]{:S(2)}) collective-permute-start(bf16[384,768]{0,1:T(8,128)(2,1)} %constant_dynamic-slice_fusion.16), channel_id=1, source_target_pairs={{0,16},{8,24},{16,0},{24,8},{1,17},{9,25},{17,1},{25,9},{2,18},{10... | collective-permute-start | bytes 1769480 | tf_op jit(solution)/shard_map/ppermute | solution.py:32
  1069.8 59.3 %collective-permute-start.30 = (bf16[512,1536]{1,0:T(8,128)(2,1)}, bf16[512,1536]{1,0:T(8,128)(2,1)}, u32[]{:S(2)}, u32[]{:S(2)}) collective-permute-start(bf16[512,1536]{1,0:T(8,128)(2,1)} %get-tuple-element.199), channel_id=1, source_target_pairs={{0,1},{1,0},{2,3},{3,2},{4,5},{5,4},{6,7},{7,6},{8,9},{9,8},{10,11... | collective-permute-start | bytes 4718600 | tf_op jit(solution)/shard_map/ppermute | solution.py:27
  1205.3 43.6 %collective-permute-start.31 = (bf16[512,1536]{1,0:T(8,128)(2,1)}, bf16[512,1536]{1,0:T(8,128)(2,1)}, u32[]{:S(2)}, u32[]{:S(2)}) collective-permute-start(bf16[512,1536]{1,0:T(8,128)(2,1)} %slice.886), channel_id=1, source_target_pairs={{0,1},{1,0},{2,3},{3,2},{4,5},{5,4},{6,7},{7,6},{8,9},{9,8},{10,11... | collective-permute-start | bytes 4718600 | tf_op jit(solution)/shard_map/ppermute | solution.py:27
  1248.2 69.4 %collective-permute-start.40 = (bf16[1536,768]{0,1:T(8,128)(2,1)}, bf16[1536,768]{0,1:T(8,128)(2,1)}, u32[]{:S(2)}, u32[]{:S(2)}) collective-permute-start(bf16[1536,768]{0,1:T(8,128)(2,1)} %broadcast_select_fusion.4), channel_id=1, source_target_pairs={{0,2},{2,0},{1,3},{3,1},{4,6},{6,4},{5,7},{7,5},{8,10},{10,8},{9,1... | collective-permute-start | bytes 7077896 | tf_op jit(solution)/shard_map/ppermute | solution.py:32
  1260.2 73.2 %collective-permute-start.54 = (bf16[384,1024]{1,0:T(8,128)(2,1)}, bf16[384,1024]{1,0:T(8,128)(2,1)}, u32[]{:S(2)}, u32[]{:S(2)}) collective-permute-start(bf16[384,1024]{1,0:T(8,128)(2,1)} %constant_dynamic-slice_fusion.10), channel_id=1, source_target_pairs={{0,16},{8,24},{16,0},{24,8},{1,17},{9,25},{17,1},{25,9},{2,18},{10... | collective-permute-start | bytes 2359304 | tf_op jit(solution)/shard_map/ppermute | solution.py:32
  (368 other events, 3949.6 us)
Sparse Core Ops, SparseCore 0:
  14.7 347.8 all-gather.3
  366.0 219.5 all-gather.5
  642.5 252.1 reduce-scatter.4
  961.1 277.1 reduce-scatter.2

commit v6 on v5

--- a/solution.py
+++ b/solution.py
@@ -90,6 +90,30 @@
     own = jnp.where(first, parts[0], parts[1]).astype(jnp.float32)
     sent = plain(jnp.where(first, parts[1], parts[0]))
     return own + flip(sent, axis, 1).astype(jnp.float32)
+
+
+def chosen(parts):
+    first = lax.axis_index("y") == 0
+    parts = [plain(p) for p in parts]
+    own = jnp.where(first, parts[0], parts[1])
+    return own, flip(plain(jnp.where(first, parts[1], parts[0])), "y", 1)
+
+
+def nearer(own, got):
+    whole = (own.astype(jnp.float32) + got.astype(jnp.float32)).astype(half)
+    rows = whole.shape[0] // 2
+    mine = lax.axis_index("near")
+    own = lax.dynamic_slice_in_dim(whole, mine * rows, rows)
+    return own, flip(plain(lax.dynamic_slice_in_dim(whole, (1 - mine) * rows, rows)), "near", 1)
+
+
+def farther(own, got):
+    part = own.astype(jnp.float32) + got.astype(jnp.float32)
+    bit = lax.axis_size("far") // 2
+    while bit:
+        part = split_rows(part.astype(half), "far", bit)
+        bit //= 2
+    return part
 
 
 def split_rows(whole, axis, bit):
@@ -424,33 +448,37 @@
 
     d_tgt, gain_six = norm_back(tgt_top, gains[6], product_right(d_logits, w_head))
     *feed_one, d_in = expand_back(tgt_norm_c, *feed[1], keep_tgt_c, collect(d_tgt.astype(half)))
-    down_one = scatter_pairs(feed_one[2])
+    early = [chosen(feed_one[2])]
     feed_one = scatter_unit(feed_one[:2], blanks[1])
     d_more, gain_five = norm_back(tgt_cross, gains[5], fold(d_in))
     d_tgt = d_tgt + d_more
     attn_two, d_query, d_keys = cross_attention_back(
         tgt_norm_b, encoded, attn[2], key_bias, keep_tgt_b, collect(d_tgt.astype(half))
     )
-    attn_two = scatter_pairs(attn_two)
+    early.append(chosen(attn_two))
     d_encoded = fold(d_keys)
     d_more, gain_four = norm_back(tgt_self, gains[4], fold(d_query))
     d_tgt = d_tgt + d_more
     attn_one, d_in = self_attention_back(
         tgt_norm_a, attn[1], causal, keep_tgt_a, collect(d_tgt.astype(half))
     )
-    attn_one = scatter_pairs(attn_one)
+    early.append(chosen(attn_one))
     d_more, gain_three = norm_back(tgt_embed, gains[3], fold(d_in))
     d_tgt = d_tgt + d_more
 
     d_src, gain_two = norm_back(src_top, gains[2], d_encoded)
     *feed_zero, d_in = expand_back(src_norm_b, *feed[0], keep_src_b, collect(d_src.astype(half)))
-    down_zero = scatter_pairs(feed_zero[2])
+    early, d_in = lax.optimization_barrier((early, d_in))
+    early = [nearer(*e) for e in early] + [chosen(feed_zero[2])]
     feed_zero = scatter_unit(feed_zero[:2], blanks[0])
     d_more, gain_one = norm_back(src_mid, gains[1], fold(d_in))
     d_src = d_src + d_more
     attn_zero, d_in = self_attention_back(
         src_norm_a, attn[0], key_bias, keep_src_a, collect(d_src.astype(half))
     )
+    early, attn_zero = lax.optimization_barrier((early, attn_zero))
+    down_one, attn_two, attn_one = [farther(*e) for e in early[:3]]
+    down_zero = farther(*nearer(*early[3]))
     attn_zero = scatter_pairs(attn_zero)
     d_more, gain_zero = norm_back(src_embed, gains[0], fold(d_in))
     d_src = d_src + d_more

time: 1490 us -> 1440 us (0.966)
  waiting for transfers between devices: 626 us -> 576 us
    ppermute x48, waiting for transfers between devices: 598 us -> 548 us  [flip(): return lax.ppermute(part, axis, [(i, i ^ bit) for i in range(size)])]
    convert_element_type x0 -> x12, other arithmetic: none -> 22.3 us  [the longest x8 13.4 us: farther(): part = split_rows(part.astype(half), 'far', bit)]
    unnamed x662 -> x654, local copies, waits for them, and re-layouts: 55.1 us -> 51.8 us
  transfers between devices with their start and end apart: 74 -> 74, of which waited for: 35 -> 33; matrix products, arithmetic and copies ran while one was open for 41% -> 43% of each run, Pallas kernels for 0% -> 0%
where the time goes in v6:
time: 1440 us; the launch traced here: 1430 us
  waiting for transfers between devices  576 us (40%)
  matrix products  348 us (24%)
  other arithmetic  200 us (14%)
  local copies, waits for them, and re-layouts  184 us (13%)
  starting transfers between devices  47.3 us (3%)
  blocking collectives  45.3 us (3%)
  between operations  29.3 us (2%)
    ppermute x48, waiting for transfers between devices, flip(): return lax.ppermute(part, axis, [(i, i ^ bit) for i in range(size)])  548 us
    dot_general x27, matrix products, product(): return jnp.dot(left, right, preferred_element_type=jnp.float32)  104 us
    dot_general x29, matrix products, product_left(): lax.dot_general(left, right, (((0,), (0,)), ((), ())), preferred_element_...  99.8 us
    dot_general x29, matrix products, product_right(): lax.dot_general(left, right, (((1,), (1,)), ((), ())), preferred_element_...  82.7 us
    unnamed x654, local copies, waits for them, and re-layouts  51.8 us
    all_gather x1, blocking collectives, on_device(): gain_part = lax.all_gather(gain_part, everywhere)  45.3 us
    ppermute x48, starting transfers between devices, flip(): return lax.ppermute(part, axis, [(i, i ^ bit) for i in range(size)])  41.3 us
  transfers between devices with their start and end apart: 74, of which 33 were waited for; matrix products, arithmetic and copies ran while one was open for 43% of the time, Pallas kernels for 0%

profile of v6, /device:TPU:0, one launch (start us, length us, event | category | flops | bytes accessed | tf_op | source)
XLA Modules:
  0.0 1430.4 jit_solution(15012648338322514362)
XLA Ops:
  17.7 45.3 %all-gather = f32[256,48]{1,0:T(8,128)S(1)} all-gather(f32[8,48]{1,0:T(8,128)S(1)} %concatenate.170), channel_id=2, replica_groups=mesh['far'=4,'near'=2,'y'=2,'c'=2] {'near','far','y','c'}, dimensions={0}, use_global_device_ids=true | all-gather | bytes 50688 | tf_op jit(solution)/shard_map/all_gather | solution.py:360
  66.2 26.8 %collective-permute-done.4 = bf16[192,768]{1,0:T(8,128)(2,1)S(1)} collective-permute-done((bf16[192,768]{1,0:T(8,128)(2,1)S(1)}, bf16[192,768]{1,0:T(8,128)(2,1)S(1)}, u32[]{:S(2)}, u32[]{:S(2)}) %collective-permute-start.4) | collective-permute-done | bytes 294944 | tf_op jit(solution)/shard_map/ppermute | solution.py:32
  93.2 15.1 %collective-permute-done.8 = bf16[192,768]{1,0:T(8,128)(2,1)S(1)} collective-permute-done((bf16[192,768]{1,0:T(8,128)(2,1)S(1)}, bf16[192,768]{1,0:T(8,128)(2,1)S(1)}, u32[]{:S(2)}, u32[]{:S(2)}) %collective-permute-start.8) | collective-permute-done | bytes 294944 | tf_op jit(solution)/shard_map/ppermute | solution.py:32
  108.5 16.7 %collective-permute-done = bf16[192,768]{1,0:T(8,128)(2,1)S(1)} collective-permute-done((bf16[192,768]{1,0:T(8,128)(2,1)S(1)}, bf16[192,768]{1,0:T(8,128)(2,1)S(1)}, u32[]{:S(2)}, u32[]{:S(2)}) %collective-permute-start) | collective-permute-done | bytes 294944 | tf_op jit(solution)/shard_map/ppermute | solution.py:32
  126.3 52.6 %collective-permute-done.5 = bf16[384,768]{1,0:T(8,128)(2,1)S(1)} collective-permute-done((bf16[384,768]{1,0:T(8,128)(2,1)S(1)}, bf16[384,768]{1,0:T(8,128)(2,1)S(1)}, u32[]{:S(2)}, u32[]{:S(2)}) %collective-permute-start.5) | collective-permute-done | bytes 589856 | tf_op jit(solution)/shard_map/ppermute | solution.py:32
  180.2 19.9 %collective-permute-done.9 = bf16[384,768]{1,0:T(8,128)(2,1)S(1)} collective-permute-done((bf16[384,768]{1,0:T(8,128)(2,1)S(1)}, bf16[384,768]{1,0:T(8,128)(2,1)S(1)}, u32[]{:S(2)}, u32[]{:S(2)}) %collective-permute-start.9) | collective-permute-done | bytes 589856 | tf_op jit(solution)/shard_map/ppermute | solution.py:32
  202.9 45.4 %collective-permute-done.1 = bf16[384,768]{1,0:T(8,128)(2,1)} collective-permute-done((bf16[384,768]{1,0:T(8,128)(2,1)}, bf16[384,768]{1,0:T(8,128)(2,1)}, u32[]{:S(2)}, u32[]{:S(2)}) %collective-permute-start.1) | collective-permute-done | bytes 589856 | tf_op jit(solution)/shard_map/ppermute | solution.py:32
  259.4 46.9 %collective-permute-done.2 = bf16[768,768]{1,0:T(8,128)(2,1)S(1)} collective-permute-done((bf16[768,768]{1,0:T(8,128)(2,1)S(1)}, bf16[768,768]{1,0:T(8,128)(2,1)S(1)}, u32[]{:S(2)}, u32[]{:S(2)}) %collective-permute-start.2) | collective-permute-done | bytes 1179680 | tf_op jit(solution)/shard_map/ppermute | solution.py:32
  311.6 51.5 %collective-permute-done.7 = bf16[1536,768]{1,0:T(8,128)(2,1)} collective-permute-done((bf16[1536,768]{1,0:T(8,128)(2,1)}, bf16[1536,768]{1,0:T(8,128)(2,1)}, u32[]{:S(2)}, u32[]{:S(2)}) %collective-permute-start.7) | collective-permute-done | bytes 2359328 | tf_op jit(solution)/shard_map/ppermute | solution.py:32
  373.9 8.9 collective-permute-done.3
  467.2 8.2 fusion.71
  480.6 8.9 multiply_convert_fusion.5
  496.4 8.7 multiply_convert_fusion.4
  505.1 7.8 convolution_add_fusion.3
  559.8 25.6 %all-gather.6.cloned.1.call-done = bf16[3072,3072]{1,0:T(8,128)(2,1)} async-done(((bf16[192,3072]{1,0:T(8,128)(2,1)}), bf16[3072,3072]{1,0:T(8,128)(2,1)}) %all-gather.6.cloned.1.call-update) | async-done | bytes 18874384 | tf_op jit(solution)/shard_map/all_gather | solution.py:44
  764.4 9.5 multiply_convert_fusion.3
  773.9 11.1 multiply_convert_fusion.2
  785.0 8.8 fusion.77
  801.1 7.3 fusion.69
  808.5 9.4 add_add_fusion
  817.9 43.9 %collective-permute-done.32 = bf16[1536,768]{0,1:T(8,128)(2,1)S(1)} collective-permute-done((bf16[1536,768]{0,1:T(8,128)(2,1)S(1)}, bf16[1536,768]{0,1:T(8,128)(2,1)S(1)}, u32[]{:S(2)}, u32[]{:S(2)}) %collective-permute-start.32) | collective-permute-done | bytes 2359328 | tf_op jit(solution)/shard_map/ppermute | solution.py:32
  867.9 7.9 broadcast_select_fusion
  922.4 10.9 multiply_reduce_fusion
  935.6 10.0 multiply_convert_fusion
  964.4 9.3 multiply_convert_fusion.1
  1058.0 82.5 %collective-permute-done.53 = bf16[384,768]{0,1:T(8,128)(2,1)} collective-permute-done((bf16[384,768]{0,1:T(8,128)(2,1)}, bf16[384,768]{0,1:T(8,128)(2,1)}, u32[]{:S(2)}, u32[]{:S(2)}) %collective-permute-start.53) | collective-permute-done | bytes 589856 | tf_op jit(solution)/shard_map/ppermute | solution.py:32
  1143.1 19.5 %collective-permute-done.51 = bf16[384,768]{0,1:T(8,128)(2,1)} collective-permute-done((bf16[384,768]{0,1:T(8,128)(2,1)}, bf16[384,768]{0,1:T(8,128)(2,1)}, u32[]{:S(2)}, u32[]{:S(2)}) %collective-permute-start.51) | collective-permute-done | bytes 589856 | tf_op jit(solution)/shard_map/ppermute | solution.py:32
  1168.3 10.2 collective-permute-done.54
  1221.8 31.9 %collective-permute-done.61 = f32[384,7]{1,0:T(8,128)S(1)} collective-permute-done((f32[384,7]{1,0:T(8,128)S(1)}, f32[384,7]{1,0:T(8,128)S(1)}, u32[]{:S(2)}, u32[]{:S(2)}) %collective-permute-start.61) | collective-permute-done | bytes 10784 | tf_op jit(solution)/shard_map/ppermute | solution.py:32
  1285.0 8.9 collective-permute-done.39
  1308.7 27.7 %collective-permute-done.41 = bf16[384,192]{1,0:T(8,128)(2,1)S(1)} collective-permute-done((bf16[384,192]{1,0:T(8,128)(2,1)S(1)}, bf16[384,192]{1,0:T(8,128)(2,1)S(1)}, u32[]{:S(2)}, u32[]{:S(2)}) %collective-permute-start.41) | collective-permute-done | bytes 147488 | tf_op jit(solution)/shard_map/ppermute | solution.py:32
  1404.1 12.2 multiply_subtract_fusion
  (1176 shorter events, 691.7 us)
Async XLA Ops:
  7.2 380.7 %all-gather.4.cloned.1.call-start = ((), (), s32[]{:S(2)}) async-start(), calls=%async_computation.2 | async-start | bytes 21725184 | tf_op jit(solution)/shard_map/all_gather | solution.py:44
  14.6 570.9 %all-gather.6.cloned.1.call-start = ((), (), s32[]{:S(2)}) async-start(), calls=%async_computation.3 | async-start | bytes 20054016 | tf_op jit(solution)/shard_map/all_gather | solution.py:44
  64.1 44.2 %collective-permute-start.8 = (bf16[192,768]{1,0:T(8,128)(2,1)S(1)}, bf16[192,768]{1,0:T(8,128)(2,1)S(1)}, u32[]{:S(2)}, u32[]{:S(2)}) collective-permute-start(bf16[192,768]{1,0:T(8,128)(2,1)S(1)} %pad_maximum_fusion.45), channel_id=1, source_target_pairs={{0,8},{8,0},{16,24},{24,16},{1,9},{9,1},{17,25},{25,17},{2,10},{10... | collective-permute-start | bytes 884744 | tf_op jit(solution)/shard_map/ppermute | solution.py:32
  66.1 59.1 %collective-permute-start = (bf16[192,768]{1,0:T(8,128)(2,1)S(1)}, bf16[192,768]{1,0:T(8,128)(2,1)S(1)}, u32[]{:S(2)}, u32[]{:S(2)}) collective-permute-start(bf16[192,768]{1,0:T(8,128)(2,1)S(1)} %get-tuple-element.53), channel_id=1, source_target_pairs={{0,8},{8,0},{16,24},{24,16},{1,9},{9,1},{17,25},{25,17},{2,10},{10... | collective-permute-start | bytes 884744 | tf_op jit(solution)/shard_map/ppermute | solution.py:32
  93.1 85.7 %collective-permute-start.5 = (bf16[384,768]{1,0:T(8,128)(2,1)S(1)}, bf16[384,768]{1,0:T(8,128)(2,1)S(1)}, u32[]{:S(2)}, u32[]{:S(2)}) collective-permute-start(bf16[384,768]{1,0:T(8,128)(2,1)S(1)} %pad_maximum_fusion.33), channel_id=1, source_target_pairs={{0,16},{8,24},{16,0},{24,8},{1,17},{9,25},{17,1},{25,9},{2,18},{10... | collective-permute-start | bytes 1769480 | tf_op jit(solution)/shard_map/ppermute | solution.py:32
  108.4 91.7 %collective-permute-start.9 = (bf16[384,768]{1,0:T(8,128)(2,1)S(1)}, bf16[384,768]{1,0:T(8,128)(2,1)S(1)}, u32[]{:S(2)}, u32[]{:S(2)}) collective-permute-start(bf16[384,768]{1,0:T(8,128)(2,1)S(1)} %pad_maximum_fusion.34), channel_id=1, source_target_pairs={{0,16},{8,24},{16,0},{24,8},{1,17},{9,25},{17,1},{25,9},{2,18},{10... | collective-permute-start | bytes 1769480 | tf_op jit(solution)/shard_map/ppermute | solution.py:32
  126.2 122.0 %collective-permute-start.1 = (bf16[384,768]{1,0:T(8,128)(2,1)}, bf16[384,768]{1,0:T(8,128)(2,1)}, u32[]{:S(2)}, u32[]{:S(2)}) collective-permute-start(bf16[384,768]{1,0:T(8,128)(2,1)} %pad_maximum_fusion.32), channel_id=1, source_target_pairs={{0,16},{8,24},{16,0},{24,8},{1,17},{9,25},{17,1},{25,9},{2,18},{10... | collective-permute-start | bytes 1769480 | tf_op jit(solution)/shard_map/ppermute | solution.py:32
  180.2 71.0 %collective-permute-start.6 = (bf16[768,768]{1,0:T(8,128)(2,1)}, bf16[768,768]{1,0:T(8,128)(2,1)S(1)}, u32[]{:S(2)}, u32[]{:S(2)}) collective-permute-start(bf16[768,768]{1,0:T(8,128)(2,1)} %pad_maximum_fusion.17), channel_id=1, source_target_pairs={{0,2},{2,0},{1,3},{3,1},{4,6},{6,4},{5,7},{7,5},{8,10},{10,8},{9,1... | collective-permute-start | bytes 3538952 | tf_op jit(solution)/shard_map/ppermute | solution.py:32
  201.4 54.4 %collective-permute-start.10 = (bf16[768,768]{1,0:T(8,128)(2,1)}, bf16[768,768]{1,0:T(8,128)(2,1)}, u32[]{:S(2)}, u32[]{:S(2)}) collective-permute-start(bf16[768,768]{1,0:T(8,128)(2,1)} %pad_maximum_fusion.18), channel_id=1, source_target_pairs={{0,4},{4,0},{1,5},{5,1},{2,6},{6,2},{3,7},{7,3},{8,12},{12,8},{9,1... | collective-permute-start | bytes 3538952 | tf_op jit(solution)/shard_map/ppermute | solution.py:32
  249.8 56.5 %collective-permute-start.2 = (bf16[768,768]{1,0:T(8,128)(2,1)S(1)}, bf16[768,768]{1,0:T(8,128)(2,1)S(1)}, u32[]{:S(2)}, u32[]{:S(2)}) collective-permute-start(bf16[768,768]{1,0:T(8,128)(2,1)S(1)} %pad_maximum_fusion.16), channel_id=1, source_target_pairs={{0,4},{4,0},{1,5},{5,1},{2,6},{6,2},{3,7},{7,3},{8,12},{12,8},{9,1... | collective-permute-start | bytes 3538952 | tf_op jit(solution)/shard_map/ppermute | solution.py:32
  253.0 110.1 %collective-permute-start.7 = (bf16[1536,768]{1,0:T(8,128)(2,1)}, bf16[1536,768]{1,0:T(8,128)(2,1)}, u32[]{:S(2)}, u32[]{:S(2)}) collective-permute-start(bf16[1536,768]{1,0:T(8,128)(2,1)} %pad_maximum_fusion.6), channel_id=1, source_target_pairs={{0,4},{4,0},{1,5},{5,1},{2,6},{6,2},{3,7},{7,3},{8,12},{12,8},{9,1... | collective-permute-start | bytes 7077896 | tf_op jit(solution)/shard_map/ppermute | solution.py:32
  259.4 106.9 %collective-permute-start.11 = (bf16[1536,768]{1,0:T(8,128)(2,1)}, bf16[1536,768]{1,0:T(8,128)(2,1)}, u32[]{:S(2)}, u32[]{:S(2)}) collective-permute-start(bf16[1536,768]{1,0:T(8,128)(2,1)} %pad_maximum_fusion.9), channel_id=1, source_target_pairs={{0,2},{2,0},{1,3},{3,1},{4,6},{6,4},{5,7},{7,5},{8,10},{10,8},{9,1... | collective-permute-start | bytes 7077896 | tf_op jit(solution)/shard_map/ppermute | solution.py:32
  308.4 74.4 %collective-permute-start.3 = (bf16[1536,768]{1,0:T(8,128)(2,1)}, bf16[1536,768]{1,0:T(8,128)(2,1)}, u32[]{:S(2)}, u32[]{:S(2)}) collective-permute-start(bf16[1536,768]{1,0:T(8,128)(2,1)} %pad_maximum_fusion.5), channel_id=1, source_target_pairs={{0,2},{2,0},{1,3},{3,1},{4,6},{6,4},{5,7},{7,5},{8,10},{10,8},{9,1... | collective-permute-start | bytes 7077896 | tf_op jit(solution)/shard_map/ppermute | solution.py:32
  309.6 1044.8 %reduce-scatter.5.cloned.1.call-start = ((), (), s32[]{:S(2)}) async-start(), calls=%async_computation.5 | async-start | bytes 13369344 | tf_op jit(solution)/shard_map/reduce_scatter | solution.py:82
  622.9 195.0 %collective-permute-start.28 = (bf16[1536,1024]{1,0:T(8,128)(2,1)}, bf16[1536,1024]{1,0:T(8,128)(2,1)}, u32[]{:S(2)}, u32[]{:S(2)}) collective-permute-start(bf16[1536,1024]{1,0:T(8,128)(2,1)} %get-tuple-element.264), channel_id=1, source_target_pairs={{0,2},{2,0},{1,3},{3,1},{4,6},{6,4},{5,7},{7,5},{8,10},{10,8},{9,1... | collective-permute-start | bytes 9437192 | tf_op jit(solution)/shard_map/ppermute | solution.py:32
  642.3 716.2 %reduce-scatter.3.cloned.1.call-start = ((), (), s32[]{:S(2)}) async-start(), calls=%async_computation.4 | async-start | bytes 13369344 | tf_op jit(solution)/shard_map/reduce_scatter | solution.py:82
  664.9 71.1 %collective-permute-start.27 = (bf16[512,1536]{1,0:T(8,128)(2,1)}, bf16[512,1536]{1,0:T(8,128)(2,1)}, u32[]{:S(2)}, u32[]{:S(2)}) collective-permute-start(bf16[512,1536]{1,0:T(8,128)(2,1)} %slice.887), channel_id=1, source_target_pairs={{0,1},{1,0},{2,3},{3,2},{4,5},{5,4},{6,7},{7,6},{8,9},{9,8},{10,11... | collective-permute-start | bytes 4718600 | tf_op jit(solution)/shard_map/ppermute | solution.py:27
  702.5 115.5 %collective-permute-start.29 = (bf16[1536,768]{0,1:T(8,128)(2,1)}, bf16[1536,768]{0,1:T(8,128)(2,1)}, u32[]{:S(2)}, u32[]{:S(2)}) collective-permute-start(bf16[1536,768]{0,1:T(8,128)(2,1)} %get-tuple-element.268), channel_id=1, source_target_pairs={{0,2},{2,0},{1,3},{3,1},{4,6},{6,4},{5,7},{7,5},{8,10},{10,8},{9,1... | collective-permute-start | bytes 7077896 | tf_op jit(solution)/shard_map/ppermute | solution.py:32
  758.5 103.4 %collective-permute-start.32 = (bf16[1536,768]{0,1:T(8,128)(2,1)S(1)}, bf16[1536,768]{0,1:T(8,128)(2,1)S(1)}, u32[]{:S(2)}, u32[]{:S(2)}) collective-permute-start(bf16[1536,768]{0,1:T(8,128)(2,1)S(1)} %get-tuple-element.266), channel_id=1, source_target_pairs={{0,2},{2,0},{1,3},{3,1},{4,6},{6,4},{5,7},{7,5},{8,10},{10,8},{9,1... | collective-permute-start | bytes 7077896 | tf_op jit(solution)/shard_map/ppermute | solution.py:32
  875.8 152.3 %collective-permute-start.46 = (bf16[1536,1024]{1,0:T(8,128)(2,1)}, bf16[1536,1024]{1,0:T(8,128)(2,1)}, u32[]{:S(2)}, u32[]{:S(2)}) collective-permute-start(bf16[1536,1024]{1,0:T(8,128)(2,1)} %get-tuple-element.262), channel_id=1, source_target_pairs={{0,2},{2,0},{1,3},{3,1},{4,6},{6,4},{5,7},{7,5},{8,10},{10,8},{9,1... | collective-permute-start | bytes 9437192 | tf_op jit(solution)/shard_map/ppermute | solution.py:32
  879.5 148.5 %collective-permute-start.45 = (bf16[768,768]{0,1:T(8,128)(2,1)}, bf16[768,768]{0,1:T(8,128)(2,1)}, u32[]{:S(2)}, u32[]{:S(2)}) collective-permute-start(bf16[768,768]{0,1:T(8,128)(2,1)} %get-tuple-element.282), channel_id=1, source_target_pairs={{0,4},{4,0},{1,5},{5,1},{2,6},{6,2},{3,7},{7,3},{8,12},{12,8},{9,1... | collective-permute-start | bytes 3538952 | tf_op jit(solution)/shard_map/ppermute | solution.py:32
  884.4 143.6 %collective-permute-start.44 = (bf16[768,768]{0,1:T(8,128)(2,1)}, bf16[768,768]{0,1:T(8,128)(2,1)}, u32[]{:S(2)}, u32[]{:S(2)}) collective-permute-start(bf16[768,768]{0,1:T(8,128)(2,1)} %get-tuple-element.284), channel_id=1, source_target_pairs={{0,4},{4,0},{1,5},{5,1},{2,6},{6,2},{3,7},{7,3},{8,12},{12,8},{9,1... | collective-permute-start | bytes 3538952 | tf_op jit(solution)/shard_map/ppermute | solution.py:32
  890.6 137.4 %collective-permute-start.43 = (bf16[768,1024]{1,0:T(8,128)(2,1)}, bf16[768,1024]{1,0:T(8,128)(2,1)}, u32[]{:S(2)}, u32[]{:S(2)}) collective-permute-start(bf16[768,1024]{1,0:T(8,128)(2,1)} %get-tuple-element.280), channel_id=1, source_target_pairs={{0,4},{4,0},{1,5},{5,1},{2,6},{6,2},{3,7},{7,3},{8,12},{12,8},{9,1... | collective-permute-start | bytes 4718600 | tf_op jit(solution)/shard_map/ppermute | solution.py:32
  998.0 200.2 %collective-permute-start.36 = (bf16[512,1536]{1,0:T(8,128)(2,1)}, bf16[512,1536]{1,0:T(8,128)(2,1)}, u32[]{:S(2)}, u32[]{:S(2)}) collective-permute-start(bf16[512,1536]{1,0:T(8,128)(2,1)} %slice.885), channel_id=1, source_target_pairs={{0,1},{1,0},{2,3},{3,2},{4,5},{5,4},{6,7},{7,6},{8,9},{9,8},{10,11... | collective-permute-start | bytes 4718600 | tf_op jit(solution)/shard_map/ppermute | solution.py:27
  1031.7 135.0 %collective-permute-start.58 = (bf16[384,1024]{1,0:T(8,128)(2,1)}, bf16[384,1024]{1,0:T(8,128)(2,1)}, u32[]{:S(2)}, u32[]{:S(2)}) collective-permute-start(bf16[384,1024]{1,0:T(8,128)(2,1)} %constant_dynamic-slice_fusion.7), channel_id=1, source_target_pairs={{0,16},{8,24},{16,0},{24,8},{1,17},{9,25},{17,1},{25,9},{2,18},{10... | collective-permute-start | bytes 2359304 | tf_op jit(solution)/shard_map/ppermute | solution.py:32
  1037.5 167.1 %collective-permute-start.55 = (bf16[768,1024]{1,0:T(8,128)(2,1)}, bf16[768,1024]{1,0:T(8,128)(2,1)}, u32[]{:S(2)}, u32[]{:S(2)}) collective-permute-start(bf16[768,1024]{1,0:T(8,128)(2,1)} %constant_dynamic-slice_fusion.10), channel_id=1, source_target_pairs={{0,4},{4,0},{1,5},{5,1},{2,6},{6,2},{3,7},{7,3},{8,12},{12,8},{9,1... | collective-permute-start | bytes 4718600 | tf_op jit(solution)/shard_map/ppermute | solution.py:32
  1041.2 99.3 %collective-permute-start.53 = (bf16[384,768]{0,1:T(8,128)(2,1)}, bf16[384,768]{0,1:T(8,128)(2,1)}, u32[]{:S(2)}, u32[]{:S(2)}) collective-permute-start(bf16[384,768]{0,1:T(8,128)(2,1)} %constant_dynamic-slice_fusion.12), channel_id=1, source_target_pairs={{0,16},{8,24},{16,0},{24,8},{1,17},{9,25},{17,1},{25,9},{2,18},{10... | collective-permute-start | bytes 1769480 | tf_op jit(solution)/shard_map/ppermute | solution.py:32
  1045.2 117.5 %collective-permute-start.51 = (bf16[384,768]{0,1:T(8,128)(2,1)}, bf16[384,768]{0,1:T(8,128)(2,1)}, u32[]{:S(2)}, u32[]{:S(2)}) collective-permute-start(bf16[384,768]{0,1:T(8,128)(2,1)} %constant_dynamic-slice_fusion.14), channel_id=1, source_target_pairs={{0,16},{8,24},{16,0},{24,8},{1,17},{9,25},{17,1},{25,9},{2,18},{10... | collective-permute-start | bytes 1769480 | tf_op jit(solution)/shard_map/ppermute | solution.py:32
  1140.5 124.8 %collective-permute-start.47 = (bf16[1536,768]{0,1:T(8,128)(2,1)}, bf16[1536,768]{0,1:T(8,128)(2,1)}, u32[]{:S(2)}, u32[]{:S(2)}) collective-permute-start(bf16[1536,768]{0,1:T(8,128)(2,1)} %broadcast_select_fusion.4), channel_id=1, source_target_pairs={{0,2},{2,0},{1,3},{3,1},{4,6},{6,4},{5,7},{7,5},{8,10},{10,8},{9,1... | collective-permute-start | bytes 7077896 | tf_op jit(solution)/shard_map/ppermute | solution.py:32
  1209.2 73.1 %collective-permute-start.56 = (bf16[384,1024]{1,0:T(8,128)(2,1)}, bf16[384,1024]{1,0:T(8,128)(2,1)}, u32[]{:S(2)}, u32[]{:S(2)}) collective-permute-start(bf16[384,1024]{1,0:T(8,128)(2,1)} %constant_dynamic-slice_fusion.9), channel_id=1, source_target_pairs={{0,16},{8,24},{16,0},{24,8},{1,17},{9,25},{17,1},{25,9},{2,18},{10... | collective-permute-start | bytes 2359304 | tf_op jit(solution)/shard_map/ppermute | solution.py:32
  1215.8 37.9 %collective-permute-start.61 = (f32[384,7]{1,0:T(8,128)S(1)}, f32[384,7]{1,0:T(8,128)S(1)}, u32[]{:S(2)}, u32[]{:S(2)}) collective-permute-start(f32[384,7]{1,0:T(8,128)S(1)} %constant_dynamic-slice_fusion.3), channel_id=1, source_target_pairs={{0,16},{8,24},{16,0},{24,8},{1,17},{9,25},{17,1},{25,9},{2,18},{10... | collective-permute-start | bytes 32264 | tf_op jit(solution)/shard_map/ppermute | solution.py:32
  1301.2 35.4 %collective-permute-start.49 = (bf16[384,768]{0,1:T(8,128)(2,1)S(1)}, bf16[384,768]{0,1:T(8,128)(2,1)S(1)}, u32[]{:S(2)}, u32[]{:S(2)}) collective-permute-start(bf16[384,768]{0,1:T(8,128)(2,1)S(1)} %constant_dynamic-slice_fusion.16), channel_id=1, source_target_pairs={{0,16},{8,24},{16,0},{24,8},{1,17},{9,25},{17,1},{25,9},{2,18},{10... | collective-permute-start | bytes 1769480 | tf_op jit(solution)/shard_map/ppermute | solution.py:32
  (364 other events, 3205.1 us)
Sparse Core Ops, SparseCore 0:
  14.7 347.8 all-gather.3
  366.0 219.4 all-gather.5
  642.5 247.9 reduce-scatter.4
  917.6 255.6 reduce-scatter.2
